TPU v7x, 256 devices: a whole 4x4x8 slice. The times are simulated.
256 devices in a mesh: tm: 32 (over x_lo, z, core), rows: 8 (over y, x_hi).
Axes of the slice: x: 4 (x_hi: 2, x_lo: 2; x = x_hi * 2 + x_lo), y: 4, z: 8, core: 2. Of those that a mesh axis runs over, the one named last changes fastest.
Arguments:
- video: bfloat16 [64, 16, 64, 384], P('tm', 'rows'), may hold values from -6 to 6
- conv_weight: bfloat16 [3, 3, 3, 384, 384], replicated, may hold values from -0.0625 to 0.0625
- norm_gain: float32 [384], replicated, may hold values from 0.1 to 1.9
- w_query: bfloat16 [384, 384], replicated, may hold values from -0.3125 to 0.3125
- w_key: bfloat16 [384, 384], replicated, may hold values from -0.875 to 0.875
- w_value: bfloat16 [384, 384], replicated, may hold values from -0.875 to 0.875
- w_out: bfloat16 [384, 384], replicated, may hold values from -0.3125 to 0.3125
- cotangent: bfloat16 [64, 16, 64, 384], P('tm', 'rows'), may hold values from -6 to 6
Outputs:
- block_out: bfloat16 [64, 16, 64, 384], P('tm', 'rows')
- video_grad: bfloat16 [64, 16, 64, 384], P('tm', 'rows')
All inputs are finite; a program needn't handle non-finite values.
Results may differ from a plain program's by a relative error of at most 0.014.
Values may be sent and summed in bfloat16 or wider, within the bound.
No kernel may reach another device: no remote copies, remote signals or barrier semaphores. Data moves between devices by JAX's collectives and lax.ppermute only.
A program may use at most 64 MiB of HBM per device.

v0:
```python
import functools

import jax
import jax.numpy as jnp
from jax import lax
from jax.experimental import pallas as pl
from jax.experimental.pallas import tpu as pltpu
from jax.sharding import PartitionSpec as P


F32 = jnp.float32
BF16 = jnp.bfloat16
MIB = 1024 * 1024
LOAD = 42 * MIB
PREPARE = 533 * MIB // 10
VM = pl.BlockSpec(memory_space=pltpu.VMEM)
SM = pl.BlockSpec(memory_space=pltpu.SMEM)
HBM = pl.BlockSpec(memory_space=pltpu.HBM)


def call(kernel, operands, specs, shapes, scratch, limit, cost=0):
    return pl.pallas_call(
        kernel,
        in_specs=specs,
        out_specs=[VM] * len(shapes),
        out_shape=[jax.ShapeDtypeStruct(dims, dtype) for dims, dtype in shapes],
        scratch_shapes=scratch,
        compiler_params=pltpu.CompilerParams(vmem_limit_bytes=limit),
        cost_estimate=pl.CostEstimate(flops=cost, bytes_accessed=1 << 20, transcendentals=0),
    )(*operands)


def prepare_kernel(place, video, cot, packet, far, same, held, sems):
    x = place[0]
    width = far.shape[0] // 2
    moves = [
        (cot.at[1 - x], packet.at[2 * width :]),
        (cot.at[x], same),
        (video, held),
    ]
    for f in range(2):
        moves.append((video.at[f, 1 - x], packet.at[f * width : (f + 1) * width]))
        moves.append((video.at[f, x], far.at[f * width : (f + 1) * width]))
    copies = [pltpu.make_async_copy(a, b, sems.at[i]) for i, (a, b) in enumerate(moves)]
    for copy in copies:
        copy.start()
    for copy in copies:
        copy.wait()


def prepare(place, video, cot):
    _, _, width, chans = video.shape
    return call(
        prepare_kernel, (place, video, cot), [SM, HBM, HBM],
        [((4 * width, chans), BF16), ((2 * width, chans), BF16), (cot.shape[1:], BF16), (video.shape, BF16)],
        [pltpu.SemaphoreType.DMA((7,))], PREPARE,
    )


def join_kernel(same, packet, out):
    half = same.shape[0]
    out[:half] = same[...]
    out[half:] = packet[half:]


def join(same, packet):
    return call(join_kernel, (same, packet), [VM, VM], [(packet.shape, BF16)], [], 4 * MIB)[0]


def merge_kernel(place, own, cached, same, other):
    x = place[0]
    same[...] = (own[x] + cached[x].astype(F32)).astype(BF16)
    other[...] = (own[1 - x] + cached[1 - x].astype(F32)).astype(BF16)


def merge(place, own, cached):
    return call(merge_kernel, (place, own, cached), [SM, VM, VM], [(own.shape[1:], BF16)] * 2, [], 8 * MIB)


def load_kernel(w_hbm, w_out, sem):
    copy = pltpu.make_async_copy(w_hbm, w_out, sem)
    copy.start()
    copy.wait()


def load(weight):
    return call(load_kernel, (weight,), [HBM], [(weight.shape, BF16)], [pltpu.SemaphoreType.DMA], LOAD)[0]


def finish_kernel(place, out0, out1, own, handed, block_out, video_grad, total, sems):
    x = place[0]
    copies = [
        pltpu.make_async_copy(out0, block_out.at[x], sems.at[0]),
        pltpu.make_async_copy(out1, block_out.at[1 - x], sems.at[1]),
    ]
    for copy in copies:
        copy.start()
    total[...] = (own[...] + handed[...].astype(F32)).astype(BF16)
    copies.append(pltpu.make_async_copy(total, video_grad, sems.at[2]))
    copies[2].start()
    for copy in copies:
        copy.wait()


def finish(place, out0, out1, own, handed):
    return pl.pallas_call(
        finish_kernel,
        in_specs=[SM] + [VM] * 4,
        out_specs=[HBM, HBM],
        out_shape=[
            jax.ShapeDtypeStruct((2,) + out0.shape, BF16),
            jax.ShapeDtypeStruct(own.shape, BF16),
        ],
        scratch_shapes=[pltpu.VMEM(own.shape, BF16), pltpu.SemaphoreType.DMA((3,))],
        compiler_params=pltpu.CompilerParams(vmem_limit_bytes=8 * MIB),
        name="finish",
    )(place, out0, out1, own, handed)


def spread(rows_f32, width):
    n = rows_f32.shape[0]
    col = lax.broadcasted_iota(jnp.int32, rows_f32.shape, 0) % width
    left = jnp.where(col == 0, 0.0, pltpu.roll(rows_f32, 1, 0))
    right = jnp.where(col == width - 1, 0.0, pltpu.roll(rows_f32, n - 1, 0))
    return left, rows_f32, right


def fill(taps, frame, row, block, width, flip):
    n, _, chans = block.shape
    shifted = spread(block.astype(F32).reshape(n * width, chans), width)
    if flip:
        shifted = shifted[::-1]
    for c in range(3):
        taps[frame, pl.ds(row, n), :, c * chans : (c + 1) * chans] = (
            shifted[c].astype(BF16).reshape(n, width, chans)
        )


def conv_steps(taps, w_ref, main, side, out, src, dst, transposed):
    chans = w_ref.shape[-1]

    def times(lhs, a, b):
        if not transposed:
            return mm(lhs, w_ref[a, b].reshape(3 * chans, chans))
        return mm_t(lhs, jnp.concatenate([w_ref[a, b, c] for c in range(3)], axis=1))

    both = extra = None
    for b in range(3):
        row = (2 - b) if transposed else b
        lhs = [taps[f, row : row + 2] for f in range(2)]
        lhs = [v.reshape(v.shape[0] * v.shape[1], v.shape[2]) for v in lhs]
        term = times(jnp.concatenate(lhs, axis=0), main, b)
        both = term if both is None else both + term
        term = times(lhs[src], side, b)
        extra = term if extra is None else extra + term
    half = both.shape[0] // 2
    for f in range(2):
        term = both[f * half : (f + 1) * half]
        out[f] = (term + extra if f == dst else term).astype(out.dtype)


def forward_kernel(main, side, src, dst, place, packet, mid, far, w_ref, out, taps):
    width, chans = mid.shape[2:]
    x = place[0]
    for f in range(2):
        line = slice(f * width, (f + 1) * width)
        fill(taps, f, 3 * (1 - x), packet[line].reshape(1, width, chans), width, False)
        fill(taps, f, 1, mid[f], width, False)
        fill(taps, f, 3 * x, far[line].reshape(1, width, chans), width, False)
    conv_steps(taps, w_ref, main, side, out, src, dst, False)


def backward_kernel(main, side, src, dst, place, r0, r1, w_ref, out, taps):
    width, chans = taps.shape[2], w_ref.shape[-1]
    x = place[0]
    fill(taps, x, 0, r0[...].reshape(4, width, chans), width, True)
    fill(taps, 1 - x, 0, r1[...].reshape(4, width, chans), width, True)
    conv_steps(taps, w_ref, main, side, out, src, dst, True)


def conv_call(kernel, place, operands, weight, width, dtype):
    chans = weight.shape[-1]
    return call(
        kernel, (place, *operands, weight), [SM] + [VM] * (len(operands) + 1),
        [((2, 2 * width, chans), dtype)], [pltpu.VMEM((2, 4, width, 3 * chans), BF16)],
        24 * MIB, 2 * 9 * 3 * 128 * chans * chans,
    )[0]


def norm_parts(conv, gain):
    convf = conv.astype(F32)
    inverse = lax.rsqrt(jnp.mean(convf * convf, axis=-1, keepdims=True) + 1e-06)
    normed = convf * inverse * gain
    return convf, inverse, normed


def mm(a, b):
    return jnp.dot(a, b, preferred_element_type=F32)


def mm_t(a, b):
    return lax.dot_general(a, b, (((1,), (1,)), ((), ())), preferred_element_type=F32)


def t_mm(a, b):
    return lax.dot_general(a, b, (((0,), (0,)), ((), ())), preferred_element_type=F32)


CHUNKS = ((0, 384), (384, 256), (640, 256), (896, 128))


def attention_kernel(
    place, c00, c01, c10, c11, s00, s01, s10, s11, t0, t2, u0, u2, gain_ref, wq, wk, wv, wo,
    out0, out1, grad0, grad1, conv_s, cot_s, act_s, q_s, k_s, v_s, g_s, gk_s, gv_s, out_s, grad_s,
):
    x, q = place[0], place[1]
    line = c00.shape[0] // 2
    own = 6 * line
    chans = wq.shape[0]
    scale = 1.0 / jnp.sqrt(jnp.float32(chans))
    gain = gain_ref[...]

    def put(dst, value, quarter, kx):
        for j in range(2):
            slot = (4 * (quarter - q) + 2 * (x + kx - 2 * x * kx) + j + 17) % 16
            dst[pl.ds(pl.multiple_of(slot * line, line), line)] = value[j * line : (j + 1) * line]

    side = q + 1 - 2 * (q % 2)
    far = (q + 2) % 4
    far_side = (side + 2) % 4
    for ref, quarter, kx in (
        (c00, q, 0), (c01, q, 1), (c10, far, 0), (c11, far, 1),
        (s00, side, 0), (s01, side, 1), (s10, far_side, 0), (s11, far_side, 1),
    ):
        put(conv_s, ref, quarter, kx)
    for ref, quarter in ((t0, q), (t2, far), (u0, side), (u2, far_side)):
        for kx in range(2):
            put(cot_s, ref.at[2 * kx * line : 2 * (kx + 1) * line], quarter, kx)

    for at, n in CHUNKS:
        rows = slice(at, at + n)
        _, _, normed = norm_parts(conv_s[rows], gain)
        act = (normed / (1.0 + jnp.exp(-normed))).astype(BF16)
        if at == 0:
            act_s[...] = act
        q_s[rows] = mm(act, wq[...]).astype(BF16)
        k_s[rows] = mm(act, wk[...]).astype(BF16)
        v_s[rows] = mm(act, wv[...]).astype(BF16)
        g_s[rows] = mm_t(cot_s[rows], wo[...]).astype(BF16)
    attended = grad_q = None
    for at, n in CHUNKS:
        rows = slice(at, at + n)
        scores = mm_t(q_s[rows], k_s[...]) * scale
        top = jnp.max(scores, axis=-1, keepdims=True)
        expo = jnp.exp(scores - top)
        inv_total = 1.0 / jnp.sum(expo, axis=-1, keepdims=True)
        dprob = mm_t(g_s[rows], v_s[...])
        delta = jnp.sum(expo * dprob, axis=-1, keepdims=True) * inv_total
        if at == 0:
            probs = expo * inv_total
            probs_b = probs.astype(BF16)
            mid = slice(line, own - line)
            attended = mm(probs_b[mid], v_s[...]).astype(BF16)
            dscore = (probs * (dprob - delta)).astype(BF16)
            grad_q = (mm(dscore, k_s[...]) * scale).astype(BF16)
            gk_s[...] = t_mm(dscore[:, :own], q_s[rows])
            gv_s[...] = t_mm(probs_b[:, :own], g_s[rows])
        else:
            probs = expo[:, :own] * inv_total
            dscore = (probs * (dprob[:, :own] - delta)).astype(BF16)
            gk_s[...] += t_mm(dscore, q_s[rows])
            gv_s[...] += t_mm(probs.astype(BF16), g_s[rows])
    out_s[...] = (act_s[line : own - line].astype(F32) + mm(attended, wo[...])).astype(BF16)
    for kx, ref in ((0, out0), (1, out1)):
        to_x = x if kx == 0 else 1 - x
        ref[...] = out_s[pl.ds(pl.multiple_of(2 * to_x * line, line), 2 * line)]
    grad_act = cot_s[:own].astype(F32)
    grad_act = grad_act + mm_t(grad_q, wq[...])
    grad_act = grad_act + mm_t((gk_s[...] * scale).astype(BF16), wk[...])
    grad_act = grad_act + mm_t(gv_s[...].astype(BF16), wv[...])
    convf, inverse, normed = norm_parts(conv_s[:own], gain)
    sigma = 1.0 / (1.0 + jnp.exp(-normed))
    scaled = grad_act * sigma * (1.0 + normed * (1.0 - sigma)) * gain
    mean = jnp.mean(scaled * convf, axis=-1, keepdims=True)
    grad_conv = inverse * (scaled - convf * inverse * inverse * mean)
    row = lax.broadcasted_iota(jnp.int32, grad_conv.shape, 0)
    first = jnp.where(q == 0, line, 0)
    last = jnp.where(q == 3, own - line, own)
    inside = jnp.logical_and(row >= first, row < last)
    grad_s[...] = jnp.where(inside, grad_conv, 0.0).astype(BF16)
    for kx, ref in ((0, grad0), (1, grad1)):
        to_x = x if kx == 0 else 1 - x
        ref[...] = grad_s[pl.ds(pl.multiple_of(2 * to_x * line, line), 4 * line)]


def attention(place, convs, cots, gain, wq, wk, wv, wo):
    block, chans = convs[0].shape
    own, whole = 3 * block, 8 * block
    act = lambda n, t=BF16: pltpu.VMEM((n, chans), t)
    return pl.pallas_call(
        attention_kernel,
        in_specs=[SM] + [VM] * (len(convs) + len(cots) + 5),
        out_specs=[VM] * 4,
        out_shape=[jax.ShapeDtypeStruct((n * block, chans), BF16) for n in (1, 1, 2, 2)],
        scratch_shapes=[act(whole), act(whole), act(own)]
        + [act(whole)] * 4
        + [act(own, F32), act(own, F32), act(2 * block), act(own)],
        compiler_params=pltpu.CompilerParams(vmem_limit_bytes=26 * MIB),
        cost_estimate=pl.CostEstimate(
            flops=4 * 10**9, bytes_accessed=4 * 10**6, transcendentals=1 << 20
        ),
        name="attention",
    )(place, *convs, *cots, gain, wq, wk, wv, wo)


def site(h, c, y, x):
    return (h * 2 + c) * 8 + 2 * y + x


def send(value, runs, to):
    pairs = []
    for h in range(runs // 2):
        for c in range(2):
            for y in range(4):
                for x in range(2):
                    there = to(c, y, x)
                    if there is not None:
                        pairs.append((site(h, c, y, x), site(h, *there)))
    return lax.ppermute(value, ("tm", "rows"), pairs)


def home(ky, kx):
    return lambda c, y, x: (y % 2, 2 * ((y // 2 + ky) % 2) + c, x ^ kx)


def swap(c, y, x):
    return 1 - c, y, x


def across(c, y, x):
    return c, y, x ^ 1


def beyond(c, y, x):
    y = y + 1 if x else y - 1
    return (c, y, x ^ 1) if 0 <= y < 4 else None


def local(video, conv_weight, norm_gain, w_query, w_key, w_value, w_out, cotangent):
    frames, height, width, chans = video.shape
    runs, slabs = lax.axis_size("tm"), lax.axis_size("rows")
    assert (frames, height, slabs) == (2, 2, 8)
    slab_at = lax.axis_index("rows")
    x = slab_at % 2
    quarter = 2 * (slab_at // 4) + lax.axis_index("tm") % 2
    place = jnp.stack([x, quarter]).astype(jnp.int32)
    block = 2 * width

    packet, far, cot_same, held = prepare(place, video, cotangent.reshape(2, block, chans))
    far = send(far, runs, beyond)
    packet = send(packet, runs, across)
    weight = load(conv_weight)
    cot_own = join(cot_same, packet)
    cot_b = send(cot_own, runs, home(0, 0))
    slab = (packet, held, far)

    def forward(main, side, src, dst, dtype):
        kernel = functools.partial(forward_kernel, main, side, src, dst)
        return conv_call(kernel, place, slab, weight, width, dtype)

    def backward(main, side, src, dst, dtype):
        kernel = functools.partial(backward_kernel, main, side, src, dst)
        return conv_call(kernel, place, slab, weight, width, dtype)

    for_next = forward(0, 1, 1, 0, BF16)
    cached = lax.ppermute(for_next, "tm", [(i, i + 1) for i in range(runs - 1)])
    own = forward(2, 1, 0, 1, F32)
    cot_c = send(cot_b, runs, lambda c, y, x: (c, y ^ 2, x))
    same, other = merge(place, own, cached)
    got, swapped = {}, {}
    for ky, kx in ((1, 1), (0, 1), (1, 0), (0, 0)):
        got[ky, kx] = send(other if kx else same, runs, home(ky, kx))
    cots = [cot_b, cot_c, send(cot_b, runs, swap), send(cot_c, runs, swap)]
    for ky, kx in ((1, 1), (0, 1), (1, 0), (0, 0)):
        swapped[ky, kx] = send(got[ky, kx], runs, swap)
    order = ((0, 0), (0, 1), (1, 0), (1, 1))
    convs = [got[k] for k in order] + [swapped[k] for k in order]

    out0, out1, grad0, grad1 = attention(
        place, convs, cots, norm_gain.reshape(1, chans), w_query, w_key, w_value, w_out
    )
    grad1 = send(grad1, runs, home(0, 1))
    grad0 = send(grad0, runs, home(0, 0))
    out0 = send(out0, runs, home(0, 0))
    out1 = send(out1, runs, home(0, 1))
    slab = (grad0, grad1)
    for_last = backward(0, 1, 0, 1, BF16)
    handed = lax.ppermute(for_last, "tm", [(i + 1, i) for i in range(runs - 1)])
    own_grad = backward(2, 1, 1, 0, F32)
    block_out, video_grad = finish(place, out0, out1, own_grad, handed)
    return block_out.reshape(video.shape), video_grad.reshape(video.shape)


def solution(mesh):
    spec = P("tm", "rows", None, None)
    return jax.shard_map(
        local,
        mesh=mesh,
        in_specs=(spec, P(), P(), P(), P(), P(), P(), spec),
        out_specs=(spec, spec),
        check_vma=False,
    )
```

profile of v0, /device:TPU:6, one launch (start us, length us, event | category | flops | bytes accessed | tf_op | source)
XLA Modules:
  0.0 83.7 jit_solution(4479594132196761611)
XLA Ops:
  0.7 1.7 %shard_map.95 = (bf16[256,384]{1,0:T(8,128)(2,1)S(1)}, bf16[128,384]{1,0:T(8,128)(2,1)S(1)}, bf16[128,384]{1,0:T(8,128)(2,1)S(1)}, bf16[2,2,64,384]{3,2,1,0:T(8,128)(2,1)S(1)}) custom-call(s32[2]{0:T(128)S(1)} %pad_add_fusion.place, bf16[2,2,64,384]{3,2,1,0:T(8,128)(2,1)} %video.1, bf16[2,128,384]{2,1,0:T(8,128)(2,1)} %bitcast.5), custom_call_target="tpu_custom_call" | custom-call | bytes 1048576 | tf_op jit(solution)/shard_map/pallas_call | solution.py:22
  2.4 1.5 %collective-permute-start = (bf16[256,384]{1,0:T(8,128)(2,1)S(1)}, bf16[256,384]{1,0:T(8,128)(2,1)S(1)}, u32[]{:S(2)}, u32[]{:S(2)}) collective-permute-start(bf16[256,384]{1,0:T(8,128)(2,1)S(1)} %get-tuple-element.14), channel_id=1, source_target_pairs={{0,1},{1,0},{2,3},{3,2},{4,5},{5,4},{6,7},{7,6},{8,9},{9,8},{10,11... | collective-permute-start | bytes 589832 | tf_op jit(solution)/shard_map/ppermute | solution.py:329
  3.9 5.0 %collective-permute-start.1 = (bf16[128,384]{1,0:T(8,128)(2,1)S(1)}, bf16[128,384]{1,0:T(8,128)(2,1)S(1)}, u32[]{:S(2)}, u32[]{:S(2)}) collective-permute-start(bf16[128,384]{1,0:T(8,128)(2,1)S(1)} %get-tuple-element.16), channel_id=1, source_target_pairs={{1,2},{2,1},{3,4},{4,3},{5,6},{6,5},{9,10},{10,9},{11,12},{12,11},... | collective-permute-start | bytes 294920 | tf_op jit(solution)/shard_map/ppermute | solution.py:329
  8.9 1.7 %collective-permute-done.packet = bf16[256,384]{1,0:T(8,128)(2,1)S(1)} collective-permute-done((bf16[256,384]{1,0:T(8,128)(2,1)S(1)}, bf16[256,384]{1,0:T(8,128)(2,1)S(1)}, u32[]{:S(2)}, u32[]{:S(2)}) %collective-permute-start) | collective-permute-done | bytes 196640 | tf_op jit(solution)/shard_map/ppermute | solution.py:329
  10.7 0.7 collective-permute-start.11
  11.3 3.3 %shard_map.96.w_ref = bf16[3,3,3,384,384]{4,3,2,1,0:T(8,128)(2,1)S(1)} custom-call(bf16[3,3,3,384,384]{4,3,2,1,0:T(8,128)(2,1)} %w_hbm.1), custom_call_target="tpu_custom_call" | custom-call | bytes 1048576 | tf_op jit(solution)/shard_map/pallas_call | solution.py:22
  14.7 2.4 %shard_map.98 = bf16[2,128,384]{2,1,0:T(8,128)(2,1)S(1)} custom-call(s32[2]{0:T(128)S(1)} %pad_add_fusion.place, bf16[256,384]{1,0:T(8,128)(2,1)S(1)} %collective-permute-done.packet, bf16[2,2,64,384]{3,2,1,0:T(8,128)(2,1)S(1)} %get-tuple-element.15.mid, bf16[128,384]{1,0:T(8,128)(2,1)S(1)} %collective-permute-done.1.far, ...), custom_call_target="tpu_custom_call" | custom-call | flops 1019215872 | bytes 1048576 | tf_op jit(solution)/shard_map/pallas_call | solution.py:22
  17.1 5.9 %collective-permute-start.2 = (bf16[2,128,384]{2,1,0:T(8,128)(2,1)S(1)}, bf16[2,128,384]{2,1,0:T(8,128)(2,1)S(1)}, u32[]{:S(2)}, u32[]{:S(2)}) collective-permute-start(bf16[2,128,384]{2,1,0:T(8,128)(2,1)S(1)} %shard_map.98), channel_id=1, source_target_pairs={{0,8},{8,16},{16,24},{24,32},{32,40},{40,48},{48,56},{56,64},{64,7... | collective-permute-start | bytes 589832 | tf_op jit(solution)/shard_map/ppermute | solution.py:376
  23.0 3.0 %collective-permute-start.12 = (bf16[256,384]{1,0:T(8,128)(2,1)S(1)}, bf16[256,384]{1,0:T(8,128)(2,1)S(1)}, u32[]{:S(2)}, u32[]{:S(2)}) collective-permute-start(bf16[256,384]{1,0:T(8,128)(2,1)S(1)} %collective-permute-done.11.t0), channel_id=1, source_target_pairs={{0,4},{1,5},{2,6},{3,7},{4,0},{5,1},{6,2},{7,3},{8,12},{9,13},{10,... | collective-permute-start | bytes 589832 | tf_op jit(solution)/shard_map/ppermute | solution.py:329
  26.0 2.4 %shard_map.97.own = f32[2,128,384]{2,1,0:T(8,128)S(1)} custom-call(s32[2]{0:T(128)S(1)} %pad_add_fusion.place, bf16[256,384]{1,0:T(8,128)(2,1)S(1)} %collective-permute-done.packet, bf16[2,2,64,384]{3,2,1,0:T(8,128)(2,1)S(1)} %get-tuple-element.15.mid, bf16[128,384]{1,0:T(8,128)(2,1)S(1)} %collective-permute-done.1.far, ...), custom_call_target="tpu_custom_call" | custom-call | flops 1019215872 | bytes 1048576 | tf_op jit(solution)/shard_map/pallas_call | solution.py:22
  28.4 3.7 %collective-permute-done.2.cached = bf16[2,128,384]{2,1,0:T(8,128)(2,1)S(1)} collective-permute-done((bf16[2,128,384]{2,1,0:T(8,128)(2,1)S(1)}, bf16[2,128,384]{2,1,0:T(8,128)(2,1)S(1)}, u32[]{:S(2)}, u32[]{:S(2)}) %collective-permute-start.2) | collective-permute-done | bytes 196640 | tf_op jit(solution)/shard_map/ppermute | solution.py:376
  32.1 0.6 shard_map.99
  32.6 3.0 %collective-permute-start.5 = (bf16[128,384]{1,0:T(8,128)(2,1)S(1)}, bf16[128,384]{1,0:T(8,128)(2,1)S(1)}, u32[]{:S(2)}, u32[]{:S(2)}) collective-permute-start(bf16[128,384]{1,0:T(8,128)(2,1)S(1)} %get-tuple-element.17), channel_id=1, source_target_pairs={{0,4},{1,5},{2,12},{3,13},{4,0},{5,1},{6,8},{7,9},{8,6},{9,7},{10,... | collective-permute-start | bytes 294920 | tf_op jit(solution)/shard_map/ppermute | solution.py:329
  35.6 0.7 collective-permute-start.3
  36.6 2.3 %collective-permute-done.5.c10 = bf16[128,384]{1,0:T(8,128)(2,1)S(1)} collective-permute-done((bf16[128,384]{1,0:T(8,128)(2,1)S(1)}, bf16[128,384]{1,0:T(8,128)(2,1)S(1)}, u32[]{:S(2)}, u32[]{:S(2)}) %collective-permute-start.5) | collective-permute-done | bytes 98336 | tf_op jit(solution)/shard_map/ppermute | solution.py:329
  38.9 1.1 %collective-permute-start.4 = (bf16[128,384]{1,0:T(8,128)(2,1)S(1)}, bf16[128,384]{1,0:T(8,128)(2,1)S(1)}, u32[]{:S(2)}, u32[]{:S(2)}) collective-permute-start(bf16[128,384]{1,0:T(8,128)(2,1)S(1)} %get-tuple-element.18), channel_id=1, source_target_pairs={{0,1},{1,0},{2,9},{3,8},{4,5},{5,4},{6,13},{7,12},{8,3},{9,2},{10,... | collective-permute-start | bytes 294920 | tf_op jit(solution)/shard_map/ppermute | solution.py:329
  40.0 0.9 %collective-permute-start.14 = (bf16[256,384]{1,0:T(8,128)(2,1)S(1)}, bf16[256,384]{1,0:T(8,128)(2,1)S(1)}, u32[]{:S(2)}, u32[]{:S(2)}) collective-permute-start(bf16[256,384]{1,0:T(8,128)(2,1)S(1)} %collective-permute-done.12.t2), channel_id=1, source_target_pairs={{0,8},{1,9},{2,10},{3,11},{4,12},{5,13},{6,14},{7,15},{8,0},{9,1},... | collective-permute-start | bytes 589832 | tf_op jit(solution)/shard_map/ppermute | solution.py:329
  40.9 1.2 %collective-permute-start.9 = (bf16[128,384]{1,0:T(8,128)(2,1)S(1)}, bf16[128,384]{1,0:T(8,128)(2,1)S(1)}, u32[]{:S(2)}, u32[]{:S(2)}) collective-permute-start(bf16[128,384]{1,0:T(8,128)(2,1)S(1)} %collective-permute-done.5.c10), channel_id=1, source_target_pairs={{0,8},{1,9},{2,10},{3,11},{4,12},{5,13},{6,14},{7,15},{8,0},{9,1},... | collective-permute-start | bytes 294920 | tf_op jit(solution)/shard_map/ppermute | solution.py:329
  42.1 2.8 %collective-permute-done.6.c11 = bf16[128,384]{1,0:T(8,128)(2,1)S(1)} collective-permute-done((bf16[128,384]{1,0:T(8,128)(2,1)S(1)}, bf16[128,384]{1,0:T(8,128)(2,1)S(1)}, u32[]{:S(2)}, u32[]{:S(2)}) %collective-permute-start.6) | collective-permute-done | bytes 98336 | tf_op jit(solution)/shard_map/ppermute | solution.py:329
  44.9 0.9 %collective-permute-start.7 = (bf16[128,384]{1,0:T(8,128)(2,1)S(1)}, bf16[128,384]{1,0:T(8,128)(2,1)S(1)}, u32[]{:S(2)}, u32[]{:S(2)}) collective-permute-start(bf16[128,384]{1,0:T(8,128)(2,1)S(1)} %collective-permute-done.3.c00), channel_id=1, source_target_pairs={{0,8},{1,9},{2,10},{3,11},{4,12},{5,13},{6,14},{7,15},{8,0},{9,1},... | collective-permute-start | bytes 294920 | tf_op jit(solution)/shard_map/ppermute | solution.py:329
  46.7 0.6 collective-permute-done.10.s11
  47.5 9.4 %attention.1 = (bf16[128,384]{1,0:T(8,128)(2,1)S(1)}, bf16[128,384]{1,0:T(8,128)(2,1)S(1)}, bf16[256,384]{1,0:T(8,128)(2,1)S(1)}, bf16[256,384]{1,0:T(8,128)(2,1)S(1)}) custom-call(s32[2]{0:T(128)S(1)} %pad_add_fusion.place, bf16[128,384]{1,0:T(8,128)(2,1)S(1)} %collective-permute-done.3.c00, bf16[128,384]{1,0:T(8,128)(2,1)S(1)} %collective-permute-done.4.c01, ...), custom_call_target="tpu_custom_call" | custom-call | flops 4000000000 | bytes 4000000 | tf_op jit(solution)/shard_map/attention/pallas_call | solution.py:300
  56.9 0.7 collective-permute-start.17
  57.6 2.4 %collective-permute-start.18 = (bf16[256,384]{1,0:T(8,128)(2,1)S(1)}, bf16[256,384]{1,0:T(8,128)(2,1)S(1)}, u32[]{:S(2)}, u32[]{:S(2)}) collective-permute-start(bf16[256,384]{1,0:T(8,128)(2,1)S(1)} %get-tuple-element.23), channel_id=1, source_target_pairs={{0,1},{1,0},{2,9},{3,8},{4,5},{5,4},{6,13},{7,12},{8,3},{9,2},{10,... | collective-permute-start | bytes 589832 | tf_op jit(solution)/shard_map/ppermute | solution.py:329
  60.0 4.9 %collective-permute-done.18.r1 = bf16[256,384]{1,0:T(8,128)(2,1)S(1)} collective-permute-done((bf16[256,384]{1,0:T(8,128)(2,1)S(1)}, bf16[256,384]{1,0:T(8,128)(2,1)S(1)}, u32[]{:S(2)}, u32[]{:S(2)}) %collective-permute-start.18) | collective-permute-done | bytes 196640 | tf_op jit(solution)/shard_map/ppermute | solution.py:329
  64.9 2.7 %shard_map.102 = bf16[2,128,384]{2,1,0:T(8,128)(2,1)S(1)} custom-call(s32[2]{0:T(128)S(1)} %pad_add_fusion.place, bf16[256,384]{1,0:T(8,128)(2,1)S(1)} %collective-permute-done.17.r0, bf16[256,384]{1,0:T(8,128)(2,1)S(1)} %collective-permute-done.18.r1, bf16[3,3,3,384,384]{4,3,2,1,0:T(8,128)(2,1)S(1)} %shard_map.96.w_ref), custom_call_target="tpu_custom_call" | custom-call | flops 1019215872 | bytes 1048576 | tf_op jit(solution)/shard_map/pallas_call | solution.py:22
  67.6 7.0 %collective-permute-start.19 = (bf16[2,128,384]{2,1,0:T(8,128)(2,1)S(1)}, bf16[2,128,384]{2,1,0:T(8,128)(2,1)S(1)}, u32[]{:S(2)}, u32[]{:S(2)}) collective-permute-start(bf16[2,128,384]{2,1,0:T(8,128)(2,1)S(1)} %shard_map.102), channel_id=1, source_target_pairs={{8,0},{16,8},{24,16},{32,24},{40,32},{48,40},{56,48},{64,56},{72,6... | collective-permute-start | bytes 589832 | tf_op jit(solution)/shard_map/ppermute | solution.py:398
  74.6 0.7 collective-permute-start.15
  75.2 1.9 %collective-permute-start.16 = (bf16[128,384]{1,0:T(8,128)(2,1)S(1)}, bf16[128,384]{1,0:T(8,128)(2,1)S(1)}, u32[]{:S(2)}, u32[]{:S(2)}) collective-permute-start(bf16[128,384]{1,0:T(8,128)(2,1)S(1)} %get-tuple-element.21), channel_id=1, source_target_pairs={{0,1},{1,0},{2,9},{3,8},{4,5},{5,4},{6,13},{7,12},{8,3},{9,2},{10,... | collective-permute-start | bytes 294920 | tf_op jit(solution)/shard_map/ppermute | solution.py:329
  77.2 2.7 %shard_map.101.own = f32[2,128,384]{2,1,0:T(8,128)S(1)} custom-call(s32[2]{0:T(128)S(1)} %pad_add_fusion.place, bf16[256,384]{1,0:T(8,128)(2,1)S(1)} %collective-permute-done.17.r0, bf16[256,384]{1,0:T(8,128)(2,1)S(1)} %collective-permute-done.18.r1, bf16[3,3,3,384,384]{4,3,2,1,0:T(8,128)(2,1)S(1)} %shard_map.96.w_ref), custom_call_target="tpu_custom_call" | custom-call | flops 1019215872 | bytes 1048576 | tf_op jit(solution)/shard_map/pallas_call | solution.py:22
  79.9 2.4 %collective-permute-done.16.out1 = bf16[128,384]{1,0:T(8,128)(2,1)S(1)} collective-permute-done((bf16[128,384]{1,0:T(8,128)(2,1)S(1)}, bf16[128,384]{1,0:T(8,128)(2,1)S(1)}, u32[]{:S(2)}, u32[]{:S(2)}) %collective-permute-start.16) | collective-permute-done | bytes 98336 | tf_op jit(solution)/shard_map/ppermute | solution.py:329
  82.3 1.3 %finish.1 = (bf16[2,128,384]{2,1,0:T(8,128)(2,1)}, bf16[2,128,384]{2,1,0:T(8,128)(2,1)}) custom-call(s32[2]{0:T(128)S(1)} %pad_add_fusion.place, bf16[128,384]{1,0:T(8,128)(2,1)S(1)} %collective-permute-done.15.out0, bf16[128,384]{1,0:T(8,128)(2,1)S(1)} %collective-permute-done.16.out1, f32[2,128,384]{2,1,0:T(8,128)S(1)} %shard_map.101.own, ...), custom_call_target="tpu_custom_call" | custom-call | tf_op jit(solution)/shard_map/finish/pallas_call | solution.py:106
  (30 shorter events, 1.5 us)
Async XLA Ops:
  2.4 8.2 %collective-permute-start = (bf16[256,384]{1,0:T(8,128)(2,1)S(1)}, bf16[256,384]{1,0:T(8,128)(2,1)S(1)}, u32[]{:S(2)}, u32[]{:S(2)}) collective-permute-start(bf16[256,384]{1,0:T(8,128)(2,1)S(1)} %get-tuple-element.14), channel_id=1, source_target_pairs={{0,1},{1,0},{2,3},{3,2},{4,5},{5,4},{6,7},{7,6},{8,9},{9,8},{10,11... | collective-permute-start | bytes 589832 | tf_op jit(solution)/shard_map/ppermute | solution.py:329
  3.9 10.7 %collective-permute-start.1 = (bf16[128,384]{1,0:T(8,128)(2,1)S(1)}, bf16[128,384]{1,0:T(8,128)(2,1)S(1)}, u32[]{:S(2)}, u32[]{:S(2)}) collective-permute-start(bf16[128,384]{1,0:T(8,128)(2,1)S(1)} %get-tuple-element.16), channel_id=1, source_target_pairs={{1,2},{2,1},{3,4},{4,3},{5,6},{6,5},{9,10},{10,9},{11,12},{12,11},... | collective-permute-start | bytes 294920 | tf_op jit(solution)/shard_map/ppermute | solution.py:329
  10.7 12.3 %collective-permute-start.11 = (bf16[256,384]{1,0:T(8,128)(2,1)S(1)}, bf16[256,384]{1,0:T(8,128)(2,1)S(1)}, u32[]{:S(2)}, u32[]{:S(2)}) collective-permute-start(bf16[256,384]{1,0:T(8,128)(2,1)S(1)} %shard_map.100), channel_id=1, source_target_pairs={{0,0},{1,1},{2,8},{3,9},{4,4},{5,5},{6,12},{7,13},{8,2},{9,3},{10,... | collective-permute-start | bytes 589832 | tf_op jit(solution)/shard_map/ppermute | solution.py:329
  14.6 31.9 %copy-start.4 = (f32[384]{0:T(512)S(1)}, f32[384]{0:T(512)}, u32[]{:S(2)}) copy-start(f32[384]{0:T(512)} %param.10) | copy-start | bytes 4612
  14.6 32.8 %copy-start = (bf16[384,384]{1,0:T(8,128)(2,1)S(1)}, bf16[384,384]{1,0:T(8,128)(2,1)}, u32[]{:S(2)}) copy-start(bf16[384,384]{1,0:T(8,128)(2,1)} %wq.1) | copy-start | bytes 884740
  14.7 32.8 %copy-start.1 = (bf16[384,384]{1,0:T(8,128)(2,1)S(1)}, bf16[384,384]{1,0:T(8,128)(2,1)}, u32[]{:S(2)}) copy-start(bf16[384,384]{1,0:T(8,128)(2,1)} %wk.1) | copy-start | bytes 884740
  14.7 32.8 %copy-start.2 = (bf16[384,384]{1,0:T(8,128)(2,1)S(1)}, bf16[384,384]{1,0:T(8,128)(2,1)}, u32[]{:S(2)}) copy-start(bf16[384,384]{1,0:T(8,128)(2,1)} %wv.1) | copy-start | bytes 884740
  14.7 32.8 %copy-start.3 = (bf16[384,384]{1,0:T(8,128)(2,1)S(1)}, bf16[384,384]{1,0:T(8,128)(2,1)}, u32[]{:S(2)}) copy-start(bf16[384,384]{1,0:T(8,128)(2,1)} %wo.1) | copy-start | bytes 884740
  17.1 15.0 %collective-permute-start.2 = (bf16[2,128,384]{2,1,0:T(8,128)(2,1)S(1)}, bf16[2,128,384]{2,1,0:T(8,128)(2,1)S(1)}, u32[]{:S(2)}, u32[]{:S(2)}) collective-permute-start(bf16[2,128,384]{2,1,0:T(8,128)(2,1)S(1)} %shard_map.98), channel_id=1, source_target_pairs={{0,8},{8,16},{16,24},{24,32},{32,40},{40,48},{48,56},{56,64},{64,7... | collective-permute-start | bytes 589832 | tf_op jit(solution)/shard_map/ppermute | solution.py:376
  23.0 17.0 %collective-permute-start.12 = (bf16[256,384]{1,0:T(8,128)(2,1)S(1)}, bf16[256,384]{1,0:T(8,128)(2,1)S(1)}, u32[]{:S(2)}, u32[]{:S(2)}) collective-permute-start(bf16[256,384]{1,0:T(8,128)(2,1)S(1)} %collective-permute-done.11.t0), channel_id=1, source_target_pairs={{0,4},{1,5},{2,6},{3,7},{4,0},{5,1},{6,2},{7,3},{8,12},{9,13},{10,... | collective-permute-start | bytes 589832 | tf_op jit(solution)/shard_map/ppermute | solution.py:329
  32.6 6.2 %collective-permute-start.5 = (bf16[128,384]{1,0:T(8,128)(2,1)S(1)}, bf16[128,384]{1,0:T(8,128)(2,1)S(1)}, u32[]{:S(2)}, u32[]{:S(2)}) collective-permute-start(bf16[128,384]{1,0:T(8,128)(2,1)S(1)} %get-tuple-element.17), channel_id=1, source_target_pairs={{0,4},{1,5},{2,12},{3,13},{4,0},{5,1},{6,8},{7,9},{8,6},{9,7},{10,... | collective-permute-start | bytes 294920 | tf_op jit(solution)/shard_map/ppermute | solution.py:329
  35.6 10.4 %collective-permute-start.13 = (bf16[256,384]{1,0:T(8,128)(2,1)S(1)}, bf16[256,384]{1,0:T(8,128)(2,1)S(1)}, u32[]{:S(2)}, u32[]{:S(2)}) collective-permute-start(bf16[256,384]{1,0:T(8,128)(2,1)S(1)} %collective-permute-done.11.t0), channel_id=1, source_target_pairs={{0,8},{1,9},{2,10},{3,11},{4,12},{5,13},{6,14},{7,15},{8,0},{9,1},... | collective-permute-start | bytes 589832 | tf_op jit(solution)/shard_map/ppermute | solution.py:329
  35.6 5.2 %collective-permute-start.3 = (bf16[128,384]{1,0:T(8,128)(2,1)S(1)}, bf16[128,384]{1,0:T(8,128)(2,1)S(1)}, u32[]{:S(2)}, u32[]{:S(2)}) collective-permute-start(bf16[128,384]{1,0:T(8,128)(2,1)S(1)} %get-tuple-element.17), channel_id=1, source_target_pairs={{0,0},{1,1},{2,8},{3,9},{4,4},{5,5},{6,12},{7,13},{8,2},{9,3},{10,... | collective-permute-start | bytes 294920 | tf_op jit(solution)/shard_map/ppermute | solution.py:329
  36.3 8.6 %collective-permute-start.6 = (bf16[128,384]{1,0:T(8,128)(2,1)S(1)}, bf16[128,384]{1,0:T(8,128)(2,1)S(1)}, u32[]{:S(2)}, u32[]{:S(2)}) collective-permute-start(bf16[128,384]{1,0:T(8,128)(2,1)S(1)} %get-tuple-element.18), channel_id=1, source_target_pairs={{0,5},{1,4},{2,13},{3,12},{4,1},{5,0},{6,9},{7,8},{8,7},{9,6},{10,... | collective-permute-start | bytes 294920 | tf_op jit(solution)/shard_map/ppermute | solution.py:329
  38.9 7.2 %collective-permute-start.4 = (bf16[128,384]{1,0:T(8,128)(2,1)S(1)}, bf16[128,384]{1,0:T(8,128)(2,1)S(1)}, u32[]{:S(2)}, u32[]{:S(2)}) collective-permute-start(bf16[128,384]{1,0:T(8,128)(2,1)S(1)} %get-tuple-element.18), channel_id=1, source_target_pairs={{0,1},{1,0},{2,9},{3,8},{4,5},{5,4},{6,13},{7,12},{8,3},{9,2},{10,... | collective-permute-start | bytes 294920 | tf_op jit(solution)/shard_map/ppermute | solution.py:329
  40.0 7.5 %collective-permute-start.14 = (bf16[256,384]{1,0:T(8,128)(2,1)S(1)}, bf16[256,384]{1,0:T(8,128)(2,1)S(1)}, u32[]{:S(2)}, u32[]{:S(2)}) collective-permute-start(bf16[256,384]{1,0:T(8,128)(2,1)S(1)} %collective-permute-done.12.t2), channel_id=1, source_target_pairs={{0,8},{1,9},{2,10},{3,11},{4,12},{5,13},{6,14},{7,15},{8,0},{9,1},... | collective-permute-start | bytes 589832 | tf_op jit(solution)/shard_map/ppermute | solution.py:329
  40.9 5.7 %collective-permute-start.9 = (bf16[128,384]{1,0:T(8,128)(2,1)S(1)}, bf16[128,384]{1,0:T(8,128)(2,1)S(1)}, u32[]{:S(2)}, u32[]{:S(2)}) collective-permute-start(bf16[128,384]{1,0:T(8,128)(2,1)S(1)} %collective-permute-done.5.c10), channel_id=1, source_target_pairs={{0,8},{1,9},{2,10},{3,11},{4,12},{5,13},{6,14},{7,15},{8,0},{9,1},... | collective-permute-start | bytes 294920 | tf_op jit(solution)/shard_map/ppermute | solution.py:329
  44.9 1.8 %collective-permute-start.7 = (bf16[128,384]{1,0:T(8,128)(2,1)S(1)}, bf16[128,384]{1,0:T(8,128)(2,1)S(1)}, u32[]{:S(2)}, u32[]{:S(2)}) collective-permute-start(bf16[128,384]{1,0:T(8,128)(2,1)S(1)} %collective-permute-done.3.c00), channel_id=1, source_target_pairs={{0,8},{1,9},{2,10},{3,11},{4,12},{5,13},{6,14},{7,15},{8,0},{9,1},... | collective-permute-start | bytes 294920 | tf_op jit(solution)/shard_map/ppermute | solution.py:329
  46.0 1.3 %collective-permute-start.10 = (bf16[128,384]{1,0:T(8,128)(2,1)S(1)}, bf16[128,384]{1,0:T(8,128)(2,1)S(1)}, u32[]{:S(2)}, u32[]{:S(2)}) collective-permute-start(bf16[128,384]{1,0:T(8,128)(2,1)S(1)} %collective-permute-done.6.c11), channel_id=1, source_target_pairs={{0,8},{1,9},{2,10},{3,11},{4,12},{5,13},{6,14},{7,15},{8,0},{9,1},... | collective-permute-start | bytes 294920 | tf_op jit(solution)/shard_map/ppermute | solution.py:329
  46.0 1.5 %collective-permute-start.8 = (bf16[128,384]{1,0:T(8,128)(2,1)S(1)}, bf16[128,384]{1,0:T(8,128)(2,1)S(1)}, u32[]{:S(2)}, u32[]{:S(2)}) collective-permute-start(bf16[128,384]{1,0:T(8,128)(2,1)S(1)} %collective-permute-done.4.c01), channel_id=1, source_target_pairs={{0,8},{1,9},{2,10},{3,11},{4,12},{5,13},{6,14},{7,15},{8,0},{9,1},... | collective-permute-start | bytes 294920 | tf_op jit(solution)/shard_map/ppermute | solution.py:329
  56.9 3.0 %collective-permute-start.17 = (bf16[256,384]{1,0:T(8,128)(2,1)S(1)}, bf16[256,384]{1,0:T(8,128)(2,1)S(1)}, u32[]{:S(2)}, u32[]{:S(2)}) collective-permute-start(bf16[256,384]{1,0:T(8,128)(2,1)S(1)} %get-tuple-element.22), channel_id=1, source_target_pairs={{0,0},{1,1},{2,8},{3,9},{4,4},{5,5},{6,12},{7,13},{8,2},{9,3},{10,... | collective-permute-start | bytes 589832 | tf_op jit(solution)/shard_map/ppermute | solution.py:329
  57.6 7.3 %collective-permute-start.18 = (bf16[256,384]{1,0:T(8,128)(2,1)S(1)}, bf16[256,384]{1,0:T(8,128)(2,1)S(1)}, u32[]{:S(2)}, u32[]{:S(2)}) collective-permute-start(bf16[256,384]{1,0:T(8,128)(2,1)S(1)} %get-tuple-element.23), channel_id=1, source_target_pairs={{0,1},{1,0},{2,9},{3,8},{4,5},{5,4},{6,13},{7,12},{8,3},{9,2},{10,... | collective-permute-start | bytes 589832 | tf_op jit(solution)/shard_map/ppermute | solution.py:329
  67.6 14.7 %collective-permute-start.19 = (bf16[2,128,384]{2,1,0:T(8,128)(2,1)S(1)}, bf16[2,128,384]{2,1,0:T(8,128)(2,1)S(1)}, u32[]{:S(2)}, u32[]{:S(2)}) collective-permute-start(bf16[2,128,384]{2,1,0:T(8,128)(2,1)S(1)} %shard_map.102), channel_id=1, source_target_pairs={{8,0},{16,8},{24,16},{32,24},{40,32},{48,40},{56,48},{64,56},{72,6... | collective-permute-start | bytes 589832 | tf_op jit(solution)/shard_map/ppermute | solution.py:398
  74.6 5.3 %collective-permute-start.15 = (bf16[128,384]{1,0:T(8,128)(2,1)S(1)}, bf16[128,384]{1,0:T(8,128)(2,1)S(1)}, u32[]{:S(2)}, u32[]{:S(2)}) collective-permute-start(bf16[128,384]{1,0:T(8,128)(2,1)S(1)} %get-tuple-element.20), channel_id=1, source_target_pairs={{0,0},{1,1},{2,8},{3,9},{4,4},{5,5},{6,12},{7,13},{8,2},{9,3},{10,... | collective-permute-start | bytes 294920 | tf_op jit(solution)/shard_map/ppermute | solution.py:329
  75.2 7.0 %collective-permute-start.16 = (bf16[128,384]{1,0:T(8,128)(2,1)S(1)}, bf16[128,384]{1,0:T(8,128)(2,1)S(1)}, u32[]{:S(2)}, u32[]{:S(2)}) collective-permute-start(bf16[128,384]{1,0:T(8,128)(2,1)S(1)} %get-tuple-element.21), channel_id=1, source_target_pairs={{0,1},{1,0},{2,9},{3,8},{4,5},{5,4},{6,13},{7,12},{8,3},{9,2},{10,... | collective-permute-start | bytes 294920 | tf_op jit(solution)/shard_map/ppermute | solution.py:329
where the time goes:
time: 84.5 us; the launch traced here: 83.7 us
  starting transfers between devices  37.2 us (44%)
  Pallas kernels  26.4 us (31%)
  waiting for transfers between devices  19 us (22%)
  between operations  1.04 us (1%)
    ppermute x18, starting transfers between devices, send(): return lax.ppermute(value, ('tm', 'rows'), pairs)  24.4 us
    pallas_call x8, Pallas kernels, call(): pl.pallas_call(kernel, in_specs=specs, out_specs=[VM] * len(shapes), out_...  15.7 us
    ppermute x18, waiting for transfers between devices, send(): return lax.ppermute(value, ('tm', 'rows'), pairs)  15.3 us
    pallas_call x1, Pallas kernels, attention(): pl.pallas_call(attention_kernel, in_specs=[SM] + [VM] * (len(convs) + len...  9.39 us
    ppermute x1, starting transfers between devices, local(): handed = lax.ppermute(for_last, 'tm', [(i + 1, i) for i in range(runs - 1)])  6.97 us
    ppermute x1, starting transfers between devices, local(): cached = lax.ppermute(for_next, 'tm', [(i, i + 1) for i in range(runs - 1)])  5.89 us
    ppermute x1, waiting for transfers between devices, local(): cached = lax.ppermute(for_next, 'tm', [(i, i + 1) for i in range(runs - 1)])  3.69 us
  transfers between devices with their start and end apart: 20, of which 10 were waited for; matrix products, arithmetic and copies ran while one was open for 0% of the time, Pallas kernels for 14%

commit v1 on v0

v1 whole, which is shorter than its diff:
```python
import functools

import jax
import jax.numpy as jnp
from jax import lax
from jax.experimental import pallas as pl
from jax.experimental.pallas import tpu as pltpu
from jax.sharding import PartitionSpec as P


F32 = jnp.float32
BF16 = jnp.bfloat16
MIB = 1024 * 1024
LOAD = 42 * MIB
VM = pl.BlockSpec(memory_space=pltpu.VMEM)
SM = pl.BlockSpec(memory_space=pltpu.SMEM)
HBM = pl.BlockSpec(memory_space=pltpu.HBM)


def call(kernel, operands, specs, shapes, scratch, limit, cost=0, outs=VM):
    return pl.pallas_call(
        kernel,
        in_specs=specs,
        out_specs=[outs] * len(shapes),
        out_shape=[jax.ShapeDtypeStruct(dims, dtype) for dims, dtype in shapes],
        scratch_shapes=scratch,
        compiler_params=pltpu.CompilerParams(vmem_limit_bytes=limit),
        cost_estimate=pl.CostEstimate(flops=cost, bytes_accessed=1 << 20, transcendentals=0),
    )(*operands)


def pick_kernel(place, first, second, same, other):
    x = place[0]
    half = first.shape[1]
    for n, ref in enumerate((first, second)):
        same[n * half : (n + 1) * half] = ref[x]
        other[n * half : (n + 1) * half] = ref[1 - x]


def pick(place, first, second):
    shape = (2 * first.shape[1], first.shape[2])
    return call(pick_kernel, (place, first, second), [SM, VM, VM], [(shape, BF16)] * 2, [], 8 * MIB)


def merge_kernel(place, own, cached, same, other):
    x = place[0]
    same[...] = (own[x] + cached[x].astype(F32)).astype(BF16)
    other[...] = (own[1 - x] + cached[1 - x].astype(F32)).astype(BF16)


def merge(place, own, cached):
    return call(
        merge_kernel, (place, own, cached), [SM, VM, VM], [(own.shape[1:], BF16)] * 2, [], 8 * MIB
    )


def load_kernel(w_hbm, w_out, sem):
    copy = pltpu.make_async_copy(w_hbm, w_out, sem)
    copy.start()
    copy.wait()


def load(weight):
    return call(
        load_kernel, (weight,), [HBM], [(weight.shape, BF16)], [pltpu.SemaphoreType.DMA], LOAD
    )[0]


def deliver_kernel(place, out0, out1, block_out, sems):
    x = place[0]
    copies = [
        pltpu.make_async_copy(out0, block_out.at[x], sems.at[0]),
        pltpu.make_async_copy(out1, block_out.at[1 - x], sems.at[1]),
    ]
    for copy in copies:
        copy.start()
    for copy in copies:
        copy.wait()


def deliver(place, out0, out1):
    return call(
        deliver_kernel, (place, out0, out1), [SM, VM, VM], [((2,) + out0.shape, BF16)],
        [pltpu.SemaphoreType.DMA((2,))], 8 * MIB, outs=HBM,
    )[0]


def finish_kernel(own, handed, video_grad, total, sems):
    copies = []
    for f in range(2):
        total[f] = (own[f] + handed[f].astype(F32)).astype(BF16)
        copies.append(pltpu.make_async_copy(total.at[f], video_grad.at[f], sems.at[f]))
        copies[f].start()
    for copy in copies:
        copy.wait()


def finish(own, handed):
    return call(
        finish_kernel, (own, handed), [VM, VM], [(own.shape, BF16)],
        [pltpu.VMEM(own.shape, BF16), pltpu.SemaphoreType.DMA((2,))], 8 * MIB, outs=HBM,
    )[0]


def spread(rows_f32, width):
    n = rows_f32.shape[0]
    col = lax.broadcasted_iota(jnp.int32, rows_f32.shape, 0) % width
    left = jnp.where(col == 0, 0.0, pltpu.roll(rows_f32, 1, 0))
    right = jnp.where(col == width - 1, 0.0, pltpu.roll(rows_f32, n - 1, 0))
    return left, rows_f32, right


def fill(taps, frame, row, block, width, flip):
    n, _, chans = block.shape
    shifted = spread(block.astype(F32).reshape(n * width, chans), width)
    if flip:
        shifted = shifted[::-1]
    for c in range(3):
        taps[frame, row : row + n, :, c * chans : (c + 1) * chans] = (
            shifted[c].astype(BF16).reshape(n, width, chans)
        )


def conv_steps(taps, w_ref, main, side, out, src, dst, transposed):
    chans = w_ref.shape[-1]

    def times(lhs, a, b):
        if not transposed:
            return mm(lhs, w_ref[a, b].reshape(3 * chans, chans))
        return mm_t(lhs, jnp.concatenate([w_ref[a, b, c] for c in range(3)], axis=1))

    both = extra = None
    for b in range(3):
        row = (2 - b) if transposed else b
        lhs = [taps[f, row : row + 2] for f in range(2)]
        lhs = [v.reshape(v.shape[0] * v.shape[1], v.shape[2]) for v in lhs]
        term = times(jnp.concatenate(lhs, axis=0), main, b)
        both = term if both is None else both + term
        term = times(lhs[src], side, b)
        extra = term if extra is None else extra + term
    half = both.shape[0] // 2
    for f in range(2):
        term = both[f * half : (f + 1) * half]
        out[f] = (term + extra if f == dst else term).astype(out.dtype)


def forward_kernel(main, side, src, dst, place, near, mid, far, w_ref, out, taps):
    width = mid.shape[2]
    swapped = place[0] == 1
    for f in range(2):
        fill(taps, f, 0, jnp.where(swapped, near[f], far[f])[None], width, False)
        fill(taps, f, 1, mid[f], width, False)
        fill(taps, f, 3, jnp.where(swapped, far[f], near[f])[None], width, False)
    conv_steps(taps, w_ref, main, side, out, src, dst, False)


def backward_kernel(main, side, src, dst, place, r0, r1, w_ref, out, taps):
    width, chans = taps.shape[2], w_ref.shape[-1]
    swapped = place[0] == 1
    for f, (a, b) in enumerate(((r0, r1), (r1, r0))):
        rows = jnp.where(swapped, b[...], a[...])
        fill(taps, f, 0, rows.reshape(4, width, chans), width, True)
    conv_steps(taps, w_ref, main, side, out, src, dst, True)


def conv_call(kernel, place, operands, weight, width, dtype):
    chans = weight.shape[-1]
    return call(
        kernel, (place, *operands, weight), [SM] + [VM] * (len(operands) + 1),
        [((2, 2 * width, chans), dtype)], [pltpu.VMEM((2, 4, width, 3 * chans), BF16)],
        24 * MIB, 2 * 9 * 3 * 128 * chans * chans,
    )[0]


def norm_parts(conv, gain):
    convf = conv.astype(F32)
    inverse = lax.rsqrt(jnp.mean(convf * convf, axis=-1, keepdims=True) + 1e-06)
    normed = convf * inverse * gain
    return convf, inverse, normed


def mm(a, b):
    return jnp.dot(a, b, preferred_element_type=F32)


def mm_t(a, b):
    return lax.dot_general(a, b, (((1,), (1,)), ((), ())), preferred_element_type=F32)


def t_mm(a, b):
    return lax.dot_general(a, b, (((0,), (0,)), ((), ())), preferred_element_type=F32)


CHUNKS = ((0, 384), (384, 256), (640, 256), (896, 128))


def put(dst, value, place, quarter, kx):
    x, q = place[0], place[1]
    line = value.shape[0] // 2
    for j in range(2):
        slot = (4 * (quarter - q) + 2 * (x + kx - 2 * x * kx) + j + 17) % 16
        dst[pl.ds(pl.multiple_of(slot * line, line), line)] = value[j * line : (j + 1) * line]


def quarters(q):
    side = q + 1 - 2 * (q % 2)
    return q, (q + 2) % 4, side, (side + 2) % 4


def attend_kernel(
    place, c00, c01, c10, c11, s00, s01, s10, s11, gain_ref, wq, wk, wv, wo,
    q_s, k_s, v_s, p_s, conv_own, out0, out1, conv_s, out_s,
):
    x = place[0]
    line = c00.shape[0] // 2
    own = 6 * line
    chans = wq.shape[0]
    scale = 1.0 / jnp.sqrt(jnp.float32(chans))
    gain = gain_ref[...]
    q, far, side, far_side = quarters(place[1])
    for ref, quarter, kx in (
        (c00, q, 0), (c01, q, 1), (c10, far, 0), (c11, far, 1),
        (s00, side, 0), (s01, side, 1), (s10, far_side, 0), (s11, far_side, 1),
    ):
        put(conv_s, ref, place, quarter, kx)
    conv_own[...] = conv_s[:own]

    act_own = None
    for at, n in CHUNKS:
        rows = slice(at, at + n)
        _, _, normed = norm_parts(conv_s[rows], gain)
        act = (normed / (1.0 + jnp.exp(-normed))).astype(BF16)
        if at == 0:
            act_own = act[line : own - line]
        q_s[rows] = mm(act, wq[...]).astype(BF16)
        k_s[rows] = mm(act, wk[...]).astype(BF16)
        v_s[rows] = mm(act, wv[...]).astype(BF16)
    for at, n in CHUNKS:
        rows = slice(at, at + n)
        scores = mm_t(q_s[rows], k_s[...]) * scale
        top = jnp.max(scores, axis=-1, keepdims=True)
        expo = jnp.exp(scores - top)
        probs = (expo * (1.0 / jnp.sum(expo, axis=-1, keepdims=True))).astype(BF16)
        p_s[rows] = probs
        if at == 0:
            attended = mm(probs[line : own - line], v_s[...]).astype(BF16)
            out_s[...] = (act_own.astype(F32) + mm(attended, wo[...])).astype(BF16)
    for kx, ref in ((0, out0), (1, out1)):
        to_x = x if kx == 0 else 1 - x
        ref[...] = out_s[pl.ds(pl.multiple_of(2 * to_x * line, line), 2 * line)]


def attend(place, convs, gain, wq, wk, wv, wo):
    block, chans = convs[0].shape
    own, whole = 3 * block, 8 * block
    return call(
        attend_kernel, (place, *convs, gain, wq, wk, wv, wo), [SM] + [VM] * 13,
        [((whole, chans), BF16)] * 3
        + [((whole, whole), BF16), ((own, chans), BF16)]
        + [((block, chans), BF16)] * 2,
        [pltpu.VMEM((whole, chans), BF16), pltpu.VMEM((2 * block, chans), BF16)],
        26 * MIB, 2 * 10**9,
    )


def attend_grad_kernel(
    place, q_s, k_s, v_s, p_s, conv_own, same, other, same_side, other_side,
    gain_ref, wq, wk, wv, wo,
    grad0, grad1, cot_s, g_s, gk_s, gv_s, grad_s,
):
    x = place[0]
    block = same.shape[0] // 2
    line = block // 2
    own = 6 * line
    chans = wq.shape[0]
    scale = 1.0 / jnp.sqrt(jnp.float32(chans))
    gain = gain_ref[...]
    q, far, side, far_side = quarters(place[1])
    for kx, near_ref, side_ref in ((0, same, same_side), (1, other, other_side)):
        for n in range(2):
            half = slice(n * block, (n + 1) * block)
            put(cot_s, near_ref.at[half], place, (q, far)[n], kx)
            put(cot_s, side_ref.at[half], place, (side, far_side)[n], kx)

    grad_q = None
    for at, n in CHUNKS:
        rows = slice(at, at + n)
        g_s[rows] = mm_t(cot_s[rows], wo[...]).astype(BF16)
        dprob = mm_t(g_s[rows], v_s[...])
        if at == 0:
            probs = p_s[rows].astype(F32)
            delta = jnp.sum(probs * dprob, axis=-1, keepdims=True)
            dscore = (probs * (dprob - delta)).astype(BF16)
            grad_q = (mm(dscore, k_s[...]) * scale).astype(BF16)
            gk_s[...] = t_mm(dscore[:, :own], q_s[rows])
            gv_s[...] = t_mm(p_s[rows, :own], g_s[rows])
        else:
            delta = jnp.sum(p_s[rows].astype(F32) * dprob, axis=-1, keepdims=True)
            dscore = (p_s[rows, :own].astype(F32) * (dprob[:, :own] - delta)).astype(BF16)
            gk_s[...] += t_mm(dscore, q_s[rows])
            gv_s[...] += t_mm(p_s[rows, :own], g_s[rows])
    grad_act = cot_s[:own].astype(F32)
    grad_act = grad_act + mm_t(grad_q, wq[...])
    grad_act = grad_act + mm_t((gk_s[...] * scale).astype(BF16), wk[...])
    grad_act = grad_act + mm_t(gv_s[...].astype(BF16), wv[...])
    convf, inverse, normed = norm_parts(conv_own[...], gain)
    sigma = 1.0 / (1.0 + jnp.exp(-normed))
    scaled = grad_act * sigma * (1.0 + normed * (1.0 - sigma)) * gain
    mean = jnp.mean(scaled * convf, axis=-1, keepdims=True)
    grad_conv = inverse * (scaled - convf * inverse * inverse * mean)
    row = lax.broadcasted_iota(jnp.int32, grad_conv.shape, 0)
    first = jnp.where(q == 0, line, 0)
    last = jnp.where(q == 3, own - line, own)
    inside = jnp.logical_and(row >= first, row < last)
    grad_s[...] = jnp.where(inside, grad_conv, 0.0).astype(BF16)
    for kx, ref in ((0, grad0), (1, grad1)):
        to_x = x if kx == 0 else 1 - x
        ref[...] = grad_s[pl.ds(pl.multiple_of(2 * to_x * line, line), 4 * line)]


def attend_grad(place, saved, cots, gain, wq, wk, wv, wo):
    own, chans = saved[-1].shape
    whole = saved[0].shape[0]
    act = lambda n, t=BF16: pltpu.VMEM((n, chans), t)
    return call(
        attend_grad_kernel, (place, *saved, *cots, gain, wq, wk, wv, wo), [SM] + [VM] * 14,
        [((2 * own // 3, chans), BF16)] * 2,
        [act(whole), act(whole), act(own, F32), act(own, F32), act(own)],
        26 * MIB, 2 * 10**9,
    )


def site(h, c, y, x):
    return (h * 2 + c) * 8 + 2 * y + x


def send(value, runs, to):
    pairs = []
    for h in range(runs // 2):
        for c in range(2):
            for y in range(4):
                for x in range(2):
                    there = to(c, y, x)
                    if there is not None:
                        pairs.append((site(h, c, y, x), site(h, *there)))
    return lax.ppermute(value, ("tm", "rows"), pairs)


def home(ky, kx):
    return lambda c, y, x: (y % 2, 2 * ((y // 2 + ky) % 2) + c, x ^ kx)


def swap(c, y, x):
    return 1 - c, y, x


def across(c, y, x):
    return c, y, x ^ 1


def beyond(c, y, x):
    y = y + 1 if x else y - 1
    return (c, y, x ^ 1) if 0 <= y < 4 else None


def local(video, conv_weight, norm_gain, w_query, w_key, w_value, w_out, cotangent):
    frames, height, width, chans = video.shape
    runs, slabs = lax.axis_size("tm"), lax.axis_size("rows")
    assert (frames, height, slabs) == (2, 2, 8)
    slab_at = lax.axis_index("rows")
    x = slab_at % 2
    quarter = 2 * (slab_at // 4) + lax.axis_index("tm") % 2
    place = jnp.stack([x, quarter]).astype(jnp.int32)
    block = 2 * width

    cot_b = send(cotangent.reshape(2, block, chans), runs, home(0, 0))
    far = send(lax.dynamic_index_in_dim(video, x, 1, keepdims=False), runs, beyond)
    near = send(lax.dynamic_index_in_dim(video, 1 - x, 1, keepdims=False), runs, across)
    weight = load(conv_weight)
    slab = (near, video, far)

    def forward(main, side, src, dst, dtype):
        kernel = functools.partial(forward_kernel, main, side, src, dst)
        return conv_call(kernel, place, slab, weight, width, dtype)

    def backward(main, side, src, dst, dtype):
        kernel = functools.partial(backward_kernel, main, side, src, dst)
        return conv_call(kernel, place, slab, weight, width, dtype)

    for_next = forward(0, 1, 1, 0, BF16)
    cached = lax.ppermute(for_next, "tm", [(i, i + 1) for i in range(runs - 1)])
    own = forward(2, 1, 0, 1, F32)
    cot_c = send(cot_b, runs, lambda c, y, x: (c, y ^ 2, x))
    cot_same, cot_other = pick(place, cot_b, cot_c)
    same, other = merge(place, own, cached)
    got, swapped = {}, {}
    for ky, kx in ((1, 1), (0, 1), (1, 0), (0, 0)):
        got[ky, kx] = send(other if kx else same, runs, home(ky, kx))
    for ky, kx in ((1, 1), (0, 1), (1, 0), (0, 0)):
        swapped[ky, kx] = send(got[ky, kx], runs, swap)
    order = ((0, 0), (0, 1), (1, 0), (1, 1))
    convs = [got[k] for k in order] + [swapped[k] for k in order]

    cot_other = send(cot_other, runs, across)
    projections = (norm_gain.reshape(1, chans), w_query, w_key, w_value, w_out)
    *saved, out0, out1 = attend(place, convs, *projections)
    cots = (
        cot_same, cot_other,
        send(cot_same, runs, swap), send(cot_other, runs, swap),
    )
    out1 = send(out1, runs, home(0, 1))
    out0 = send(out0, runs, home(0, 0))
    grad0, grad1 = attend_grad(place, saved, cots, *projections)
    grad1 = send(grad1, runs, home(0, 1))
    grad0 = send(grad0, runs, home(0, 0))
    slab = (grad0, grad1)
    for_last = backward(0, 1, 0, 1, BF16)
    handed = lax.ppermute(for_last, "tm", [(i + 1, i) for i in range(runs - 1)])
    own_grad = backward(2, 1, 1, 0, F32)
    block_out = deliver(place, out0, out1)
    video_grad = finish(own_grad, handed)
    return block_out.reshape(video.shape), video_grad.reshape(video.shape)


def solution(mesh):
    spec = P("tm", "rows", None, None)
    return jax.shard_map(
        local,
        mesh=mesh,
        in_specs=(spec, P(), P(), P(), P(), P(), P(), spec),
        out_specs=(spec, spec),
        check_vma=False,
    )
```

time: 84.5 us -> 92.9 us (1.099)
  local copies, waits for them, and re-layouts: 0.03 us -> 7.34 us
  waiting for transfers between devices: 19 us -> 22.6 us
  starting transfers between devices: 37.2 us -> 33.9 us
    unnamed x10 -> x20, local copies, waits for them, and re-layouts: 0.03 us -> 6.37 us
    ppermute x1, waiting for transfers between devices: 3.69 us -> 5.92 us  [local(): cached = lax.ppermute(for_next, 'tm', [(i, i + 1) for i in range(runs - 1)])]
    ppermute x1, starting transfers between devices: 5.89 us -> 3.96 us  [local(): cached = lax.ppermute(for_next, 'tm', [(i, i + 1) for i in range(runs - 1)])]
    ppermute x18 -> x19, starting transfers between devices: 24.4 us -> 22.9 us  [send(): return lax.ppermute(value, ('tm', 'rows'), pairs)]
    ppermute x18 -> x19, waiting for transfers between devices: 15.3 us -> 16.7 us  [send(): return lax.ppermute(value, ('tm', 'rows'), pairs)]
    squeeze x0 -> x1, local copies, waits for them, and re-layouts: none -> 0.97 us  [local(): lax.dynamic_index_in_dim(video, x, 1, keepdims=False)]
    pallas_call x10 -> x11, Pallas kernels: 26.4 us -> 27 us  [call(): pl.pallas_call(kernel, in_specs=specs, out_specs=[outs] * len(shapes), ou...]
  transfers between devices with their start and end apart: 20 -> 21, of which waited for: 10 -> 6; matrix products, arithmetic and copies ran while one was open for 0% -> 0% of each run, Pallas kernels for 14% -> 19%
where the time goes in v1:
time: 92.9 us; the launch traced here: 92.1 us
  starting transfers between devices  33.9 us (36%)
  Pallas kernels  27 us (29%)
  waiting for transfers between devices  22.6 us (24%)
  local copies, waits for them, and re-layouts  7.34 us (8%)
  between operations  1.06 us (1%)
    pallas_call x11, Pallas kernels, call(): pl.pallas_call(kernel, in_specs=specs, out_specs=[outs] * len(shapes), ou...  27 us
    ppermute x19, starting transfers between devices, send(): return lax.ppermute(value, ('tm', 'rows'), pairs)  22.9 us
    ppermute x19, waiting for transfers between devices, send(): return lax.ppermute(value, ('tm', 'rows'), pairs)  16.7 us
    ppermute x1, starting transfers between devices, local(): handed = lax.ppermute(for_last, 'tm', [(i + 1, i) for i in range(runs - 1)])  7.06 us
    unnamed x20, local copies, waits for them, and re-layouts  6.37 us
    ppermute x1, waiting for transfers between devices, local(): cached = lax.ppermute(for_next, 'tm', [(i, i + 1) for i in range(runs - 1)])  5.92 us
    ppermute x1, starting transfers between devices, local(): cached = lax.ppermute(for_next, 'tm', [(i, i + 1) for i in range(runs - 1)])  3.96 us
  transfers between devices with their start and end apart: 21, of which 6 were waited for; matrix products, arithmetic and copies ran while one was open for 0% of the time, Pallas kernels for 19%

profile of v1, /device:TPU:6, one launch (start us, length us, event | category | flops | bytes accessed | tf_op | source)
XLA Modules:
  0.0 92.1 jit_solution(14860355376699515489)
XLA Ops:
  0.7 1.0 %dynamic-slice_bitcast_fusion = (bf16[2,64,384]{2,1,0:T(8,128)(2,1)S(1)}, bf16[2,64,384]{2,1,0:T(8,128)(2,1)S(1)}) fusion(bf16[2,2,64,384]{3,2,1,0:T(8,128)(2,1)} %mid.3, s32[]{:T(128)S(6)} %select_n.26, s32[]{:T(128)S(6)} %select_n.25), kind=kLoop, calls=%fused_computation | loop fusion | bytes 393224 | tf_op jit(solution)/shard_map/jit(dynamic_index_in_dim)/squeeze | solution.py:377
  1.6 1.5 %collective-permute-start = (bf16[2,64,384]{2,1,0:T(8,128)(2,1)S(1)}, bf16[2,64,384]{2,1,0:T(8,128)(2,1)S(1)}, u32[]{:S(2)}, u32[]{:S(2)}) collective-permute-start(bf16[2,64,384]{2,1,0:T(8,128)(2,1)S(1)} %get-tuple-element.29), channel_id=1, source_target_pairs={{0,1},{1,0},{2,3},{3,2},{4,5},{5,4},{6,7},{7,6},{8,9},{9,8},{10,11... | collective-permute-start | bytes 294920 | tf_op jit(solution)/shard_map/ppermute | solution.py:346
  3.1 5.0 %collective-permute-start.1 = (bf16[2,64,384]{2,1,0:T(8,128)(2,1)S(1)}, bf16[2,64,384]{2,1,0:T(8,128)(2,1)S(1)}, u32[]{:S(2)}, u32[]{:S(2)}) collective-permute-start(bf16[2,64,384]{2,1,0:T(8,128)(2,1)S(1)} %get-tuple-element.28), channel_id=1, source_target_pairs={{1,2},{2,1},{3,4},{4,3},{5,6},{6,5},{9,10},{10,9},{11,12},{12,11},... | collective-permute-start | bytes 294920 | tf_op jit(solution)/shard_map/ppermute | solution.py:346
  8.2 1.6 %collective-permute-start.13 = (bf16[2,128,384]{2,1,0:T(8,128)(2,1)}, bf16[2,128,384]{2,1,0:T(8,128)(2,1)S(1)}, u32[]{:S(2)}, u32[]{:S(2)}) collective-permute-start(bf16[2,128,384]{2,1,0:T(8,128)(2,1)} %bitcast.13), channel_id=1, source_target_pairs={{0,0},{1,1},{2,8},{3,9},{4,4},{5,5},{6,12},{7,13},{8,2},{9,3},{10,... | collective-permute-start | bytes 589832 | tf_op jit(solution)/shard_map/ppermute | solution.py:346
  9.8 3.3 %shard_map.95.w_ref = bf16[3,3,3,384,384]{4,3,2,1,0:T(8,128)(2,1)S(1)} custom-call(bf16[3,3,3,384,384]{4,3,2,1,0:T(8,128)(2,1)} %w_hbm.1), custom_call_target="tpu_custom_call" | custom-call | bytes 1048576 | tf_op jit(solution)/shard_map/pallas_call | solution.py:21
  13.1 3.1 %copy-done = bf16[3,3,3,384,384]{4,3,2,1,0:T(8,128)(2,1)} copy-done((bf16[3,3,3,384,384]{4,3,2,1,0:T(8,128)(2,1)}, bf16[3,3,3,384,384]{4,3,2,1,0:T(8,128)(2,1)S(1)}, u32[]{:S(2)}) %copy-start) | copy-done | bytes 7962648
  16.3 3.3 %copy-done.1 = bf16[3,3,3,384,384]{4,3,2,1,0:T(8,128)(2,1)S(1)} copy-done((bf16[3,3,3,384,384]{4,3,2,1,0:T(8,128)(2,1)S(1)}, bf16[3,3,3,384,384]{4,3,2,1,0:T(8,128)(2,1)}, u32[]{:S(2)}) %copy-start.1) | copy-done | bytes 7962648
  19.5 2.2 %shard_map.97 = bf16[2,128,384]{2,1,0:T(8,128)(2,1)S(1)} custom-call(s32[2]{0:T(128)S(1)} %pad_add_fusion.place, bf16[2,64,384]{2,1,0:T(8,128)(2,1)S(1)} %collective-permute-done.near, bf16[2,2,64,384]{3,2,1,0:T(8,128)(2,1)S(1)} %copy-done.2, bf16[2,64,384]{2,1,0:T(8,128)(2,1)S(1)} %collective-permute-done.1.far, bf16[3,3,3,384,384]{4,3,2,1,0:T(8,128)(2,1)S(1)} %copy-done.1), custom_call_target="tpu_custom_call" | custom-call | flops 1019215872 | bytes 1048576 | tf_op jit(solution)/shard_map/pallas_call | solution.py:21
  21.7 4.0 %collective-permute-start.2 = (bf16[2,128,384]{2,1,0:T(8,128)(2,1)S(1)}, bf16[2,128,384]{2,1,0:T(8,128)(2,1)S(1)}, u32[]{:S(2)}, u32[]{:S(2)}) collective-permute-start(bf16[2,128,384]{2,1,0:T(8,128)(2,1)S(1)} %shard_map.97), channel_id=1, source_target_pairs={{0,8},{8,16},{16,24},{24,32},{32,40},{40,48},{48,56},{56,64},{64,7... | collective-permute-start | bytes 589832 | tf_op jit(solution)/shard_map/ppermute | solution.py:391
  25.7 0.9 %collective-permute-start.14 = (bf16[2,128,384]{2,1,0:T(8,128)(2,1)S(1)}, bf16[2,128,384]{2,1,0:T(8,128)(2,1)S(1)}, u32[]{:S(2)}, u32[]{:S(2)}) collective-permute-start(bf16[2,128,384]{2,1,0:T(8,128)(2,1)S(1)} %collective-permute-done.13.first), channel_id=1, source_target_pairs={{0,4},{1,5},{2,6},{3,7},{4,0},{5,1},{6,2},{7,3},{8,12},{9,13},{10,... | collective-permute-start | bytes 589832 | tf_op jit(solution)/shard_map/ppermute | solution.py:346
  26.6 2.2 %shard_map.96.own = f32[2,128,384]{2,1,0:T(8,128)S(1)} custom-call(s32[2]{0:T(128)S(1)} %pad_add_fusion.place, bf16[2,64,384]{2,1,0:T(8,128)(2,1)S(1)} %collective-permute-done.near, bf16[2,2,64,384]{3,2,1,0:T(8,128)(2,1)S(1)} %copy-done.2, bf16[2,64,384]{2,1,0:T(8,128)(2,1)S(1)} %collective-permute-done.1.far, bf16[3,3,3,384,384]{4,3,2,1,0:T(8,128)(2,1)S(1)} %copy-done.1), custom_call_target="tpu_custom_call" | custom-call | flops 1019215872 | bytes 1048576 | tf_op jit(solution)/shard_map/pallas_call | solution.py:21
  28.8 5.9 %collective-permute-done.2.cached = bf16[2,128,384]{2,1,0:T(8,128)(2,1)S(1)} collective-permute-done((bf16[2,128,384]{2,1,0:T(8,128)(2,1)S(1)}, bf16[2,128,384]{2,1,0:T(8,128)(2,1)S(1)}, u32[]{:S(2)}, u32[]{:S(2)}) %collective-permute-start.2) | collective-permute-done | bytes 196640 | tf_op jit(solution)/shard_map/ppermute | solution.py:391
  34.8 0.6 shard_map.98
  35.4 0.7 collective-permute-start.3
  36.0 0.6 shard_map.101
  36.7 3.5 %collective-permute-start.4 = (bf16[128,384]{1,0:T(8,128)(2,1)S(1)}, bf16[128,384]{1,0:T(8,128)(2,1)S(1)}, u32[]{:S(2)}, u32[]{:S(2)}) collective-permute-start(bf16[128,384]{1,0:T(8,128)(2,1)S(1)} %get-tuple-element.16), channel_id=1, source_target_pairs={{0,1},{1,0},{2,9},{3,8},{4,5},{5,4},{6,13},{7,12},{8,3},{9,2},{10,... | collective-permute-start | bytes 294920 | tf_op jit(solution)/shard_map/ppermute | solution.py:346
  40.7 2.6 %collective-permute-start.6 = (bf16[128,384]{1,0:T(8,128)(2,1)S(1)}, bf16[128,384]{1,0:T(8,128)(2,1)S(1)}, u32[]{:S(2)}, u32[]{:S(2)}) collective-permute-start(bf16[128,384]{1,0:T(8,128)(2,1)S(1)} %get-tuple-element.16), channel_id=1, source_target_pairs={{0,5},{1,4},{2,13},{3,12},{4,1},{5,0},{6,9},{7,8},{8,7},{9,6},{10,... | collective-permute-start | bytes 294920 | tf_op jit(solution)/shard_map/ppermute | solution.py:346
  43.3 4.6 %collective-permute-done.4.c01 = bf16[128,384]{1,0:T(8,128)(2,1)S(1)} collective-permute-done((bf16[128,384]{1,0:T(8,128)(2,1)S(1)}, bf16[128,384]{1,0:T(8,128)(2,1)S(1)}, u32[]{:S(2)}, u32[]{:S(2)}) %collective-permute-start.4) | collective-permute-done | bytes 98336 | tf_op jit(solution)/shard_map/ppermute | solution.py:346
  48.5 1.7 %collective-permute-done.6.c11 = bf16[128,384]{1,0:T(8,128)(2,1)S(1)} collective-permute-done((bf16[128,384]{1,0:T(8,128)(2,1)S(1)}, bf16[128,384]{1,0:T(8,128)(2,1)S(1)}, u32[]{:S(2)}, u32[]{:S(2)}) %collective-permute-start.6) | collective-permute-done | bytes 98336 | tf_op jit(solution)/shard_map/ppermute | solution.py:346
  51.5 5.1 %shard_map.99 = (bf16[1024,384]{1,0:T(8,128)(2,1)S(1)}, bf16[1024,384]{1,0:T(8,128)(2,1)S(1)}, bf16[1024,384]{1,0:T(8,128)(2,1)S(1)}, bf16[1024,1024]{1,0:T(8,12...) custom-call(s32[2]{0:T(128)S(1)} %pad_add_fusion.place, ...), custom_call_target="tpu_custom_call" | custom-call | flops 2000000000 | bytes 1048576 | tf_op jit(solution)/shard_map/pallas_call | solution.py:21
  56.6 6.1 %shard_map.102 = (bf16[256,384]{1,0:T(8,128)(2,1)S(1)}, bf16[256,384]{1,0:T(8,128)(2,1)S(1)}) custom-call(s32[2]{0:T(128)S(1)} %pad_add_fusion.place, bf16[1024,384]{1,0:T(8,128)(2,1)S(1)} %get-tuple-element.19.q_s, bf16[1024,384]{1,0:T(8,128)(2,1)S(1)} %get-tuple-element.20.k_s, bf16[1024,384]{1,0:T(8,128)(2,1)S(1)} %get-tuple-element.21.v_s, ...), custom_call_target="tpu_custom_call" | custom-call | flops 2000000000 | bytes 1048576 | tf_op jit(solution)/shard_map/pallas_call | solution.py:21
  62.8 0.7 collective-permute-start.18
  63.4 1.9 %collective-permute-start.19 = (bf16[256,384]{1,0:T(8,128)(2,1)S(1)}, bf16[256,384]{1,0:T(8,128)(2,1)S(1)}, u32[]{:S(2)}, u32[]{:S(2)}) collective-permute-start(bf16[256,384]{1,0:T(8,128)(2,1)S(1)} %get-tuple-element.27), channel_id=1, source_target_pairs={{0,1},{1,0},{2,9},{3,8},{4,5},{5,4},{6,13},{7,12},{8,3},{9,2},{10,... | collective-permute-start | bytes 589832 | tf_op jit(solution)/shard_map/ppermute | solution.py:346
  65.4 5.6 %collective-permute-done.19.r1 = bf16[256,384]{1,0:T(8,128)(2,1)S(1)} collective-permute-done((bf16[256,384]{1,0:T(8,128)(2,1)S(1)}, bf16[256,384]{1,0:T(8,128)(2,1)S(1)}, u32[]{:S(2)}, u32[]{:S(2)}) %collective-permute-start.19) | collective-permute-done | bytes 196640 | tf_op jit(solution)/shard_map/ppermute | solution.py:346
  71.0 2.5 %shard_map.104 = bf16[2,128,384]{2,1,0:T(8,128)(2,1)S(1)} custom-call(s32[2]{0:T(128)S(1)} %pad_add_fusion.place, bf16[256,384]{1,0:T(8,128)(2,1)S(1)} %collective-permute-done.18.r0, bf16[256,384]{1,0:T(8,128)(2,1)S(1)} %collective-permute-done.19.r1, bf16[3,3,3,384,384]{4,3,2,1,0:T(8,128)(2,1)S(1)} %bitcast.10), custom_call_target="tpu_custom_call" | custom-call | flops 1019215872 | bytes 1048576 | tf_op jit(solution)/shard_map/pallas_call | solution.py:21
  73.5 7.1 %collective-permute-start.20 = (bf16[2,128,384]{2,1,0:T(8,128)(2,1)S(1)}, bf16[2,128,384]{2,1,0:T(8,128)(2,1)S(1)}, u32[]{:S(2)}, u32[]{:S(2)}) collective-permute-start(bf16[2,128,384]{2,1,0:T(8,128)(2,1)S(1)} %shard_map.104), channel_id=1, source_target_pairs={{8,0},{16,8},{24,16},{32,24},{40,32},{48,40},{56,48},{64,56},{72,6... | collective-permute-start | bytes 589832 | tf_op jit(solution)/shard_map/ppermute | solution.py:418
  80.5 0.7 collective-permute-start.11
  81.2 2.0 %collective-permute-start.12 = (bf16[128,384]{1,0:T(8,128)(2,1)S(1)}, bf16[128,384]{1,0:T(8,128)(2,1)S(1)}, u32[]{:S(2)}, u32[]{:S(2)}) collective-permute-start(bf16[128,384]{1,0:T(8,128)(2,1)S(1)} %get-tuple-element.18), channel_id=1, source_target_pairs={{0,1},{1,0},{2,9},{3,8},{4,5},{5,4},{6,13},{7,12},{8,3},{9,2},{10,... | collective-permute-start | bytes 294920 | tf_op jit(solution)/shard_map/ppermute | solution.py:346
  83.2 4.2 %collective-permute-done.12.out1 = bf16[128,384]{1,0:T(8,128)(2,1)S(1)} collective-permute-done((bf16[128,384]{1,0:T(8,128)(2,1)S(1)}, bf16[128,384]{1,0:T(8,128)(2,1)S(1)}, u32[]{:S(2)}, u32[]{:S(2)}) %collective-permute-start.12) | collective-permute-done | bytes 98336 | tf_op jit(solution)/shard_map/ppermute | solution.py:346
  87.4 1.2 %shard_map.100 = bf16[2,128,384]{2,1,0:T(8,128)(2,1)} custom-call(s32[2]{0:T(128)S(1)} %pad_add_fusion.place, bf16[128,384]{1,0:T(8,128)(2,1)S(1)} %collective-permute-done.11.out0, bf16[128,384]{1,0:T(8,128)(2,1)S(1)} %collective-permute-done.12.out1), custom_call_target="tpu_custom_call" | custom-call | bytes 1048576 | tf_op jit(solution)/shard_map/pallas_call | solution.py:21
  88.7 2.5 %shard_map.103.own = f32[2,128,384]{2,1,0:T(8,128)S(1)} custom-call(s32[2]{0:T(128)S(1)} %pad_add_fusion.place, bf16[256,384]{1,0:T(8,128)(2,1)S(1)} %collective-permute-done.18.r0, bf16[256,384]{1,0:T(8,128)(2,1)S(1)} %collective-permute-done.19.r1, bf16[3,3,3,384,384]{4,3,2,1,0:T(8,128)(2,1)S(1)} %bitcast.10), custom_call_target="tpu_custom_call" | custom-call | flops 1019215872 | bytes 1048576 | tf_op jit(solution)/shard_map/pallas_call | solution.py:21
  91.2 0.7 shard_map.105
  (45 shorter events, 2.5 us)
Async XLA Ops:
  1.6 14.6 %collective-permute-start = (bf16[2,64,384]{2,1,0:T(8,128)(2,1)S(1)}, bf16[2,64,384]{2,1,0:T(8,128)(2,1)S(1)}, u32[]{:S(2)}, u32[]{:S(2)}) collective-permute-start(bf16[2,64,384]{2,1,0:T(8,128)(2,1)S(1)} %get-tuple-element.29), channel_id=1, source_target_pairs={{0,1},{1,0},{2,3},{3,2},{4,5},{5,4},{6,7},{7,6},{8,9},{9,8},{10,11... | collective-permute-start | bytes 294920 | tf_op jit(solution)/shard_map/ppermute | solution.py:346
  3.1 13.1 %collective-permute-start.1 = (bf16[2,64,384]{2,1,0:T(8,128)(2,1)S(1)}, bf16[2,64,384]{2,1,0:T(8,128)(2,1)S(1)}, u32[]{:S(2)}, u32[]{:S(2)}) collective-permute-start(bf16[2,64,384]{2,1,0:T(8,128)(2,1)S(1)} %get-tuple-element.28), channel_id=1, source_target_pairs={{1,2},{2,1},{3,4},{4,3},{5,6},{6,5},{9,10},{10,9},{11,12},{12,11},... | collective-permute-start | bytes 294920 | tf_op jit(solution)/shard_map/ppermute | solution.py:346
  8.2 17.5 %collective-permute-start.13 = (bf16[2,128,384]{2,1,0:T(8,128)(2,1)}, bf16[2,128,384]{2,1,0:T(8,128)(2,1)S(1)}, u32[]{:S(2)}, u32[]{:S(2)}) collective-permute-start(bf16[2,128,384]{2,1,0:T(8,128)(2,1)} %bitcast.13), channel_id=1, source_target_pairs={{0,0},{1,1},{2,8},{3,9},{4,4},{5,5},{6,12},{7,13},{8,2},{9,3},{10,... | collective-permute-start | bytes 589832 | tf_op jit(solution)/shard_map/ppermute | solution.py:346
  9.7 6.5 %copy-start.2 = (bf16[2,2,64,384]{3,2,1,0:T(8,128)(2,1)S(1)}, bf16[2,2,64,384]{3,2,1,0:T(8,128)(2,1)}, u32[]{:S(2)}) copy-start(bf16[2,2,64,384]{3,2,1,0:T(8,128)(2,1)} %mid.3) | copy-start | bytes 589828
  13.1 3.1 %copy-start = (bf16[3,3,3,384,384]{4,3,2,1,0:T(8,128)(2,1)}, bf16[3,3,3,384,384]{4,3,2,1,0:T(8,128)(2,1)S(1)}, u32[]{:S(2)}) copy-start(bf16[3,3,3,384,384]{4,3,2,1,0:T(8,128)(2,1)S(1)} %shard_map.95.w_ref) | copy-start | bytes 23887876
  16.2 3.3 %copy-start.1 = (bf16[3,3,3,384,384]{4,3,2,1,0:T(8,128)(2,1)S(1)}, bf16[3,3,3,384,384]{4,3,2,1,0:T(8,128)(2,1)}, u32[]{:S(2)}) copy-start(bf16[3,3,3,384,384]{4,3,2,1,0:T(8,128)(2,1)} %copy-done) | copy-start | bytes 23887876
  19.5 31.5 %copy-start.7 = (f32[384]{0:T(512)S(1)}, f32[384]{0:T(512)}, u32[]{:S(2)}) copy-start(f32[384]{0:T(512)} %param.10) | copy-start | bytes 4612
  19.5 32.0 %copy-start.3 = (bf16[384,384]{1,0:T(8,128)(2,1)S(1)}, bf16[384,384]{1,0:T(8,128)(2,1)}, u32[]{:S(2)}) copy-start(bf16[384,384]{1,0:T(8,128)(2,1)} %wq.3) | copy-start | bytes 884740
  19.5 32.0 %copy-start.4 = (bf16[384,384]{1,0:T(8,128)(2,1)S(1)}, bf16[384,384]{1,0:T(8,128)(2,1)}, u32[]{:S(2)}) copy-start(bf16[384,384]{1,0:T(8,128)(2,1)} %wk.3) | copy-start | bytes 884740
  19.5 32.0 %copy-start.5 = (bf16[384,384]{1,0:T(8,128)(2,1)S(1)}, bf16[384,384]{1,0:T(8,128)(2,1)}, u32[]{:S(2)}) copy-start(bf16[384,384]{1,0:T(8,128)(2,1)} %wv.3) | copy-start | bytes 884740
  19.5 32.0 %copy-start.6 = (bf16[384,384]{1,0:T(8,128)(2,1)S(1)}, bf16[384,384]{1,0:T(8,128)(2,1)}, u32[]{:S(2)}) copy-start(bf16[384,384]{1,0:T(8,128)(2,1)} %wo.3) | copy-start | bytes 884740
  21.7 13.0 %collective-permute-start.2 = (bf16[2,128,384]{2,1,0:T(8,128)(2,1)S(1)}, bf16[2,128,384]{2,1,0:T(8,128)(2,1)S(1)}, u32[]{:S(2)}, u32[]{:S(2)}) collective-permute-start(bf16[2,128,384]{2,1,0:T(8,128)(2,1)S(1)} %shard_map.97), channel_id=1, source_target_pairs={{0,8},{8,16},{16,24},{24,32},{32,40},{40,48},{48,56},{56,64},{64,7... | collective-permute-start | bytes 589832 | tf_op jit(solution)/shard_map/ppermute | solution.py:391
  25.7 10.3 %collective-permute-start.14 = (bf16[2,128,384]{2,1,0:T(8,128)(2,1)S(1)}, bf16[2,128,384]{2,1,0:T(8,128)(2,1)S(1)}, u32[]{:S(2)}, u32[]{:S(2)}) collective-permute-start(bf16[2,128,384]{2,1,0:T(8,128)(2,1)S(1)} %collective-permute-done.13.first), channel_id=1, source_target_pairs={{0,4},{1,5},{2,6},{3,7},{4,0},{5,1},{6,2},{7,3},{8,12},{9,13},{10,... | collective-permute-start | bytes 589832 | tf_op jit(solution)/shard_map/ppermute | solution.py:346
  28.8 42.1 %slice-start = ((s8[7962624]{0:T(1024)(128)(4,1)}), s8[4194304]{0:T(1024)(128)(4,1)S(1)}, s32[]{:S(2)}) async-start(s8[7962624]{0:T(1024)(128)(4,1)} %bitcast.9), calls=%async_computation | async-start | bytes 8388608
  35.4 8.0 %collective-permute-start.3 = (bf16[128,384]{1,0:T(8,128)(2,1)S(1)}, bf16[128,384]{1,0:T(8,128)(2,1)S(1)}, u32[]{:S(2)}, u32[]{:S(2)}) collective-permute-start(bf16[128,384]{1,0:T(8,128)(2,1)S(1)} %get-tuple-element.15), channel_id=1, source_target_pairs={{0,0},{1,1},{2,8},{3,9},{4,4},{5,5},{6,12},{7,13},{8,2},{9,3},{10,... | collective-permute-start | bytes 294920 | tf_op jit(solution)/shard_map/ppermute | solution.py:346
  36.6 14.1 %collective-permute-start.15 = (bf16[256,384]{1,0:T(8,128)(2,1)S(1)}, bf16[256,384]{1,0:T(8,128)(2,1)S(1)}, u32[]{:S(2)}, u32[]{:S(2)}) collective-permute-start(bf16[256,384]{1,0:T(8,128)(2,1)S(1)} %get-tuple-element.25), channel_id=1, source_target_pairs={{0,1},{1,0},{2,3},{3,2},{4,5},{5,4},{6,7},{7,6},{8,9},{9,8},{10,11... | collective-permute-start | bytes 589832 | tf_op jit(solution)/shard_map/ppermute | solution.py:346
  36.7 11.2 %collective-permute-start.4 = (bf16[128,384]{1,0:T(8,128)(2,1)S(1)}, bf16[128,384]{1,0:T(8,128)(2,1)S(1)}, u32[]{:S(2)}, u32[]{:S(2)}) collective-permute-start(bf16[128,384]{1,0:T(8,128)(2,1)S(1)} %get-tuple-element.16), channel_id=1, source_target_pairs={{0,1},{1,0},{2,9},{3,8},{4,5},{5,4},{6,13},{7,12},{8,3},{9,2},{10,... | collective-permute-start | bytes 294920 | tf_op jit(solution)/shard_map/ppermute | solution.py:346
  40.2 7.7 %collective-permute-start.5 = (bf16[128,384]{1,0:T(8,128)(2,1)S(1)}, bf16[128,384]{1,0:T(8,128)(2,1)S(1)}, u32[]{:S(2)}, u32[]{:S(2)}) collective-permute-start(bf16[128,384]{1,0:T(8,128)(2,1)S(1)} %get-tuple-element.15), channel_id=1, source_target_pairs={{0,4},{1,5},{2,12},{3,13},{4,0},{5,1},{6,8},{7,9},{8,6},{9,7},{10,... | collective-permute-start | bytes 294920 | tf_op jit(solution)/shard_map/ppermute | solution.py:346
  40.7 9.4 %collective-permute-start.6 = (bf16[128,384]{1,0:T(8,128)(2,1)S(1)}, bf16[128,384]{1,0:T(8,128)(2,1)S(1)}, u32[]{:S(2)}, u32[]{:S(2)}) collective-permute-start(bf16[128,384]{1,0:T(8,128)(2,1)S(1)} %get-tuple-element.16), channel_id=1, source_target_pairs={{0,5},{1,4},{2,13},{3,12},{4,1},{5,0},{6,9},{7,8},{8,7},{9,6},{10,... | collective-permute-start | bytes 294920 | tf_op jit(solution)/shard_map/ppermute | solution.py:346
  43.3 6.9 %collective-permute-start.7 = (bf16[128,384]{1,0:T(8,128)(2,1)S(1)}, bf16[128,384]{1,0:T(8,128)(2,1)S(1)}, u32[]{:S(2)}, u32[]{:S(2)}) collective-permute-start(bf16[128,384]{1,0:T(8,128)(2,1)S(1)} %collective-permute-done.3.c00), channel_id=1, source_target_pairs={{0,8},{1,9},{2,10},{3,11},{4,12},{5,13},{6,14},{7,15},{8,0},{9,1},... | collective-permute-start | bytes 294920 | tf_op jit(solution)/shard_map/ppermute | solution.py:346
  47.9 3.0 %collective-permute-start.8 = (bf16[128,384]{1,0:T(8,128)(2,1)S(1)}, bf16[128,384]{1,0:T(8,128)(2,1)S(1)}, u32[]{:S(2)}, u32[]{:S(2)}) collective-permute-start(bf16[128,384]{1,0:T(8,128)(2,1)S(1)} %collective-permute-done.4.c01), channel_id=1, source_target_pairs={{0,8},{1,9},{2,10},{3,11},{4,12},{5,13},{6,14},{7,15},{8,0},{9,1},... | collective-permute-start | bytes 294920 | tf_op jit(solution)/shard_map/ppermute | solution.py:346
  48.0 3.0 %collective-permute-start.9 = (bf16[128,384]{1,0:T(8,128)(2,1)S(1)}, bf16[128,384]{1,0:T(8,128)(2,1)S(1)}, u32[]{:S(2)}, u32[]{:S(2)}) collective-permute-start(bf16[128,384]{1,0:T(8,128)(2,1)S(1)} %collective-permute-done.5.c10), channel_id=1, source_target_pairs={{0,8},{1,9},{2,10},{3,11},{4,12},{5,13},{6,14},{7,15},{8,0},{9,1},... | collective-permute-start | bytes 294920 | tf_op jit(solution)/shard_map/ppermute | solution.py:346
  50.2 1.3 %collective-permute-start.10 = (bf16[128,384]{1,0:T(8,128)(2,1)S(1)}, bf16[128,384]{1,0:T(8,128)(2,1)S(1)}, u32[]{:S(2)}, u32[]{:S(2)}) collective-permute-start(bf16[128,384]{1,0:T(8,128)(2,1)S(1)} %collective-permute-done.6.c11), channel_id=1, source_target_pairs={{0,8},{1,9},{2,10},{3,11},{4,12},{5,13},{6,14},{7,15},{8,0},{9,1},... | collective-permute-start | bytes 294920 | tf_op jit(solution)/shard_map/ppermute | solution.py:346
  50.2 6.4 %collective-permute-start.16 = (bf16[256,384]{1,0:T(8,128)(2,1)S(1)}, bf16[256,384]{1,0:T(8,128)(2,1)S(1)}, u32[]{:S(2)}, u32[]{:S(2)}) collective-permute-start(bf16[256,384]{1,0:T(8,128)(2,1)S(1)} %get-tuple-element.24.same), channel_id=1, source_target_pairs={{0,8},{1,9},{2,10},{3,11},{4,12},{5,13},{6,14},{7,15},{8,0},{9,1},... | collective-permute-start | bytes 589832 | tf_op jit(solution)/shard_map/ppermute | solution.py:346
  50.7 5.9 %collective-permute-start.17 = (bf16[256,384]{1,0:T(8,128)(2,1)S(1)}, bf16[256,384]{1,0:T(8,128)(2,1)S(1)}, u32[]{:S(2)}, u32[]{:S(2)}) collective-permute-start(bf16[256,384]{1,0:T(8,128)(2,1)S(1)} %collective-permute-done.15.other), channel_id=1, source_target_pairs={{0,8},{1,9},{2,10},{3,11},{4,12},{5,13},{6,14},{7,15},{8,0},{9,1},... | collective-permute-start | bytes 589832 | tf_op jit(solution)/shard_map/ppermute | solution.py:346
  51.0 20.0 %slice-start.1 = ((s8[7962624]{0:T(1024)(128)(4,1)}), s8[3768320]{0:T(1024)(128)(4,1)S(1)}, s32[]{:S(2)}) async-start(s8[7962624]{0:T(1024)(128)(4,1)} %bitcast.9), calls=%async_computation.1 | async-start | bytes 7536640
  62.8 2.6 %collective-permute-start.18 = (bf16[256,384]{1,0:T(8,128)(2,1)S(1)}, bf16[256,384]{1,0:T(8,128)(2,1)S(1)}, u32[]{:S(2)}, u32[]{:S(2)}) collective-permute-start(bf16[256,384]{1,0:T(8,128)(2,1)S(1)} %get-tuple-element.26), channel_id=1, source_target_pairs={{0,0},{1,1},{2,8},{3,9},{4,4},{5,5},{6,12},{7,13},{8,2},{9,3},{10,... | collective-permute-start | bytes 589832 | tf_op jit(solution)/shard_map/ppermute | solution.py:346
  63.4 7.5 %collective-permute-start.19 = (bf16[256,384]{1,0:T(8,128)(2,1)S(1)}, bf16[256,384]{1,0:T(8,128)(2,1)S(1)}, u32[]{:S(2)}, u32[]{:S(2)}) collective-permute-start(bf16[256,384]{1,0:T(8,128)(2,1)S(1)} %get-tuple-element.27), channel_id=1, source_target_pairs={{0,1},{1,0},{2,9},{3,8},{4,5},{5,4},{6,13},{7,12},{8,3},{9,2},{10,... | collective-permute-start | bytes 589832 | tf_op jit(solution)/shard_map/ppermute | solution.py:346
  73.5 17.7 %collective-permute-start.20 = (bf16[2,128,384]{2,1,0:T(8,128)(2,1)S(1)}, bf16[2,128,384]{2,1,0:T(8,128)(2,1)S(1)}, u32[]{:S(2)}, u32[]{:S(2)}) collective-permute-start(bf16[2,128,384]{2,1,0:T(8,128)(2,1)S(1)} %shard_map.104), channel_id=1, source_target_pairs={{8,0},{16,8},{24,16},{32,24},{40,32},{48,40},{56,48},{64,56},{72,6... | collective-permute-start | bytes 589832 | tf_op jit(solution)/shard_map/ppermute | solution.py:418
  80.5 2.6 %collective-permute-start.11 = (bf16[128,384]{1,0:T(8,128)(2,1)S(1)}, bf16[128,384]{1,0:T(8,128)(2,1)S(1)}, u32[]{:S(2)}, u32[]{:S(2)}) collective-permute-start(bf16[128,384]{1,0:T(8,128)(2,1)S(1)} %get-tuple-element.17), channel_id=1, source_target_pairs={{0,0},{1,1},{2,8},{3,9},{4,4},{5,5},{6,12},{7,13},{8,2},{9,3},{10,... | collective-permute-start | bytes 294920 | tf_op jit(solution)/shard_map/ppermute | solution.py:346
  81.2 6.2 %collective-permute-start.12 = (bf16[128,384]{1,0:T(8,128)(2,1)S(1)}, bf16[128,384]{1,0:T(8,128)(2,1)S(1)}, u32[]{:S(2)}, u32[]{:S(2)}) collective-permute-start(bf16[128,384]{1,0:T(8,128)(2,1)S(1)} %get-tuple-element.18), channel_id=1, source_target_pairs={{0,1},{1,0},{2,9},{3,8},{4,5},{5,4},{6,13},{7,12},{8,3},{9,2},{10,... | collective-permute-start | bytes 294920 | tf_op jit(solution)/shard_map/ppermute | solution.py:346

commit v2 on v0

--- a/solution.py
+++ b/solution.py
@@ -12,17 +12,16 @@
 BF16 = jnp.bfloat16
 MIB = 1024 * 1024
 LOAD = 42 * MIB
-PREPARE = 533 * MIB // 10
 VM = pl.BlockSpec(memory_space=pltpu.VMEM)
 SM = pl.BlockSpec(memory_space=pltpu.SMEM)
 HBM = pl.BlockSpec(memory_space=pltpu.HBM)
 
 
-def call(kernel, operands, specs, shapes, scratch, limit, cost=0):
+def call(kernel, operands, specs, shapes, scratch, limit, cost=0, outs=VM):
     return pl.pallas_call(
         kernel,
         in_specs=specs,
-        out_specs=[VM] * len(shapes),
+        out_specs=[outs] * len(shapes),
         out_shape=[jax.ShapeDtypeStruct(dims, dtype) for dims, dtype in shapes],
         scratch_shapes=scratch,
         compiler_params=pltpu.CompilerParams(vmem_limit_bytes=limit),
@@ -30,51 +29,36 @@
     )(*operands)
 
 
-def prepare_kernel(place, video, cot, packet, far, same, held, sems):
+def pick_kernel(place, both, same, other):
     x = place[0]
-    width = far.shape[0] // 2
-    moves = [
-        (cot.at[1 - x], packet.at[2 * width :]),
-        (cot.at[x], same),
-        (video, held),
-    ]
-    for f in range(2):
-        moves.append((video.at[f, 1 - x], packet.at[f * width : (f + 1) * width]))
-        moves.append((video.at[f, x], far.at[f * width : (f + 1) * width]))
-    copies = [pltpu.make_async_copy(a, b, sems.at[i]) for i, (a, b) in enumerate(moves)]
-    for copy in copies:
-        copy.start()
-    for copy in copies:
-        copy.wait()
-
-
-def prepare(place, video, cot):
-    _, _, width, chans = video.shape
+    same[...] = both[x]
+    other[...] = both[1 - x]
+
+
+def pick(place, both):
     return call(
-        prepare_kernel, (place, video, cot), [SM, HBM, HBM],
-        [((4 * width, chans), BF16), ((2 * width, chans), BF16), (cot.shape[1:], BF16), (video.shape, BF16)],
-        [pltpu.SemaphoreType.DMA((7,))], PREPARE,
+        pick_kernel, (place, both), [SM, VM], [(both.shape[1:], both.dtype)] * 2, [], 4 * MIB
     )
 
 
-def join_kernel(same, packet, out):
+def join_kernel(place, same, other, out):
+    x = place[0]
     half = same.shape[0]
-    out[:half] = same[...]
-    out[half:] = packet[half:]
-
-
-def join(same, packet):
-    return call(join_kernel, (same, packet), [VM, VM], [(packet.shape, BF16)], [], 4 * MIB)[0]
-
-
-def merge_kernel(place, own, cached, same, other):
-    x = place[0]
-    same[...] = (own[x] + cached[x].astype(F32)).astype(BF16)
-    other[...] = (own[1 - x] + cached[1 - x].astype(F32)).astype(BF16)
-
-
-def merge(place, own, cached):
-    return call(merge_kernel, (place, own, cached), [SM, VM, VM], [(own.shape[1:], BF16)] * 2, [], 8 * MIB)
+    out[pl.ds(pl.multiple_of(x * half, half), half)] = same[...]
+    out[pl.ds(pl.multiple_of((1 - x) * half, half), half)] = other[...]
+
+
+def join(place, same, other):
+    shape = (2 * same.shape[0], same.shape[1])
+    return call(join_kernel, (place, same, other), [SM, VM, VM], [(shape, BF16)], [], 4 * MIB)[0]
+
+
+def merge_kernel(own, cached, out):
+    out[...] = (own[...] + cached[...].astype(F32)).astype(BF16)
+
+
+def merge(own, cached):
+    return call(merge_kernel, (own, cached), [VM, VM], [(own.shape, BF16)], [], 8 * MIB)[0]
 
 
 def load_kernel(w_hbm, w_out, sem):
@@ -84,10 +68,12 @@
 
 
 def load(weight):
-    return call(load_kernel, (weight,), [HBM], [(weight.shape, BF16)], [pltpu.SemaphoreType.DMA], LOAD)[0]
-
-
-def finish_kernel(place, out0, out1, own, handed, block_out, video_grad, total, sems):
+    return call(
+        load_kernel, (weight,), [HBM], [(weight.shape, BF16)], [pltpu.SemaphoreType.DMA], LOAD
+    )[0]
+
+
+def deliver_kernel(place, out0, out1, block_out, sems):
     x = place[0]
     copies = [
         pltpu.make_async_copy(out0, block_out.at[x], sems.at[0]),
@@ -95,26 +81,32 @@
     ]
     for copy in copies:
         copy.start()
-    total[...] = (own[...] + handed[...].astype(F32)).astype(BF16)
-    copies.append(pltpu.make_async_copy(total, video_grad, sems.at[2]))
-    copies[2].start()
     for copy in copies:
         copy.wait()
 
 
-def finish(place, out0, out1, own, handed):
-    return pl.pallas_call(
-        finish_kernel,
-        in_specs=[SM] + [VM] * 4,
-        out_specs=[HBM, HBM],
-        out_shape=[
-            jax.ShapeDtypeStruct((2,) + out0.shape, BF16),
-            jax.ShapeDtypeStruct(own.shape, BF16),
-        ],
-        scratch_shapes=[pltpu.VMEM(own.shape, BF16), pltpu.SemaphoreType.DMA((3,))],
-        compiler_params=pltpu.CompilerParams(vmem_limit_bytes=8 * MIB),
-        name="finish",
-    )(place, out0, out1, own, handed)
+def deliver(place, out0, out1):
+    return call(
+        deliver_kernel, (place, out0, out1), [SM, VM, VM], [((2,) + out0.shape, BF16)],
+        [pltpu.SemaphoreType.DMA((2,))], 8 * MIB, outs=HBM,
+    )[0]
+
+
+def finish_kernel(own, handed, video_grad, total, sems):
+    copies = []
+    for f in range(2):
+        total[f] = (own[f] + handed[f].astype(F32)).astype(BF16)
+        copies.append(pltpu.make_async_copy(total.at[f], video_grad.at[f], sems.at[f]))
+        copies[f].start()
+    for copy in copies:
+        copy.wait()
+
+
+def finish(own, handed):
+    return call(
+        finish_kernel, (own, handed), [VM, VM], [(own.shape, BF16)],
+        [pltpu.VMEM(own.shape, BF16), pltpu.SemaphoreType.DMA((2,))], 8 * MIB, outs=HBM,
+    )[0]
 
 
 def spread(rows_f32, width):
@@ -131,7 +123,7 @@
     if flip:
         shifted = shifted[::-1]
     for c in range(3):
-        taps[frame, pl.ds(row, n), :, c * chans : (c + 1) * chans] = (
+        taps[frame, row : row + n, :, c * chans : (c + 1) * chans] = (
             shifted[c].astype(BF16).reshape(n, width, chans)
         )
 
@@ -159,22 +151,59 @@
         out[f] = (term + extra if f == dst else term).astype(out.dtype)
 
 
-def forward_kernel(main, side, src, dst, place, packet, mid, far, w_ref, out, taps):
-    width, chans = mid.shape[2:]
+def frame_taps(taps, frame, rows):
+    piece = taps[frame, rows : rows + 4]
+    return piece.reshape(piece.shape[0] * piece.shape[1], piece.shape[2])
+
+
+def frame_conv(taps, w_ref, frame, a):
+    chans = w_ref.shape[-1]
+    total = None
+    for b in range(3):
+        term = mm(frame_taps(taps, frame, b), w_ref[a, b].reshape(3 * chans, chans))
+        total = term if total is None else total + term
+    return total
+
+
+def next_kernel(place, mine, packet, far_same, far_other, w_ref, out, taps, acc):
     x = place[0]
+    flip = x == 1
+    width = taps.shape[2]
+    chans = w_ref.shape[-1]
     for f in range(2):
         line = slice(f * width, (f + 1) * width)
-        fill(taps, f, 3 * (1 - x), packet[line].reshape(1, width, chans), width, False)
-        fill(taps, f, 1, mid[f], width, False)
-        fill(taps, f, 3 * x, far[line].reshape(1, width, chans), width, False)
-    conv_steps(taps, w_ref, main, side, out, src, dst, False)
+        pair = slice(2 * f * width, 2 * (f + 1) * width)
+        a, b = mine[pair], packet[pair]
+        top = jnp.where(flip, far_same[line], far_other[line])
+        bottom = jnp.where(flip, far_other[line], far_same[line])
+        for row, rows in (
+            (0, top), (1, jnp.where(flip, b, a)), (3, jnp.where(flip, a, b)), (5, bottom)
+        ):
+            fill(taps, f, row, rows.reshape(-1, width, chans), width, False)
+    acc[...] = frame_conv(taps, w_ref, x, 0)
+
+    @pl.when(x == 0)
+    def _():
+        acc[...] += frame_conv(taps, w_ref, 1, 1)
+
+    out[...] = acc[...].astype(out.dtype)
+
+
+def own_kernel(place, taps, w_ref, out):
+    x = place[0]
+    out[...] = frame_conv(taps, w_ref, x, 2)
+
+    @pl.when(x == 1)
+    def _():
+        out[...] += frame_conv(taps, w_ref, 0, 1)
 
 
 def backward_kernel(main, side, src, dst, place, r0, r1, w_ref, out, taps):
     width, chans = taps.shape[2], w_ref.shape[-1]
-    x = place[0]
-    fill(taps, x, 0, r0[...].reshape(4, width, chans), width, True)
-    fill(taps, 1 - x, 0, r1[...].reshape(4, width, chans), width, True)
+    swapped = place[0] == 1
+    for f, (a, b) in enumerate(((r0, r1), (r1, r0))):
+        rows = jnp.where(swapped, b[...], a[...])
+        fill(taps, f, 0, rows.reshape(4, width, chans), width, True)
     conv_steps(taps, w_ref, main, side, out, src, dst, True)
 
 
@@ -210,32 +239,22 @@
 
 
 def attention_kernel(
-    place, c00, c01, c10, c11, s00, s01, s10, s11, t0, t2, u0, u2, gain_ref, wq, wk, wv, wo,
+    place, c0, c2, c1, c3, t0, t2, t1, t3, gain_ref, wq, wk, wv, wo,
     out0, out1, grad0, grad1, conv_s, cot_s, act_s, q_s, k_s, v_s, g_s, gk_s, gv_s, out_s, grad_s,
 ):
     x, q = place[0], place[1]
-    line = c00.shape[0] // 2
+    line = c0.shape[0] // 4
     own = 6 * line
     chans = wq.shape[0]
     scale = 1.0 / jnp.sqrt(jnp.float32(chans))
     gain = gain_ref[...]
-
-    def put(dst, value, quarter, kx):
-        for j in range(2):
-            slot = (4 * (quarter - q) + 2 * (x + kx - 2 * x * kx) + j + 17) % 16
-            dst[pl.ds(pl.multiple_of(slot * line, line), line)] = value[j * line : (j + 1) * line]
-
     side = q + 1 - 2 * (q % 2)
-    far = (q + 2) % 4
-    far_side = (side + 2) % 4
-    for ref, quarter, kx in (
-        (c00, q, 0), (c01, q, 1), (c10, far, 0), (c11, far, 1),
-        (s00, side, 0), (s01, side, 1), (s10, far_side, 0), (s11, far_side, 1),
-    ):
-        put(conv_s, ref, quarter, kx)
-    for ref, quarter in ((t0, q), (t2, far), (u0, side), (u2, far_side)):
-        for kx in range(2):
-            put(cot_s, ref.at[2 * kx * line : 2 * (kx + 1) * line], quarter, kx)
+    quarters = (q, (q + 2) % 4, side, (side + 2) % 4)
+    for dst, refs in ((conv_s, (c0, c2, c1, c3)), (cot_s, (t0, t2, t1, t3))):
+        for ref, quarter in zip(refs, quarters):
+            for j in range(4):
+                slot = (4 * (quarter - q) + j + 17) % 16
+                dst[pl.ds(pl.multiple_of(slot * line, line), line)] = ref[j * line : (j + 1) * line]
 
     for at, n in CHUNKS:
         rows = slice(at, at + n)
@@ -294,7 +313,7 @@
 
 
 def attention(place, convs, cots, gain, wq, wk, wv, wo):
-    block, chans = convs[0].shape
+    block, chans = convs[0].shape[0] // 2, convs[0].shape[1]
     own, whole = 3 * block, 8 * block
     act = lambda n, t=BF16: pltpu.VMEM((n, chans), t)
     return pl.pallas_call(
@@ -346,6 +365,11 @@
     return (c, y, x ^ 1) if 0 <= y < 4 else None
 
 
+def straight(c, y, x):
+    y = y + 1 if x else y - 1
+    return (c, y, x) if 0 <= y < 4 else None
+
+
 def local(video, conv_weight, norm_gain, w_query, w_key, w_value, w_out, cotangent):
     frames, height, width, chans = video.shape
     runs, slabs = lax.axis_size("tm"), lax.axis_size("rows")
@@ -356,48 +380,51 @@
     place = jnp.stack([x, quarter]).astype(jnp.int32)
     block = 2 * width
 
-    packet, far, cot_same, held = prepare(place, video, cotangent.reshape(2, block, chans))
-    far = send(far, runs, beyond)
-    packet = send(packet, runs, across)
+    edge = lax.dynamic_index_in_dim(video, x, 1, keepdims=False).reshape(block, chans)
+    mine = video.reshape(2 * block, chans)
+    far_other = send(edge, runs, beyond)
+    packet = send(mine, runs, across)
+    far_same = send(edge, runs, straight)
+    cot_b = send(cotangent.reshape(2, block, chans), runs, home(0, 0))
     weight = load(conv_weight)
-    cot_own = join(cot_same, packet)
-    cot_b = send(cot_own, runs, home(0, 0))
-    slab = (packet, held, far)
-
-    def forward(main, side, src, dst, dtype):
-        kernel = functools.partial(forward_kernel, main, side, src, dst)
-        return conv_call(kernel, place, slab, weight, width, dtype)
-
-    def backward(main, side, src, dst, dtype):
-        kernel = functools.partial(backward_kernel, main, side, src, dst)
-        return conv_call(kernel, place, slab, weight, width, dtype)
-
-    for_next = forward(0, 1, 1, 0, BF16)
+    cot_same, cot_other = pick(place, cot_b)
+    quad = (2 * block, chans)
+    for_next, taps = call(
+        next_kernel, (place, mine, packet, far_same, far_other, weight), [SM] + [VM] * 5,
+        [(quad, BF16), ((2, 6, width, 3 * chans), BF16)], [pltpu.VMEM(quad, F32)],
+        24 * MIB, 10**9,
+    )
     cached = lax.ppermute(for_next, "tm", [(i, i + 1) for i in range(runs - 1)])
-    own = forward(2, 1, 0, 1, F32)
+    cot_other = send(cot_other, runs, across)
+    own = call(
+        own_kernel, (place, taps, weight), [SM, VM, VM], [(quad, F32)], [],
+        24 * MIB, 10**9,
+    )[0]
+    cot_b = join(place, cot_same, cot_other)
     cot_c = send(cot_b, runs, lambda c, y, x: (c, y ^ 2, x))
-    same, other = merge(place, own, cached)
-    got, swapped = {}, {}
-    for ky, kx in ((1, 1), (0, 1), (1, 0), (0, 0)):
-        got[ky, kx] = send(other if kx else same, runs, home(ky, kx))
-    cots = [cot_b, cot_c, send(cot_b, runs, swap), send(cot_c, runs, swap)]
-    for ky, kx in ((1, 1), (0, 1), (1, 0), (0, 0)):
-        swapped[ky, kx] = send(got[ky, kx], runs, swap)
-    order = ((0, 0), (0, 1), (1, 0), (1, 1))
-    convs = [got[k] for k in order] + [swapped[k] for k in order]
-
+    conv = merge(own, cached)
+    conv_c = send(conv, runs, home(1, 0))
+    conv_b = send(conv, runs, home(0, 0))
+    cots = (cot_b, cot_c, send(cot_b, runs, swap), send(cot_c, runs, swap))
+    convs = (conv_b, conv_c, send(conv_b, runs, swap), send(conv_c, runs, swap))
     out0, out1, grad0, grad1 = attention(
         place, convs, cots, norm_gain.reshape(1, chans), w_query, w_key, w_value, w_out
     )
     grad1 = send(grad1, runs, home(0, 1))
     grad0 = send(grad0, runs, home(0, 0))
+    out1 = send(out1, runs, home(0, 1))
     out0 = send(out0, runs, home(0, 0))
-    out1 = send(out1, runs, home(0, 1))
+
+    def backward(main, side, src, dst, dtype):
+        kernel = functools.partial(backward_kernel, main, side, src, dst)
+        return conv_call(kernel, place, slab, weight, width, dtype)
+
     slab = (grad0, grad1)
     for_last = backward(0, 1, 0, 1, BF16)
     handed = lax.ppermute(for_last, "tm", [(i + 1, i) for i in range(runs - 1)])
     own_grad = backward(2, 1, 1, 0, F32)
-    block_out, video_grad = finish(place, out0, out1, own_grad, handed)
+    block_out = deliver(place, out0, out1)
+    video_grad = finish(own_grad, handed)
     return block_out.reshape(video.shape), video_grad.reshape(video.shape)
 
 

time: 84.5 us -> 86.1 us (1.019)
  the two profiles are of different devices: /device:TPU:6 before, /device:TPU:1 now
where the time goes in v2:
time: 86.1 us; the launch traced here: 85.8 us
  starting transfers between devices  36.3 us (42%)
  Pallas kernels  25.6 us (30%)
  waiting for transfers between devices  21.8 us (25%)
  between operations  1.09 us (1%)
  local copies, waits for them, and re-layouts  0.97 us (1%)
    ppermute x16, starting transfers between devices, send(): return lax.ppermute(value, ('tm', 'rows'), pairs)  32.4 us
    ppermute x16, waiting for transfers between devices, send(): return lax.ppermute(value, ('tm', 'rows'), pairs)  21.8 us
    pallas_call x10, Pallas kernels, call(): pl.pallas_call(kernel, in_specs=specs, out_specs=[outs] * len(shapes), ou...  16.2 us
    pallas_call x1, Pallas kernels, attention(): pl.pallas_call(attention_kernel, in_specs=[SM] + [VM] * (len(convs) + len...  9.34 us
    ppermute x1, starting transfers between devices, local(): cached = lax.ppermute(for_next, 'tm', [(i, i + 1) for i in range(runs - 1)])  1.92 us
    ppermute x1, starting transfers between devices, local(): handed = lax.ppermute(for_last, 'tm', [(i + 1, i) for i in range(runs - 1)])  1.92 us
  transfers between devices with their start and end apart: 18, of which 9 were waited for; matrix products, arithmetic and copies ran while one was open for 1% of the time, Pallas kernels for 15%

profile of v2, /device:TPU:1, one launch (start us, length us, event | category | flops | bytes accessed | tf_op | source)
XLA Modules:
  0.0 85.8 jit_solution(11383252590864288726)
XLA Ops:
  0.6 3.6 %collective-permute-start = (bf16[256,384]{1,0:T(8,128)(2,1)}, bf16[256,384]{1,0:T(8,128)(2,1)S(1)}, u32[]{:S(2)}, u32[]{:S(2)}) collective-permute-start(bf16[256,384]{1,0:T(8,128)(2,1)} %bitcast.7), channel_id=1, source_target_pairs={{0,1},{1,0},{2,3},{3,2},{4,5},{5,4},{6,7},{7,6},{8,9},{9,8},{10,11... | collective-permute-start | bytes 589832 | tf_op jit(solution)/shard_map/ppermute | solution.py:348
  4.3 0.9 %constant_dynamic-slice_fusion = bf16[2,1,64,384]{3,2,1,0:T(8,128)(2,1)S(1)} fusion(bf16[2,2,64,384]{3,2,1,0:T(8,128)(2,1)} %param.8, s32[]{:T(128)S(6)} %select_n.22), kind=kLoop, calls=%fused_computation.1 | loop fusion | bytes 196612 | tf_op jit(solution)/shard_map/jit(dynamic_index_in_dim)/dynamic_slice | solution.py:383
  5.2 1.3 %collective-permute-start.1 = (bf16[128,384]{1,0:T(8,128)(2,1)S(1)}, bf16[128,384]{1,0:T(8,128)(2,1)S(1)}, u32[]{:S(2)}, u32[]{:S(2)}) collective-permute-start(bf16[128,384]{1,0:T(8,128)(2,1)S(1)} %bitcast.11), channel_id=1, source_target_pairs={{1,3},{2,0},{3,5},{4,2},{5,7},{6,4},{9,11},{10,8},{11,13},{12,10},... | collective-permute-start | bytes 294920 | tf_op jit(solution)/shard_map/ppermute | solution.py:348
  6.5 0.7 collective-permute-start.2
  7.2 7.9 %collective-permute-start.8 = (bf16[2,128,384]{2,1,0:T(8,128)(2,1)}, bf16[2,128,384]{2,1,0:T(8,128)(2,1)S(1)}, u32[]{:S(2)}, u32[]{:S(2)}) collective-permute-start(bf16[2,128,384]{2,1,0:T(8,128)(2,1)} %bitcast.13), channel_id=1, source_target_pairs={{0,0},{1,1},{2,8},{3,9},{4,4},{5,5},{6,12},{7,13},{8,2},{9,3},{10,... | collective-permute-start | bytes 589832 | tf_op jit(solution)/shard_map/ppermute | solution.py:348
  15.2 3.3 %shard_map.95.w_ref = bf16[3,3,3,384,384]{4,3,2,1,0:T(8,128)(2,1)S(1)} custom-call(bf16[3,3,3,384,384]{4,3,2,1,0:T(8,128)(2,1)} %w_hbm.1), custom_call_target="tpu_custom_call" | custom-call | bytes 1048576 | tf_op jit(solution)/shard_map/pallas_call | solution.py:21
  18.6 3.2 %shard_map.96 = (bf16[256,384]{1,0:T(8,128)(2,1)S(1)}, bf16[2,6,64,1152]{3,2,1,0:T(8,128)(2,1)S(1)}) custom-call(s32[2]{0:T(128)S(1)} %pad_add_fusion.place, bf16[256,384]{1,0:T(8,128)(2,1)S(1)} %bitcast.8, bf16[256,384]{1,0:T(8,128)(2,1)S(1)} %collective-permute-done.packet, bf16[128,384]{1,0:T(8,128)(2,1)S(1)} %collective-permute-done.1.far_same, ...), custom_call_target="tpu_custom_call" | custom-call | flops 1000000000 | bytes 1048576 | tf_op jit(solution)/shard_map/pallas_call | solution.py:21
  21.8 1.9 %collective-permute-start.3 = (bf16[256,384]{1,0:T(8,128)(2,1)S(1)}, bf16[256,384]{1,0:T(8,128)(2,1)S(1)}, u32[]{:S(2)}, u32[]{:S(2)}) collective-permute-start(bf16[256,384]{1,0:T(8,128)(2,1)S(1)} %get-tuple-element.11), channel_id=1, source_target_pairs={{0,8},{8,16},{16,24},{24,32},{32,40},{40,48},{48,56},{56,64},{64,7... | collective-permute-start | bytes 589832 | tf_op jit(solution)/shard_map/ppermute | solution.py:397
  24.3 1.7 %collective-permute-start.9 = (bf16[128,384]{1,0:T(8,128)(2,1)S(1)}, bf16[128,384]{1,0:T(8,128)(2,1)S(1)}, u32[]{:S(2)}, u32[]{:S(2)}) collective-permute-start(bf16[128,384]{1,0:T(8,128)(2,1)S(1)} %get-tuple-element.13), channel_id=1, source_target_pairs={{0,1},{1,0},{2,3},{3,2},{4,5},{5,4},{6,7},{7,6},{8,9},{9,8},{10,11... | collective-permute-start | bytes 294920 | tf_op jit(solution)/shard_map/ppermute | solution.py:348
  26.0 1.7 %shard_map.97.own = f32[256,384]{1,0:T(8,128)S(1)} custom-call(s32[2]{0:T(128)S(1)} %pad_add_fusion.place, bf16[2,6,64,1152]{3,2,1,0:T(8,128)(2,1)S(1)} %get-tuple-element.10.taps, bf16[3,3,3,384,384]{4,3,2,1,0:T(8,128)(2,1)S(1)} %shard_map.95.w_ref), custom_call_target="tpu_custom_call" | custom-call | flops 1000000000 | bytes 1048576 | tf_op jit(solution)/shard_map/pallas_call | solution.py:21
  27.7 2.1 %collective-permute-done.9.other = bf16[128,384]{1,0:T(8,128)(2,1)S(1)} collective-permute-done((bf16[128,384]{1,0:T(8,128)(2,1)S(1)}, bf16[128,384]{1,0:T(8,128)(2,1)S(1)}, u32[]{:S(2)}, u32[]{:S(2)}) %collective-permute-start.9) | collective-permute-done | bytes 98336 | tf_op jit(solution)/shard_map/ppermute | solution.py:348
  30.4 6.2 %collective-permute-start.10 = (bf16[256,384]{1,0:T(8,128)(2,1)S(1)}, bf16[256,384]{1,0:T(8,128)(2,1)S(1)}, u32[]{:S(2)}, u32[]{:S(2)}) collective-permute-start(bf16[256,384]{1,0:T(8,128)(2,1)S(1)} %shard_map.100.t0), channel_id=1, source_target_pairs={{0,4},{1,5},{2,6},{3,7},{4,0},{5,1},{6,2},{7,3},{8,12},{9,13},{10,... | collective-permute-start | bytes 589832 | tf_op jit(solution)/shard_map/ppermute | solution.py:348
  36.6 1.9 %collective-permute-start.4 = (bf16[256,384]{1,0:T(8,128)(2,1)S(1)}, bf16[256,384]{1,0:T(8,128)(2,1)S(1)}, u32[]{:S(2)}, u32[]{:S(2)}) collective-permute-start(bf16[256,384]{1,0:T(8,128)(2,1)S(1)} %shard_map.98), channel_id=1, source_target_pairs={{0,0},{1,1},{2,8},{3,9},{4,4},{5,5},{6,12},{7,13},{8,2},{9,3},{10,... | collective-permute-start | bytes 589832 | tf_op jit(solution)/shard_map/ppermute | solution.py:348
  39.2 1.9 %collective-permute-done.10.t2 = bf16[256,384]{1,0:T(8,128)(2,1)S(1)} collective-permute-done((bf16[256,384]{1,0:T(8,128)(2,1)S(1)}, bf16[256,384]{1,0:T(8,128)(2,1)S(1)}, u32[]{:S(2)}, u32[]{:S(2)}) %collective-permute-start.10) | collective-permute-done | bytes 196640 | tf_op jit(solution)/shard_map/ppermute | solution.py:348
  41.1 2.1 %collective-permute-start.12 = (bf16[256,384]{1,0:T(8,128)(2,1)S(1)}, bf16[256,384]{1,0:T(8,128)(2,1)S(1)}, u32[]{:S(2)}, u32[]{:S(2)}) collective-permute-start(bf16[256,384]{1,0:T(8,128)(2,1)S(1)} %collective-permute-done.10.t2), channel_id=1, source_target_pairs={{0,8},{1,9},{2,10},{3,11},{4,12},{5,13},{6,14},{7,15},{8,0},{9,1},... | collective-permute-start | bytes 589832 | tf_op jit(solution)/shard_map/ppermute | solution.py:348
  43.2 2.2 %collective-permute-done.4.c0 = bf16[256,384]{1,0:T(8,128)(2,1)S(1)} collective-permute-done((bf16[256,384]{1,0:T(8,128)(2,1)S(1)}, bf16[256,384]{1,0:T(8,128)(2,1)S(1)}, u32[]{:S(2)}, u32[]{:S(2)}) %collective-permute-start.4) | collective-permute-done | bytes 196640 | tf_op jit(solution)/shard_map/ppermute | solution.py:348
  45.4 1.5 %collective-permute-done.5.c2 = bf16[256,384]{1,0:T(8,128)(2,1)S(1)} collective-permute-done((bf16[256,384]{1,0:T(8,128)(2,1)S(1)}, bf16[256,384]{1,0:T(8,128)(2,1)S(1)}, u32[]{:S(2)}, u32[]{:S(2)}) %collective-permute-start.5) | collective-permute-done | bytes 196640 | tf_op jit(solution)/shard_map/ppermute | solution.py:348
  47.0 1.4 %collective-permute-done.7.c3 = bf16[256,384]{1,0:T(8,128)(2,1)S(1)} collective-permute-done((bf16[256,384]{1,0:T(8,128)(2,1)S(1)}, bf16[256,384]{1,0:T(8,128)(2,1)S(1)}, u32[]{:S(2)}, u32[]{:S(2)}) %collective-permute-start.7) | collective-permute-done | bytes 196640 | tf_op jit(solution)/shard_map/ppermute | solution.py:348
  48.4 9.3 %attention.1 = (bf16[128,384]{1,0:T(8,128)(2,1)S(1)}, bf16[128,384]{1,0:T(8,128)(2,1)S(1)}, bf16[256,384]{1,0:T(8,128)(2,1)S(1)}, bf16[256,384]{1,0:T(8,128)(2,1)S(1)}) custom-call(s32[2]{0:T(128)S(1)} %pad_add_fusion.place, bf16[256,384]{1,0:T(8,128)(2,1)S(1)} %collective-permute-done.4.c0, bf16[256,384]{1,0:T(8,128)(2,1)S(1)} %collective-permute-done.5.c2, ...), custom_call_target="tpu_custom_call" | custom-call | flops 4000000000 | bytes 4000000 | tf_op jit(solution)/shard_map/attention/pallas_call | solution.py:319
  57.8 2.0 %collective-permute-start.15 = (bf16[256,384]{1,0:T(8,128)(2,1)S(1)}, bf16[256,384]{1,0:T(8,128)(2,1)S(1)}, u32[]{:S(2)}, u32[]{:S(2)}) collective-permute-start(bf16[256,384]{1,0:T(8,128)(2,1)S(1)} %get-tuple-element.16), channel_id=1, source_target_pairs={{0,0},{1,1},{2,8},{3,9},{4,4},{5,5},{6,12},{7,13},{8,2},{9,3},{10,... | collective-permute-start | bytes 589832 | tf_op jit(solution)/shard_map/ppermute | solution.py:348
  59.8 0.7 collective-permute-start.16
  60.5 4.5 %collective-permute-done.15.r0 = bf16[256,384]{1,0:T(8,128)(2,1)S(1)} collective-permute-done((bf16[256,384]{1,0:T(8,128)(2,1)S(1)}, bf16[256,384]{1,0:T(8,128)(2,1)S(1)}, u32[]{:S(2)}, u32[]{:S(2)}) %collective-permute-start.15) | collective-permute-done | bytes 196640 | tf_op jit(solution)/shard_map/ppermute | solution.py:348
  65.0 2.3 %collective-permute-done.16.r1 = bf16[256,384]{1,0:T(8,128)(2,1)S(1)} collective-permute-done((bf16[256,384]{1,0:T(8,128)(2,1)S(1)}, bf16[256,384]{1,0:T(8,128)(2,1)S(1)}, u32[]{:S(2)}, u32[]{:S(2)}) %collective-permute-start.16) | collective-permute-done | bytes 196640 | tf_op jit(solution)/shard_map/ppermute | solution.py:348
  67.4 2.5 %shard_map.103 = bf16[2,128,384]{2,1,0:T(8,128)(2,1)S(1)} custom-call(s32[2]{0:T(128)S(1)} %pad_add_fusion.place, bf16[256,384]{1,0:T(8,128)(2,1)S(1)} %collective-permute-done.15.r0, bf16[256,384]{1,0:T(8,128)(2,1)S(1)} %collective-permute-done.16.r1, bf16[3,3,3,384,384]{4,3,2,1,0:T(8,128)(2,1)S(1)} %shard_map.95.w_ref), custom_call_target="tpu_custom_call" | custom-call | flops 1019215872 | bytes 1048576 | tf_op jit(solution)/shard_map/pallas_call | solution.py:21
  69.8 1.9 %collective-permute-start.17 = (bf16[2,128,384]{2,1,0:T(8,128)(2,1)S(1)}, bf16[2,128,384]{2,1,0:T(8,128)(2,1)S(1)}, u32[]{:S(2)}, u32[]{:S(2)}) collective-permute-start(bf16[2,128,384]{2,1,0:T(8,128)(2,1)S(1)} %shard_map.103), channel_id=1, source_target_pairs={{8,0},{16,8},{24,16},{32,24},{40,32},{48,40},{56,48},{64,56},{72,6... | collective-permute-start | bytes 589832 | tf_op jit(solution)/shard_map/ppermute | solution.py:424
  71.8 2.9 %collective-permute-start.13 = (bf16[128,384]{1,0:T(8,128)(2,1)S(1)}, bf16[128,384]{1,0:T(8,128)(2,1)S(1)}, u32[]{:S(2)}, u32[]{:S(2)}) collective-permute-start(bf16[128,384]{1,0:T(8,128)(2,1)S(1)} %get-tuple-element.14), channel_id=1, source_target_pairs={{0,0},{1,1},{2,8},{3,9},{4,4},{5,5},{6,12},{7,13},{8,2},{9,3},{10,... | collective-permute-start | bytes 294920 | tf_op jit(solution)/shard_map/ppermute | solution.py:348
  74.7 0.7 collective-permute-start.14
  75.4 2.3 %collective-permute-done.13.out0 = bf16[128,384]{1,0:T(8,128)(2,1)S(1)} collective-permute-done((bf16[128,384]{1,0:T(8,128)(2,1)S(1)}, bf16[128,384]{1,0:T(8,128)(2,1)S(1)}, u32[]{:S(2)}, u32[]{:S(2)}) %collective-permute-start.13) | collective-permute-done | bytes 98336 | tf_op jit(solution)/shard_map/ppermute | solution.py:348
  77.7 3.5 %collective-permute-done.14.out1 = bf16[128,384]{1,0:T(8,128)(2,1)S(1)} collective-permute-done((bf16[128,384]{1,0:T(8,128)(2,1)S(1)}, bf16[128,384]{1,0:T(8,128)(2,1)S(1)}, u32[]{:S(2)}, u32[]{:S(2)}) %collective-permute-start.14) | collective-permute-done | bytes 98336 | tf_op jit(solution)/shard_map/ppermute | solution.py:348
  81.2 1.2 %shard_map.101 = bf16[2,128,384]{2,1,0:T(8,128)(2,1)} custom-call(s32[2]{0:T(128)S(1)} %pad_add_fusion.place, bf16[128,384]{1,0:T(8,128)(2,1)S(1)} %collective-permute-done.13.out0, bf16[128,384]{1,0:T(8,128)(2,1)S(1)} %collective-permute-done.14.out1), custom_call_target="tpu_custom_call" | custom-call | bytes 1048576 | tf_op jit(solution)/shard_map/pallas_call | solution.py:21
  82.5 2.5 %shard_map.102.own = f32[2,128,384]{2,1,0:T(8,128)S(1)} custom-call(s32[2]{0:T(128)S(1)} %pad_add_fusion.place, bf16[256,384]{1,0:T(8,128)(2,1)S(1)} %collective-permute-done.15.r0, bf16[256,384]{1,0:T(8,128)(2,1)S(1)} %collective-permute-done.16.r1, bf16[3,3,3,384,384]{4,3,2,1,0:T(8,128)(2,1)S(1)} %shard_map.95.w_ref), custom_call_target="tpu_custom_call" | custom-call | flops 1019215872 | bytes 1048576 | tf_op jit(solution)/shard_map/pallas_call | solution.py:21
  84.9 0.7 shard_map.104
  (30 shorter events, 2.0 us)
Async XLA Ops:
  0.6 17.9 %collective-permute-start = (bf16[256,384]{1,0:T(8,128)(2,1)}, bf16[256,384]{1,0:T(8,128)(2,1)S(1)}, u32[]{:S(2)}, u32[]{:S(2)}) collective-permute-start(bf16[256,384]{1,0:T(8,128)(2,1)} %bitcast.7), channel_id=1, source_target_pairs={{0,1},{1,0},{2,3},{3,2},{4,5},{5,4},{6,7},{7,6},{8,9},{9,8},{10,11... | collective-permute-start | bytes 589832 | tf_op jit(solution)/shard_map/ppermute | solution.py:348
  5.2 13.3 %collective-permute-start.1 = (bf16[128,384]{1,0:T(8,128)(2,1)S(1)}, bf16[128,384]{1,0:T(8,128)(2,1)S(1)}, u32[]{:S(2)}, u32[]{:S(2)}) collective-permute-start(bf16[128,384]{1,0:T(8,128)(2,1)S(1)} %bitcast.11), channel_id=1, source_target_pairs={{1,3},{2,0},{3,5},{4,2},{5,7},{6,4},{9,11},{10,8},{11,13},{12,10},... | collective-permute-start | bytes 294920 | tf_op jit(solution)/shard_map/ppermute | solution.py:348
  6.5 12.1 %collective-permute-start.2 = (bf16[128,384]{1,0:T(8,128)(2,1)S(1)}, bf16[128,384]{1,0:T(8,128)(2,1)S(1)}, u32[]{:S(2)}, u32[]{:S(2)}) collective-permute-start(bf16[128,384]{1,0:T(8,128)(2,1)S(1)} %bitcast.12), channel_id=1, source_target_pairs={{1,2},{2,1},{3,4},{4,3},{5,6},{6,5},{9,10},{10,9},{11,12},{12,11},... | collective-permute-start | bytes 294920 | tf_op jit(solution)/shard_map/ppermute | solution.py:348
  7.2 16.6 %collective-permute-start.8 = (bf16[2,128,384]{2,1,0:T(8,128)(2,1)}, bf16[2,128,384]{2,1,0:T(8,128)(2,1)S(1)}, u32[]{:S(2)}, u32[]{:S(2)}) collective-permute-start(bf16[2,128,384]{2,1,0:T(8,128)(2,1)} %bitcast.13), channel_id=1, source_target_pairs={{0,0},{1,1},{2,8},{3,9},{4,4},{5,5},{6,12},{7,13},{8,2},{9,3},{10,... | collective-permute-start | bytes 589832 | tf_op jit(solution)/shard_map/ppermute | solution.py:348
  15.2 3.4 %copy-start = (bf16[2,2,64,384]{3,2,1,0:T(8,128)(2,1)S(1)}, bf16[2,2,64,384]{3,2,1,0:T(8,128)(2,1)}, u32[]{:S(2)}) copy-start(bf16[2,2,64,384]{3,2,1,0:T(8,128)(2,1)} %param.8) | copy-start | bytes 589828
  18.5 28.5 %copy-start.5 = (f32[384]{0:T(512)S(1)}, f32[384]{0:T(512)}, u32[]{:S(2)}) copy-start(f32[384]{0:T(512)} %param.10) | copy-start | bytes 4612
  18.5 29.9 %copy-start.1 = (bf16[384,384]{1,0:T(8,128)(2,1)S(1)}, bf16[384,384]{1,0:T(8,128)(2,1)}, u32[]{:S(2)}) copy-start(bf16[384,384]{1,0:T(8,128)(2,1)} %wq.1) | copy-start | bytes 884740
  18.5 29.9 %copy-start.2 = (bf16[384,384]{1,0:T(8,128)(2,1)S(1)}, bf16[384,384]{1,0:T(8,128)(2,1)}, u32[]{:S(2)}) copy-start(bf16[384,384]{1,0:T(8,128)(2,1)} %wk.1) | copy-start | bytes 884740
  18.5 29.9 %copy-start.3 = (bf16[384,384]{1,0:T(8,128)(2,1)S(1)}, bf16[384,384]{1,0:T(8,128)(2,1)}, u32[]{:S(2)}) copy-start(bf16[384,384]{1,0:T(8,128)(2,1)} %wv.1) | copy-start | bytes 884740
  18.5 29.9 %copy-start.4 = (bf16[384,384]{1,0:T(8,128)(2,1)S(1)}, bf16[384,384]{1,0:T(8,128)(2,1)}, u32[]{:S(2)}) copy-start(bf16[384,384]{1,0:T(8,128)(2,1)} %wo.1) | copy-start | bytes 884740
  21.8 14.7 %collective-permute-start.3 = (bf16[256,384]{1,0:T(8,128)(2,1)S(1)}, bf16[256,384]{1,0:T(8,128)(2,1)S(1)}, u32[]{:S(2)}, u32[]{:S(2)}) collective-permute-start(bf16[256,384]{1,0:T(8,128)(2,1)S(1)} %get-tuple-element.11), channel_id=1, source_target_pairs={{0,8},{8,16},{16,24},{24,32},{32,40},{40,48},{48,56},{56,64},{64,7... | collective-permute-start | bytes 589832 | tf_op jit(solution)/shard_map/ppermute | solution.py:397
  24.3 5.4 %collective-permute-start.9 = (bf16[128,384]{1,0:T(8,128)(2,1)S(1)}, bf16[128,384]{1,0:T(8,128)(2,1)S(1)}, u32[]{:S(2)}, u32[]{:S(2)}) collective-permute-start(bf16[128,384]{1,0:T(8,128)(2,1)S(1)} %get-tuple-element.13), channel_id=1, source_target_pairs={{0,1},{1,0},{2,3},{3,2},{4,5},{5,4},{6,7},{7,6},{8,9},{9,8},{10,11... | collective-permute-start | bytes 294920 | tf_op jit(solution)/shard_map/ppermute | solution.py:348
  30.4 10.7 %collective-permute-start.10 = (bf16[256,384]{1,0:T(8,128)(2,1)S(1)}, bf16[256,384]{1,0:T(8,128)(2,1)S(1)}, u32[]{:S(2)}, u32[]{:S(2)}) collective-permute-start(bf16[256,384]{1,0:T(8,128)(2,1)S(1)} %shard_map.100.t0), channel_id=1, source_target_pairs={{0,4},{1,5},{2,6},{3,7},{4,0},{5,1},{6,2},{7,3},{8,12},{9,13},{10,... | collective-permute-start | bytes 589832 | tf_op jit(solution)/shard_map/ppermute | solution.py:348
  36.6 8.8 %collective-permute-start.4 = (bf16[256,384]{1,0:T(8,128)(2,1)S(1)}, bf16[256,384]{1,0:T(8,128)(2,1)S(1)}, u32[]{:S(2)}, u32[]{:S(2)}) collective-permute-start(bf16[256,384]{1,0:T(8,128)(2,1)S(1)} %shard_map.98), channel_id=1, source_target_pairs={{0,0},{1,1},{2,8},{3,9},{4,4},{5,5},{6,12},{7,13},{8,2},{9,3},{10,... | collective-permute-start | bytes 589832 | tf_op jit(solution)/shard_map/ppermute | solution.py:348
  38.5 8.4 %collective-permute-start.5 = (bf16[256,384]{1,0:T(8,128)(2,1)S(1)}, bf16[256,384]{1,0:T(8,128)(2,1)S(1)}, u32[]{:S(2)}, u32[]{:S(2)}) collective-permute-start(bf16[256,384]{1,0:T(8,128)(2,1)S(1)} %shard_map.98), channel_id=1, source_target_pairs={{0,4},{1,5},{2,12},{3,13},{4,0},{5,1},{6,8},{7,9},{8,6},{9,7},{10,... | collective-permute-start | bytes 589832 | tf_op jit(solution)/shard_map/ppermute | solution.py:348
  39.2 7.8 %collective-permute-start.11 = (bf16[256,384]{1,0:T(8,128)(2,1)S(1)}, bf16[256,384]{1,0:T(8,128)(2,1)S(1)}, u32[]{:S(2)}, u32[]{:S(2)}) collective-permute-start(bf16[256,384]{1,0:T(8,128)(2,1)S(1)} %shard_map.100.t0), channel_id=1, source_target_pairs={{0,8},{1,9},{2,10},{3,11},{4,12},{5,13},{6,14},{7,15},{8,0},{9,1},... | collective-permute-start | bytes 589832 | tf_op jit(solution)/shard_map/ppermute | solution.py:348
  41.1 5.9 %collective-permute-start.12 = (bf16[256,384]{1,0:T(8,128)(2,1)S(1)}, bf16[256,384]{1,0:T(8,128)(2,1)S(1)}, u32[]{:S(2)}, u32[]{:S(2)}) collective-permute-start(bf16[256,384]{1,0:T(8,128)(2,1)S(1)} %collective-permute-done.10.t2), channel_id=1, source_target_pairs={{0,8},{1,9},{2,10},{3,11},{4,12},{5,13},{6,14},{7,15},{8,0},{9,1},... | collective-permute-start | bytes 589832 | tf_op jit(solution)/shard_map/ppermute | solution.py:348
  45.4 1.6 %collective-permute-start.6 = (bf16[256,384]{1,0:T(8,128)(2,1)S(1)}, bf16[256,384]{1,0:T(8,128)(2,1)S(1)}, u32[]{:S(2)}, u32[]{:S(2)}) collective-permute-start(bf16[256,384]{1,0:T(8,128)(2,1)S(1)} %collective-permute-done.4.c0), channel_id=1, source_target_pairs={{0,8},{1,9},{2,10},{3,11},{4,12},{5,13},{6,14},{7,15},{8,0},{9,1},... | collective-permute-start | bytes 589832 | tf_op jit(solution)/shard_map/ppermute | solution.py:348
  46.9 1.4 %collective-permute-start.7 = (bf16[256,384]{1,0:T(8,128)(2,1)S(1)}, bf16[256,384]{1,0:T(8,128)(2,1)S(1)}, u32[]{:S(2)}, u32[]{:S(2)}) collective-permute-start(bf16[256,384]{1,0:T(8,128)(2,1)S(1)} %collective-permute-done.5.c2), channel_id=1, source_target_pairs={{0,8},{1,9},{2,10},{3,11},{4,12},{5,13},{6,14},{7,15},{8,0},{9,1},... | collective-permute-start | bytes 589832 | tf_op jit(solution)/shard_map/ppermute | solution.py:348
  57.8 7.3 %collective-permute-start.15 = (bf16[256,384]{1,0:T(8,128)(2,1)S(1)}, bf16[256,384]{1,0:T(8,128)(2,1)S(1)}, u32[]{:S(2)}, u32[]{:S(2)}) collective-permute-start(bf16[256,384]{1,0:T(8,128)(2,1)S(1)} %get-tuple-element.16), channel_id=1, source_target_pairs={{0,0},{1,1},{2,8},{3,9},{4,4},{5,5},{6,12},{7,13},{8,2},{9,3},{10,... | collective-permute-start | bytes 589832 | tf_op jit(solution)/shard_map/ppermute | solution.py:348
  59.8 7.6 %collective-permute-start.16 = (bf16[256,384]{1,0:T(8,128)(2,1)S(1)}, bf16[256,384]{1,0:T(8,128)(2,1)S(1)}, u32[]{:S(2)}, u32[]{:S(2)}) collective-permute-start(bf16[256,384]{1,0:T(8,128)(2,1)S(1)} %get-tuple-element.17), channel_id=1, source_target_pairs={{0,1},{1,0},{2,9},{3,8},{4,5},{5,4},{6,13},{7,12},{8,3},{9,2},{10,... | collective-permute-start | bytes 589832 | tf_op jit(solution)/shard_map/ppermute | solution.py:348
  69.8 15.1 %collective-permute-start.17 = (bf16[2,128,384]{2,1,0:T(8,128)(2,1)S(1)}, bf16[2,128,384]{2,1,0:T(8,128)(2,1)S(1)}, u32[]{:S(2)}, u32[]{:S(2)}) collective-permute-start(bf16[2,128,384]{2,1,0:T(8,128)(2,1)S(1)} %shard_map.103), channel_id=1, source_target_pairs={{8,0},{16,8},{24,16},{32,24},{40,32},{48,40},{56,48},{64,56},{72,6... | collective-permute-start | bytes 589832 | tf_op jit(solution)/shard_map/ppermute | solution.py:424
  71.8 5.9 %collective-permute-start.13 = (bf16[128,384]{1,0:T(8,128)(2,1)S(1)}, bf16[128,384]{1,0:T(8,128)(2,1)S(1)}, u32[]{:S(2)}, u32[]{:S(2)}) collective-permute-start(bf16[128,384]{1,0:T(8,128)(2,1)S(1)} %get-tuple-element.14), channel_id=1, source_target_pairs={{0,0},{1,1},{2,8},{3,9},{4,4},{5,5},{6,12},{7,13},{8,2},{9,3},{10,... | collective-permute-start | bytes 294920 | tf_op jit(solution)/shard_map/ppermute | solution.py:348
  74.7 6.5 %collective-permute-start.14 = (bf16[128,384]{1,0:T(8,128)(2,1)S(1)}, bf16[128,384]{1,0:T(8,128)(2,1)S(1)}, u32[]{:S(2)}, u32[]{:S(2)}) collective-permute-start(bf16[128,384]{1,0:T(8,128)(2,1)S(1)} %get-tuple-element.15), channel_id=1, source_target_pairs={{0,1},{1,0},{2,9},{3,8},{4,5},{5,4},{6,13},{7,12},{8,3},{9,2},{10,... | collective-permute-start | bytes 294920 | tf_op jit(solution)/shard_map/ppermute | solution.py:348

commit v3 on v2

--- a/solution.py
+++ b/solution.py
@@ -11,6 +11,7 @@
 F32 = jnp.float32
 BF16 = jnp.bfloat16
 MIB = 1024 * 1024
+LOG2E = 1.4426950408889634
 LOAD = 42 * MIB
 VM = pl.BlockSpec(memory_space=pltpu.VMEM)
 SM = pl.BlockSpec(memory_space=pltpu.SMEM)
@@ -21,7 +22,7 @@
     return pl.pallas_call(
         kernel,
         in_specs=specs,
-        out_specs=[outs] * len(shapes),
+        out_specs=list(outs) if isinstance(outs, tuple) else [outs] * len(shapes),
         out_shape=[jax.ShapeDtypeStruct(dims, dtype) for dims, dtype in shapes],
         scratch_shapes=scratch,
         compiler_params=pltpu.CompilerParams(vmem_limit_bytes=limit),
@@ -29,18 +30,6 @@
     )(*operands)
 
 
-def pick_kernel(place, both, same, other):
-    x = place[0]
-    same[...] = both[x]
-    other[...] = both[1 - x]
-
-
-def pick(place, both):
-    return call(
-        pick_kernel, (place, both), [SM, VM], [(both.shape[1:], both.dtype)] * 2, [], 4 * MIB
-    )
-
-
 def join_kernel(place, same, other, out):
     x = place[0]
     half = same.shape[0]
@@ -53,14 +42,6 @@
     return call(join_kernel, (place, same, other), [SM, VM, VM], [(shape, BF16)], [], 4 * MIB)[0]
 
 
-def merge_kernel(own, cached, out):
-    out[...] = (own[...] + cached[...].astype(F32)).astype(BF16)
-
-
-def merge(own, cached):
-    return call(merge_kernel, (own, cached), [VM, VM], [(own.shape, BF16)], [], 8 * MIB)[0]
-
-
 def load_kernel(w_hbm, w_out, sem):
     copy = pltpu.make_async_copy(w_hbm, w_out, sem)
     copy.start()
@@ -70,25 +51,6 @@
 def load(weight):
     return call(
         load_kernel, (weight,), [HBM], [(weight.shape, BF16)], [pltpu.SemaphoreType.DMA], LOAD
-    )[0]
-
-
-def deliver_kernel(place, out0, out1, block_out, sems):
-    x = place[0]
-    copies = [
-        pltpu.make_async_copy(out0, block_out.at[x], sems.at[0]),
-        pltpu.make_async_copy(out1, block_out.at[1 - x], sems.at[1]),
-    ]
-    for copy in copies:
-        copy.start()
-    for copy in copies:
-        copy.wait()
-
-
-def deliver(place, out0, out1):
-    return call(
-        deliver_kernel, (place, out0, out1), [SM, VM, VM], [((2,) + out0.shape, BF16)],
-        [pltpu.SemaphoreType.DMA((2,))], 8 * MIB, outs=HBM,
     )[0]
 
 
@@ -205,6 +167,19 @@
         rows = jnp.where(swapped, b[...], a[...])
         fill(taps, f, 0, rows.reshape(4, width, chans), width, True)
     conv_steps(taps, w_ref, main, side, out, src, dst, True)
+
+
+def last_kernel(place, r0, r1, out0, out1, w_ref, out, block_out, taps, sems):
+    x = place[0]
+    copies = [
+        pltpu.make_async_copy(out0, block_out.at[x], sems.at[0]),
+        pltpu.make_async_copy(out1, block_out.at[1 - x], sems.at[1]),
+    ]
+    for copy in copies:
+        copy.start()
+    backward_kernel(2, 1, 1, 0, place, r0, r1, w_ref, out, taps)
+    for copy in copies:
+        copy.wait()
 
 
 def conv_call(kernel, place, operands, weight, width, dtype):
@@ -267,13 +242,20 @@
         v_s[rows] = mm(act, wv[...]).astype(BF16)
         g_s[rows] = mm_t(cot_s[rows], wo[...]).astype(BF16)
     attended = grad_q = None
-    for at, n in CHUNKS:
+
+    def products(at, n):
         rows = slice(at, at + n)
-        scores = mm_t(q_s[rows], k_s[...]) * scale
+        return mm_t(q_s[rows], k_s[...]), mm_t(g_s[rows], v_s[...])
+
+    ahead = products(*CHUNKS[0])
+    for i, (at, n) in enumerate(CHUNKS):
+        rows = slice(at, at + n)
+        scores, dprob = ahead
+        if i + 1 < len(CHUNKS):
+            ahead = products(*CHUNKS[i + 1])
         top = jnp.max(scores, axis=-1, keepdims=True)
-        expo = jnp.exp(scores - top)
+        expo = jnp.exp2((scores - top) * (scale * LOG2E))
         inv_total = 1.0 / jnp.sum(expo, axis=-1, keepdims=True)
-        dprob = mm_t(g_s[rows], v_s[...])
         delta = jnp.sum(expo * dprob, axis=-1, keepdims=True) * inv_total
         if at == 0:
             probs = expo * inv_total
@@ -387,7 +369,8 @@
     far_same = send(edge, runs, straight)
     cot_b = send(cotangent.reshape(2, block, chans), runs, home(0, 0))
     weight = load(conv_weight)
-    cot_same, cot_other = pick(place, cot_b)
+    cot_same = lax.dynamic_index_in_dim(cot_b, x, 0, keepdims=False)
+    cot_other = lax.dynamic_index_in_dim(cot_b, 1 - x, 0, keepdims=False)
     quad = (2 * block, chans)
     for_next, taps = call(
         next_kernel, (place, mine, packet, far_same, far_other, weight), [SM] + [VM] * 5,
@@ -402,7 +385,7 @@
     )[0]
     cot_b = join(place, cot_same, cot_other)
     cot_c = send(cot_b, runs, lambda c, y, x: (c, y ^ 2, x))
-    conv = merge(own, cached)
+    conv = (own + cached.astype(F32)).astype(BF16)
     conv_c = send(conv, runs, home(1, 0))
     conv_b = send(conv, runs, home(0, 0))
     cots = (cot_b, cot_c, send(cot_b, runs, swap), send(cot_c, runs, swap))
@@ -422,8 +405,12 @@
     slab = (grad0, grad1)
     for_last = backward(0, 1, 0, 1, BF16)
     handed = lax.ppermute(for_last, "tm", [(i + 1, i) for i in range(runs - 1)])
-    own_grad = backward(2, 1, 1, 0, F32)
-    block_out = deliver(place, out0, out1)
+    own_grad, block_out = call(
+        last_kernel, (place, grad0, grad1, out0, out1, weight), [SM] + [VM] * 5,
+        [((2, block, chans), F32), ((2, block, chans), BF16)],
+        [pltpu.VMEM((2, 4, width, 3 * chans), BF16), pltpu.SemaphoreType.DMA((2,))],
+        24 * MIB, 10**9, outs=(VM, HBM),
+    )
     video_grad = finish(own_grad, handed)
     return block_out.reshape(video.shape), video_grad.reshape(video.shape)
 

time: 86.1 us -> 90 us (1.045)
  local copies, waits for them, and re-layouts: 0.97 us -> 7.37 us
  Pallas kernels: 25.6 us -> 23.6 us
  waiting for transfers between devices: 21.8 us -> 20.8 us
    unnamed x12 -> x20, local copies, waits for them, and re-layouts: 0.04 us -> 6.4 us
    pallas_call x10 -> x7, Pallas kernels: 16.2 us -> 15.1 us  [call(): pl.pallas_call(kernel, in_specs=specs, out_specs=list(outs) if isinstance...]
    ppermute x16, waiting for transfers between devices: 21.8 us -> 20.8 us  [send(): return lax.ppermute(value, ('tm', 'rows'), pairs)]
  transfers between devices with their start and end apart: 18 -> 18, of which waited for: 9 -> 9; matrix products, arithmetic and copies ran while one was open for 1% -> 1% of each run, Pallas kernels for 15% -> 13%
where the time goes in v3:
time: 90 us; the launch traced here: 89.7 us
  starting transfers between devices  36.7 us (41%)
  Pallas kernels  23.6 us (26%)
  waiting for transfers between devices  20.8 us (23%)
  local copies, waits for them, and re-layouts  7.37 us (8%)
  between operations  1.09 us (1%)
    ppermute x16, starting transfers between devices, send(): return lax.ppermute(value, ('tm', 'rows'), pairs)  32.7 us
    ppermute x16, waiting for transfers between devices, send(): return lax.ppermute(value, ('tm', 'rows'), pairs)  20.8 us
    pallas_call x7, Pallas kernels, call(): pl.pallas_call(kernel, in_specs=specs, out_specs=list(outs) if isinstance...  15.1 us
    pallas_call x1, Pallas kernels, attention(): pl.pallas_call(attention_kernel, in_specs=[SM] + [VM] * (len(convs) + len...  8.46 us
    unnamed x20, local copies, waits for them, and re-layouts  6.4 us
    ppermute x1, starting transfers between devices, local(): cached = lax.ppermute(for_next, 'tm', [(i, i + 1) for i in range(runs - 1)])  2.05 us
    ppermute x1, starting transfers between devices, local(): handed = lax.ppermute(for_last, 'tm', [(i + 1, i) for i in range(runs - 1)])  1.92 us
  transfers between devices with their start and end apart: 18, of which 9 were waited for; matrix products, arithmetic and copies ran while one was open for 1% of the time, Pallas kernels for 13%

profile of v3, /device:TPU:1, one launch (start us, length us, event | category | flops | bytes accessed | tf_op | source)
XLA Modules:
  0.0 89.7 jit_solution(10218726366151226885)
XLA Ops:
  0.6 3.6 %collective-permute-start = (bf16[256,384]{1,0:T(8,128)(2,1)}, bf16[256,384]{1,0:T(8,128)(2,1)S(1)}, u32[]{:S(2)}, u32[]{:S(2)}) collective-permute-start(bf16[256,384]{1,0:T(8,128)(2,1)} %bitcast.13), channel_id=1, source_target_pairs={{0,1},{1,0},{2,3},{3,2},{4,5},{5,4},{6,7},{7,6},{8,9},{9,8},{10,11... | collective-permute-start | bytes 589832 | tf_op jit(solution)/shard_map/ppermute | solution.py:330
  4.3 0.9 %constant_dynamic-slice_fusion = bf16[2,1,64,384]{3,2,1,0:T(8,128)(2,1)S(1)} fusion(bf16[2,2,64,384]{3,2,1,0:T(8,128)(2,1)} %param.8, s32[]{:T(128)S(6)} %select_n.27), kind=kLoop, calls=%fused_computation.3 | loop fusion | bytes 196612 | tf_op jit(solution)/shard_map/jit(dynamic_index_in_dim)/dynamic_slice | solution.py:365
  5.2 1.3 %collective-permute-start.1 = (bf16[128,384]{1,0:T(8,128)(2,1)S(1)}, bf16[128,384]{1,0:T(8,128)(2,1)S(1)}, u32[]{:S(2)}, u32[]{:S(2)}) collective-permute-start(bf16[128,384]{1,0:T(8,128)(2,1)S(1)} %bitcast.16), channel_id=1, source_target_pairs={{1,3},{2,0},{3,5},{4,2},{5,7},{6,4},{9,11},{10,8},{11,13},{12,10},... | collective-permute-start | bytes 294920 | tf_op jit(solution)/shard_map/ppermute | solution.py:330
  7.2 7.9 %collective-permute-start.8 = (bf16[2,128,384]{2,1,0:T(8,128)(2,1)}, bf16[2,128,384]{2,1,0:T(8,128)(2,1)S(1)}, u32[]{:S(2)}, u32[]{:S(2)}) collective-permute-start(bf16[2,128,384]{2,1,0:T(8,128)(2,1)} %bitcast.18), channel_id=1, source_target_pairs={{0,0},{1,1},{2,8},{3,9},{4,4},{5,5},{6,12},{7,13},{8,2},{9,3},{10,... | collective-permute-start | bytes 589832 | tf_op jit(solution)/shard_map/ppermute | solution.py:330
  15.1 3.3 %shard_map.95.w_ref = bf16[3,3,3,384,384]{4,3,2,1,0:T(8,128)(2,1)S(1)} custom-call(bf16[3,3,3,384,384]{4,3,2,1,0:T(8,128)(2,1)} %w_hbm.1), custom_call_target="tpu_custom_call" | custom-call | bytes 1048576 | tf_op jit(solution)/shard_map/pallas_call | solution.py:22
  18.4 3.1 %copy-done = bf16[3,3,3,384,384]{4,3,2,1,0:T(8,128)(2,1)} copy-done((bf16[3,3,3,384,384]{4,3,2,1,0:T(8,128)(2,1)}, bf16[3,3,3,384,384]{4,3,2,1,0:T(8,128)(2,1)S(1)}, u32[]{:S(2)}) %copy-start) | copy-done | bytes 7962648
  21.6 3.3 %copy-done.1 = bf16[3,3,3,384,384]{4,3,2,1,0:T(8,128)(2,1)S(1)} copy-done((bf16[3,3,3,384,384]{4,3,2,1,0:T(8,128)(2,1)S(1)}, bf16[3,3,3,384,384]{4,3,2,1,0:T(8,128)(2,1)}, u32[]{:S(2)}) %copy-start.1) | copy-done | bytes 7962648
  24.9 3.3 %shard_map.96 = (bf16[256,384]{1,0:T(8,128)(2,1)S(1)}, bf16[2,6,64,1152]{3,2,1,0:T(8,128)(2,1)S(1)}) custom-call(s32[2]{0:T(128)S(1)} %pad_add_fusion.place, bf16[256,384]{1,0:T(8,128)(2,1)S(1)} %bitcast.14, bf16[256,384]{1,0:T(8,128)(2,1)S(1)} %collective-permute-done.packet, bf16[128,384]{1,0:T(8,128)(2,1)S(1)} %collective-permute-done.1.far_same, ...), custom_call_target="tpu_custom_call" | custom-call | flops 1000000000 | bytes 1048576 | tf_op jit(solution)/shard_map/pallas_call | solution.py:22
  28.2 2.1 %collective-permute-start.3 = (bf16[256,384]{1,0:T(8,128)(2,1)S(1)}, bf16[256,384]{1,0:T(8,128)(2,1)S(1)}, u32[]{:S(2)}, u32[]{:S(2)}) collective-permute-start(bf16[256,384]{1,0:T(8,128)(2,1)S(1)} %get-tuple-element.11), channel_id=1, source_target_pairs={{0,8},{8,16},{16,24},{24,32},{32,40},{40,48},{48,56},{56,64},{64,7... | collective-permute-start | bytes 589832 | tf_op jit(solution)/shard_map/ppermute | solution.py:380
  30.3 1.7 %collective-permute-start.9 = (bf16[128,384]{1,0:T(8,128)(2,1)S(1)}, bf16[128,384]{1,0:T(8,128)(2,1)S(1)}, u32[]{:S(2)}, u32[]{:S(2)}) collective-permute-start(bf16[128,384]{1,0:T(8,128)(2,1)S(1)} %get-tuple-element.18), channel_id=1, source_target_pairs={{0,1},{1,0},{2,3},{3,2},{4,5},{5,4},{6,7},{7,6},{8,9},{9,8},{10,11... | collective-permute-start | bytes 294920 | tf_op jit(solution)/shard_map/ppermute | solution.py:330
  32.0 1.7 %shard_map.97 = f32[256,384]{1,0:T(8,128)S(1)} custom-call(s32[2]{0:T(128)S(1)} %pad_add_fusion.place, bf16[2,6,64,1152]{3,2,1,0:T(8,128)(2,1)S(1)} %get-tuple-element.10.taps, bf16[3,3,3,384,384]{4,3,2,1,0:T(8,128)(2,1)S(1)} %copy-done.1), custom_call_target="tpu_custom_call" | custom-call | flops 1000000000 | bytes 1048576 | tf_op jit(solution)/shard_map/pallas_call | solution.py:22
  33.7 2.1 %collective-permute-done.9.other = bf16[128,384]{1,0:T(8,128)(2,1)S(1)} collective-permute-done((bf16[128,384]{1,0:T(8,128)(2,1)S(1)}, bf16[128,384]{1,0:T(8,128)(2,1)S(1)}, u32[]{:S(2)}, u32[]{:S(2)}) %collective-permute-start.9) | collective-permute-done | bytes 98336 | tf_op jit(solution)/shard_map/ppermute | solution.py:330
  36.4 5.3 %collective-permute-start.10 = (bf16[256,384]{1,0:T(8,128)(2,1)S(1)}, bf16[256,384]{1,0:T(8,128)(2,1)S(1)}, u32[]{:S(2)}, u32[]{:S(2)}) collective-permute-start(bf16[256,384]{1,0:T(8,128)(2,1)S(1)} %shard_map.98.t0), channel_id=1, source_target_pairs={{0,4},{1,5},{2,6},{3,7},{4,0},{5,1},{6,2},{7,3},{8,12},{9,13},{10,... | collective-permute-start | bytes 589832 | tf_op jit(solution)/shard_map/ppermute | solution.py:330
  41.7 1.9 %collective-permute-start.4 = (bf16[256,384]{1,0:T(8,128)(2,1)S(1)}, bf16[256,384]{1,0:T(8,128)(2,1)S(1)}, u32[]{:S(2)}, u32[]{:S(2)}) collective-permute-start(bf16[256,384]{1,0:T(8,128)(2,1)S(1)} %add_convert_fusion), channel_id=1, source_target_pairs={{0,0},{1,1},{2,8},{3,9},{4,4},{5,5},{6,12},{7,13},{8,2},{9,3},{10,... | collective-permute-start | bytes 589832 | tf_op jit(solution)/shard_map/ppermute | solution.py:330
  43.7 0.8 collective-permute-start.5
  44.4 1.4 %collective-permute-done.10.t2 = bf16[256,384]{1,0:T(8,128)(2,1)S(1)} collective-permute-done((bf16[256,384]{1,0:T(8,128)(2,1)S(1)}, bf16[256,384]{1,0:T(8,128)(2,1)S(1)}, u32[]{:S(2)}, u32[]{:S(2)}) %collective-permute-start.10) | collective-permute-done | bytes 196640 | tf_op jit(solution)/shard_map/ppermute | solution.py:330
  45.8 3.0 %collective-permute-start.12 = (bf16[256,384]{1,0:T(8,128)(2,1)S(1)}, bf16[256,384]{1,0:T(8,128)(2,1)S(1)}, u32[]{:S(2)}, u32[]{:S(2)}) collective-permute-start(bf16[256,384]{1,0:T(8,128)(2,1)S(1)} %collective-permute-done.10.t2), channel_id=1, source_target_pairs={{0,8},{1,9},{2,10},{3,11},{4,12},{5,13},{6,14},{7,15},{8,0},{9,1},... | collective-permute-start | bytes 589832 | tf_op jit(solution)/shard_map/ppermute | solution.py:330
  48.8 2.1 %collective-permute-done.4.c0 = bf16[256,384]{1,0:T(8,128)(2,1)S(1)} collective-permute-done((bf16[256,384]{1,0:T(8,128)(2,1)S(1)}, bf16[256,384]{1,0:T(8,128)(2,1)S(1)}, u32[]{:S(2)}, u32[]{:S(2)}) %collective-permute-start.4) | collective-permute-done | bytes 196640 | tf_op jit(solution)/shard_map/ppermute | solution.py:330
  50.9 1.4 %collective-permute-done.5.c2 = bf16[256,384]{1,0:T(8,128)(2,1)S(1)} collective-permute-done((bf16[256,384]{1,0:T(8,128)(2,1)S(1)}, bf16[256,384]{1,0:T(8,128)(2,1)S(1)}, u32[]{:S(2)}, u32[]{:S(2)}) %collective-permute-start.5) | collective-permute-done | bytes 196640 | tf_op jit(solution)/shard_map/ppermute | solution.py:330
  52.3 1.4 %collective-permute-done.7.c3 = bf16[256,384]{1,0:T(8,128)(2,1)S(1)} collective-permute-done((bf16[256,384]{1,0:T(8,128)(2,1)S(1)}, bf16[256,384]{1,0:T(8,128)(2,1)S(1)}, u32[]{:S(2)}, u32[]{:S(2)}) %collective-permute-start.7) | collective-permute-done | bytes 196640 | tf_op jit(solution)/shard_map/ppermute | solution.py:330
  53.7 8.5 %attention.1 = (bf16[128,384]{1,0:T(8,128)(2,1)S(1)}, bf16[128,384]{1,0:T(8,128)(2,1)S(1)}, bf16[256,384]{1,0:T(8,128)(2,1)S(1)}, bf16[256,384]{1,0:T(8,128)(2,1)S(1)}) custom-call(s32[2]{0:T(128)S(1)} %pad_add_fusion.place, bf16[256,384]{1,0:T(8,128)(2,1)S(1)} %collective-permute-done.4.c0, bf16[256,384]{1,0:T(8,128)(2,1)S(1)} %collective-permute-done.5.c2, ...), custom_call_target="tpu_custom_call" | custom-call | flops 4000000000 | bytes 4000000 | tf_op jit(solution)/shard_map/attention/pallas_call | solution.py:301
  62.2 1.9 %collective-permute-start.13 = (bf16[256,384]{1,0:T(8,128)(2,1)S(1)}, bf16[256,384]{1,0:T(8,128)(2,1)S(1)}, u32[]{:S(2)}, u32[]{:S(2)}) collective-permute-start(bf16[256,384]{1,0:T(8,128)(2,1)S(1)} %get-tuple-element.12), channel_id=1, source_target_pairs={{0,0},{1,1},{2,8},{3,9},{4,4},{5,5},{6,12},{7,13},{8,2},{9,3},{10,... | collective-permute-start | bytes 589832 | tf_op jit(solution)/shard_map/ppermute | solution.py:330
  64.7 4.8 %collective-permute-done.13.r0 = bf16[256,384]{1,0:T(8,128)(2,1)S(1)} collective-permute-done((bf16[256,384]{1,0:T(8,128)(2,1)S(1)}, bf16[256,384]{1,0:T(8,128)(2,1)S(1)}, u32[]{:S(2)}, u32[]{:S(2)}) %collective-permute-start.13) | collective-permute-done | bytes 196640 | tf_op jit(solution)/shard_map/ppermute | solution.py:330
  69.5 2.2 %collective-permute-done.14.r1 = bf16[256,384]{1,0:T(8,128)(2,1)S(1)} collective-permute-done((bf16[256,384]{1,0:T(8,128)(2,1)S(1)}, bf16[256,384]{1,0:T(8,128)(2,1)S(1)}, u32[]{:S(2)}, u32[]{:S(2)}) %collective-permute-start.14) | collective-permute-done | bytes 196640 | tf_op jit(solution)/shard_map/ppermute | solution.py:330
  71.7 2.5 %shard_map.100 = bf16[2,128,384]{2,1,0:T(8,128)(2,1)S(1)} custom-call(s32[2]{0:T(128)S(1)} %pad_add_fusion.place, bf16[256,384]{1,0:T(8,128)(2,1)S(1)} %collective-permute-done.13.r0, bf16[256,384]{1,0:T(8,128)(2,1)S(1)} %collective-permute-done.14.r1, bf16[3,3,3,384,384]{4,3,2,1,0:T(8,128)(2,1)S(1)} %bitcast.12), custom_call_target="tpu_custom_call" | custom-call | flops 1019215872 | bytes 1048576 | tf_op jit(solution)/shard_map/pallas_call | solution.py:22
  74.2 1.9 %collective-permute-start.17 = (bf16[2,128,384]{2,1,0:T(8,128)(2,1)S(1)}, bf16[2,128,384]{2,1,0:T(8,128)(2,1)S(1)}, u32[]{:S(2)}, u32[]{:S(2)}) collective-permute-start(bf16[2,128,384]{2,1,0:T(8,128)(2,1)S(1)} %shard_map.100), channel_id=1, source_target_pairs={{8,0},{16,8},{24,16},{32,24},{40,32},{48,40},{56,48},{64,56},{72,6... | collective-permute-start | bytes 589832 | tf_op jit(solution)/shard_map/ppermute | solution.py:407
  76.2 3.0 %collective-permute-start.15 = (bf16[128,384]{1,0:T(8,128)(2,1)S(1)}, bf16[128,384]{1,0:T(8,128)(2,1)S(1)}, u32[]{:S(2)}, u32[]{:S(2)}) collective-permute-start(bf16[128,384]{1,0:T(8,128)(2,1)S(1)} %get-tuple-element.14), channel_id=1, source_target_pairs={{0,0},{1,1},{2,8},{3,9},{4,4},{5,5},{6,12},{7,13},{8,2},{9,3},{10,... | collective-permute-start | bytes 294920 | tf_op jit(solution)/shard_map/ppermute | solution.py:330
  79.2 1.0 %collective-permute-start.16 = (bf16[128,384]{1,0:T(8,128)(2,1)S(1)}, bf16[128,384]{1,0:T(8,128)(2,1)S(1)}, u32[]{:S(2)}, u32[]{:S(2)}) collective-permute-start(bf16[128,384]{1,0:T(8,128)(2,1)S(1)} %get-tuple-element.15), channel_id=1, source_target_pairs={{0,1},{1,0},{2,9},{3,8},{4,5},{5,4},{6,13},{7,12},{8,3},{9,2},{10,... | collective-permute-start | bytes 294920 | tf_op jit(solution)/shard_map/ppermute | solution.py:330
  80.2 1.9 %collective-permute-done.15.out0 = bf16[128,384]{1,0:T(8,128)(2,1)S(1)} collective-permute-done((bf16[128,384]{1,0:T(8,128)(2,1)S(1)}, bf16[128,384]{1,0:T(8,128)(2,1)S(1)}, u32[]{:S(2)}, u32[]{:S(2)}) %collective-permute-start.15) | collective-permute-done | bytes 98336 | tf_op jit(solution)/shard_map/ppermute | solution.py:330
  82.1 3.6 %collective-permute-done.16.out1 = bf16[128,384]{1,0:T(8,128)(2,1)S(1)} collective-permute-done((bf16[128,384]{1,0:T(8,128)(2,1)S(1)}, bf16[128,384]{1,0:T(8,128)(2,1)S(1)}, u32[]{:S(2)}, u32[]{:S(2)}) %collective-permute-start.16) | collective-permute-done | bytes 98336 | tf_op jit(solution)/shard_map/ppermute | solution.py:330
  85.7 3.0 %shard_map.99 = (f32[2,128,384]{2,1,0:T(8,128)S(1)}, bf16[2,128,384]{2,1,0:T(8,128)(2,1)}) custom-call(s32[2]{0:T(128)S(1)} %pad_add_fusion.place, bf16[256,384]{1,0:T(8,128)(2,1)S(1)} %collective-permute-done.13.r0, bf16[256,384]{1,0:T(8,128)(2,1)S(1)} %collective-permute-done.14.r1, bf16[128,384]{1,0:T(8,128)(2,1)S(1)} %collective-permute-done.15.out0, ...), custom_call_target="tpu_custom_call" | custom-call | flops 1000000000 | bytes 1048576 | tf_op jit(solution)/shard_map/pallas_call | solution.py:22
  88.8 0.7 shard_map.101
  (38 shorter events, 2.1 us)
Async XLA Ops:
  0.6 21.0 %collective-permute-start = (bf16[256,384]{1,0:T(8,128)(2,1)}, bf16[256,384]{1,0:T(8,128)(2,1)S(1)}, u32[]{:S(2)}, u32[]{:S(2)}) collective-permute-start(bf16[256,384]{1,0:T(8,128)(2,1)} %bitcast.13), channel_id=1, source_target_pairs={{0,1},{1,0},{2,3},{3,2},{4,5},{5,4},{6,7},{7,6},{8,9},{9,8},{10,11... | collective-permute-start | bytes 589832 | tf_op jit(solution)/shard_map/ppermute | solution.py:330
  5.2 16.4 %collective-permute-start.1 = (bf16[128,384]{1,0:T(8,128)(2,1)S(1)}, bf16[128,384]{1,0:T(8,128)(2,1)S(1)}, u32[]{:S(2)}, u32[]{:S(2)}) collective-permute-start(bf16[128,384]{1,0:T(8,128)(2,1)S(1)} %bitcast.16), channel_id=1, source_target_pairs={{1,3},{2,0},{3,5},{4,2},{5,7},{6,4},{9,11},{10,8},{11,13},{12,10},... | collective-permute-start | bytes 294920 | tf_op jit(solution)/shard_map/ppermute | solution.py:330
  6.5 15.1 %collective-permute-start.2 = (bf16[128,384]{1,0:T(8,128)(2,1)S(1)}, bf16[128,384]{1,0:T(8,128)(2,1)S(1)}, u32[]{:S(2)}, u32[]{:S(2)}) collective-permute-start(bf16[128,384]{1,0:T(8,128)(2,1)S(1)} %bitcast.17), channel_id=1, source_target_pairs={{1,2},{2,1},{3,4},{4,3},{5,6},{6,5},{9,10},{10,9},{11,12},{12,11},... | collective-permute-start | bytes 294920 | tf_op jit(solution)/shard_map/ppermute | solution.py:330
  7.2 23.1 %collective-permute-start.8 = (bf16[2,128,384]{2,1,0:T(8,128)(2,1)}, bf16[2,128,384]{2,1,0:T(8,128)(2,1)S(1)}, u32[]{:S(2)}, u32[]{:S(2)}) collective-permute-start(bf16[2,128,384]{2,1,0:T(8,128)(2,1)} %bitcast.18), channel_id=1, source_target_pairs={{0,0},{1,1},{2,8},{3,9},{4,4},{5,5},{6,12},{7,13},{8,2},{9,3},{10,... | collective-permute-start | bytes 589832 | tf_op jit(solution)/shard_map/ppermute | solution.py:330
  15.1 6.5 %copy-start.2 = (bf16[2,2,64,384]{3,2,1,0:T(8,128)(2,1)S(1)}, bf16[2,2,64,384]{3,2,1,0:T(8,128)(2,1)}, u32[]{:S(2)}) copy-start(bf16[2,2,64,384]{3,2,1,0:T(8,128)(2,1)} %param.8) | copy-start | bytes 589828
  18.4 3.1 %copy-start = (bf16[3,3,3,384,384]{4,3,2,1,0:T(8,128)(2,1)}, bf16[3,3,3,384,384]{4,3,2,1,0:T(8,128)(2,1)S(1)}, u32[]{:S(2)}) copy-start(bf16[3,3,3,384,384]{4,3,2,1,0:T(8,128)(2,1)S(1)} %shard_map.95.w_ref) | copy-start | bytes 23887876
  21.6 3.3 %copy-start.1 = (bf16[3,3,3,384,384]{4,3,2,1,0:T(8,128)(2,1)S(1)}, bf16[3,3,3,384,384]{4,3,2,1,0:T(8,128)(2,1)}, u32[]{:S(2)}) copy-start(bf16[3,3,3,384,384]{4,3,2,1,0:T(8,128)(2,1)} %copy-done) | copy-start | bytes 23887876
  28.2 24.1 %copy-start.7 = (f32[384]{0:T(512)S(1)}, f32[384]{0:T(512)}, u32[]{:S(2)}) copy-start(f32[384]{0:T(512)} %param.10) | copy-start | bytes 4612
  28.2 25.5 %copy-start.3 = (bf16[384,384]{1,0:T(8,128)(2,1)S(1)}, bf16[384,384]{1,0:T(8,128)(2,1)}, u32[]{:S(2)}) copy-start(bf16[384,384]{1,0:T(8,128)(2,1)} %wq.1) | copy-start | bytes 884740
  28.2 25.5 %copy-start.4 = (bf16[384,384]{1,0:T(8,128)(2,1)S(1)}, bf16[384,384]{1,0:T(8,128)(2,1)}, u32[]{:S(2)}) copy-start(bf16[384,384]{1,0:T(8,128)(2,1)} %wk.1) | copy-start | bytes 884740
  28.2 25.5 %copy-start.5 = (bf16[384,384]{1,0:T(8,128)(2,1)S(1)}, bf16[384,384]{1,0:T(8,128)(2,1)}, u32[]{:S(2)}) copy-start(bf16[384,384]{1,0:T(8,128)(2,1)} %wv.1) | copy-start | bytes 884740
  28.2 25.5 %copy-start.6 = (bf16[384,384]{1,0:T(8,128)(2,1)S(1)}, bf16[384,384]{1,0:T(8,128)(2,1)}, u32[]{:S(2)}) copy-start(bf16[384,384]{1,0:T(8,128)(2,1)} %wo.1) | copy-start | bytes 884740
  28.2 13.4 %collective-permute-start.3 = (bf16[256,384]{1,0:T(8,128)(2,1)S(1)}, bf16[256,384]{1,0:T(8,128)(2,1)S(1)}, u32[]{:S(2)}, u32[]{:S(2)}) collective-permute-start(bf16[256,384]{1,0:T(8,128)(2,1)S(1)} %get-tuple-element.11), channel_id=1, source_target_pairs={{0,8},{8,16},{16,24},{24,32},{32,40},{40,48},{48,56},{56,64},{64,7... | collective-permute-start | bytes 589832 | tf_op jit(solution)/shard_map/ppermute | solution.py:380
  30.3 5.4 %collective-permute-start.9 = (bf16[128,384]{1,0:T(8,128)(2,1)S(1)}, bf16[128,384]{1,0:T(8,128)(2,1)S(1)}, u32[]{:S(2)}, u32[]{:S(2)}) collective-permute-start(bf16[128,384]{1,0:T(8,128)(2,1)S(1)} %get-tuple-element.18), channel_id=1, source_target_pairs={{0,1},{1,0},{2,3},{3,2},{4,5},{5,4},{6,7},{7,6},{8,9},{9,8},{10,11... | collective-permute-start | bytes 294920 | tf_op jit(solution)/shard_map/ppermute | solution.py:330
  35.8 35.9 %slice-start = ((s8[7962624]{0:T(1024)(128)(4,1)}), s8[4194304]{0:T(1024)(128)(4,1)S(1)}, s32[]{:S(2)}) async-start(s8[7962624]{0:T(1024)(128)(4,1)} %bitcast.11), calls=%async_computation | async-start | bytes 8388608
  36.4 9.5 %collective-permute-start.10 = (bf16[256,384]{1,0:T(8,128)(2,1)S(1)}, bf16[256,384]{1,0:T(8,128)(2,1)S(1)}, u32[]{:S(2)}, u32[]{:S(2)}) collective-permute-start(bf16[256,384]{1,0:T(8,128)(2,1)S(1)} %shard_map.98.t0), channel_id=1, source_target_pairs={{0,4},{1,5},{2,6},{3,7},{4,0},{5,1},{6,2},{7,3},{8,12},{9,13},{10,... | collective-permute-start | bytes 589832 | tf_op jit(solution)/shard_map/ppermute | solution.py:330
  41.7 9.1 %collective-permute-start.4 = (bf16[256,384]{1,0:T(8,128)(2,1)S(1)}, bf16[256,384]{1,0:T(8,128)(2,1)S(1)}, u32[]{:S(2)}, u32[]{:S(2)}) collective-permute-start(bf16[256,384]{1,0:T(8,128)(2,1)S(1)} %add_convert_fusion), channel_id=1, source_target_pairs={{0,0},{1,1},{2,8},{3,9},{4,4},{5,5},{6,12},{7,13},{8,2},{9,3},{10,... | collective-permute-start | bytes 589832 | tf_op jit(solution)/shard_map/ppermute | solution.py:330
  43.7 8.6 %collective-permute-start.5 = (bf16[256,384]{1,0:T(8,128)(2,1)S(1)}, bf16[256,384]{1,0:T(8,128)(2,1)S(1)}, u32[]{:S(2)}, u32[]{:S(2)}) collective-permute-start(bf16[256,384]{1,0:T(8,128)(2,1)S(1)} %add_convert_fusion), channel_id=1, source_target_pairs={{0,4},{1,5},{2,12},{3,13},{4,0},{5,1},{6,8},{7,9},{8,6},{9,7},{10,... | collective-permute-start | bytes 589832 | tf_op jit(solution)/shard_map/ppermute | solution.py:330
  44.4 7.8 %collective-permute-start.11 = (bf16[256,384]{1,0:T(8,128)(2,1)S(1)}, bf16[256,384]{1,0:T(8,128)(2,1)S(1)}, u32[]{:S(2)}, u32[]{:S(2)}) collective-permute-start(bf16[256,384]{1,0:T(8,128)(2,1)S(1)} %shard_map.98.t0), channel_id=1, source_target_pairs={{0,8},{1,9},{2,10},{3,11},{4,12},{5,13},{6,14},{7,15},{8,0},{9,1},... | collective-permute-start | bytes 589832 | tf_op jit(solution)/shard_map/ppermute | solution.py:330
  45.8 6.4 %collective-permute-start.12 = (bf16[256,384]{1,0:T(8,128)(2,1)S(1)}, bf16[256,384]{1,0:T(8,128)(2,1)S(1)}, u32[]{:S(2)}, u32[]{:S(2)}) collective-permute-start(bf16[256,384]{1,0:T(8,128)(2,1)S(1)} %collective-permute-done.10.t2), channel_id=1, source_target_pairs={{0,8},{1,9},{2,10},{3,11},{4,12},{5,13},{6,14},{7,15},{8,0},{9,1},... | collective-permute-start | bytes 589832 | tf_op jit(solution)/shard_map/ppermute | solution.py:330
  50.9 1.4 %collective-permute-start.6 = (bf16[256,384]{1,0:T(8,128)(2,1)S(1)}, bf16[256,384]{1,0:T(8,128)(2,1)S(1)}, u32[]{:S(2)}, u32[]{:S(2)}) collective-permute-start(bf16[256,384]{1,0:T(8,128)(2,1)S(1)} %collective-permute-done.4.c0), channel_id=1, source_target_pairs={{0,8},{1,9},{2,10},{3,11},{4,12},{5,13},{6,14},{7,15},{8,0},{9,1},... | collective-permute-start | bytes 589832 | tf_op jit(solution)/shard_map/ppermute | solution.py:330
  52.2 1.4 %collective-permute-start.7 = (bf16[256,384]{1,0:T(8,128)(2,1)S(1)}, bf16[256,384]{1,0:T(8,128)(2,1)S(1)}, u32[]{:S(2)}, u32[]{:S(2)}) collective-permute-start(bf16[256,384]{1,0:T(8,128)(2,1)S(1)} %collective-permute-done.5.c2), channel_id=1, source_target_pairs={{0,8},{1,9},{2,10},{3,11},{4,12},{5,13},{6,14},{7,15},{8,0},{9,1},... | collective-permute-start | bytes 589832 | tf_op jit(solution)/shard_map/ppermute | solution.py:330
  52.3 19.4 %slice-start.1 = ((s8[7962624]{0:T(1024)(128)(4,1)}), s8[3768320]{0:T(1024)(128)(4,1)S(1)}, s32[]{:S(2)}) async-start(s8[7962624]{0:T(1024)(128)(4,1)} %bitcast.11), calls=%async_computation.1 | async-start | bytes 7536640
  62.2 7.3 %collective-permute-start.13 = (bf16[256,384]{1,0:T(8,128)(2,1)S(1)}, bf16[256,384]{1,0:T(8,128)(2,1)S(1)}, u32[]{:S(2)}, u32[]{:S(2)}) collective-permute-start(bf16[256,384]{1,0:T(8,128)(2,1)S(1)} %get-tuple-element.12), channel_id=1, source_target_pairs={{0,0},{1,1},{2,8},{3,9},{4,4},{5,5},{6,12},{7,13},{8,2},{9,3},{10,... | collective-permute-start | bytes 589832 | tf_op jit(solution)/shard_map/ppermute | solution.py:330
  64.1 7.6 %collective-permute-start.14 = (bf16[256,384]{1,0:T(8,128)(2,1)S(1)}, bf16[256,384]{1,0:T(8,128)(2,1)S(1)}, u32[]{:S(2)}, u32[]{:S(2)}) collective-permute-start(bf16[256,384]{1,0:T(8,128)(2,1)S(1)} %get-tuple-element.13), channel_id=1, source_target_pairs={{0,1},{1,0},{2,9},{3,8},{4,5},{5,4},{6,13},{7,12},{8,3},{9,2},{10,... | collective-permute-start | bytes 589832 | tf_op jit(solution)/shard_map/ppermute | solution.py:330
  74.2 14.5 %collective-permute-start.17 = (bf16[2,128,384]{2,1,0:T(8,128)(2,1)S(1)}, bf16[2,128,384]{2,1,0:T(8,128)(2,1)S(1)}, u32[]{:S(2)}, u32[]{:S(2)}) collective-permute-start(bf16[2,128,384]{2,1,0:T(8,128)(2,1)S(1)} %shard_map.100), channel_id=1, source_target_pairs={{8,0},{16,8},{24,16},{32,24},{40,32},{48,40},{56,48},{64,56},{72,6... | collective-permute-start | bytes 589832 | tf_op jit(solution)/shard_map/ppermute | solution.py:407
  76.2 5.9 %collective-permute-start.15 = (bf16[128,384]{1,0:T(8,128)(2,1)S(1)}, bf16[128,384]{1,0:T(8,128)(2,1)S(1)}, u32[]{:S(2)}, u32[]{:S(2)}) collective-permute-start(bf16[128,384]{1,0:T(8,128)(2,1)S(1)} %get-tuple-element.14), channel_id=1, source_target_pairs={{0,0},{1,1},{2,8},{3,9},{4,4},{5,5},{6,12},{7,13},{8,2},{9,3},{10,... | collective-permute-start | bytes 294920 | tf_op jit(solution)/shard_map/ppermute | solution.py:330
  79.2 6.5 %collective-permute-start.16 = (bf16[128,384]{1,0:T(8,128)(2,1)S(1)}, bf16[128,384]{1,0:T(8,128)(2,1)S(1)}, u32[]{:S(2)}, u32[]{:S(2)}) collective-permute-start(bf16[128,384]{1,0:T(8,128)(2,1)S(1)} %get-tuple-element.15), channel_id=1, source_target_pairs={{0,1},{1,0},{2,9},{3,8},{4,5},{5,4},{6,13},{7,12},{8,3},{9,2},{10,... | collective-permute-start | bytes 294920 | tf_op jit(solution)/shard_map/ppermute | solution.py:330

commit v4 on v3

--- a/solution.py
+++ b/solution.py
@@ -1,5 +1,3 @@
-import functools
-
 import jax
 import jax.numpy as jnp
 from jax import lax
@@ -12,7 +10,8 @@
 BF16 = jnp.bfloat16
 MIB = 1024 * 1024
 LOG2E = 1.4426950408889634
-LOAD = 42 * MIB
+LOAD = 44 * MIB
+NEXT = 42 * MIB
 VM = pl.BlockSpec(memory_space=pltpu.VMEM)
 SM = pl.BlockSpec(memory_space=pltpu.SMEM)
 HBM = pl.BlockSpec(memory_space=pltpu.HBM)
@@ -43,14 +42,15 @@
 
 
 def load_kernel(w_hbm, w_out, sem):
-    copy = pltpu.make_async_copy(w_hbm, w_out, sem)
+    copy = pltpu.make_async_copy(w_hbm.at[0:2], w_out, sem)
     copy.start()
     copy.wait()
 
 
 def load(weight):
     return call(
-        load_kernel, (weight,), [HBM], [(weight.shape, BF16)], [pltpu.SemaphoreType.DMA], LOAD
+        load_kernel, (weight,), [HBM], [((2,) + weight.shape[1:], weight.dtype)],
+        [pltpu.SemaphoreType.DMA], LOAD,
     )[0]
 
 
@@ -90,22 +90,18 @@
         )
 
 
-def conv_steps(taps, w_ref, main, side, out, src, dst, transposed):
-    chans = w_ref.shape[-1]
-
-    def times(lhs, a, b):
-        if not transposed:
-            return mm(lhs, w_ref[a, b].reshape(3 * chans, chans))
-        return mm_t(lhs, jnp.concatenate([w_ref[a, b, c] for c in range(3)], axis=1))
+def conv_steps(taps, w_main, w_side, out, src, dst):
+    def times(lhs, w_ref, b):
+        return mm_t(lhs, jnp.concatenate([w_ref[b, c] for c in range(3)], axis=1))
 
     both = extra = None
     for b in range(3):
-        row = (2 - b) if transposed else b
+        row = 2 - b
         lhs = [taps[f, row : row + 2] for f in range(2)]
         lhs = [v.reshape(v.shape[0] * v.shape[1], v.shape[2]) for v in lhs]
-        term = times(jnp.concatenate(lhs, axis=0), main, b)
+        term = times(jnp.concatenate(lhs, axis=0), w_main, b)
         both = term if both is None else both + term
-        term = times(lhs[src], side, b)
+        term = times(lhs[src], w_side, b)
         extra = term if extra is None else extra + term
     half = both.shape[0] // 2
     for f in range(2):
@@ -118,16 +114,18 @@
     return piece.reshape(piece.shape[0] * piece.shape[1], piece.shape[2])
 
 
-def frame_conv(taps, w_ref, frame, a):
+def frame_conv(taps, w_ref, frame):
     chans = w_ref.shape[-1]
     total = None
     for b in range(3):
-        term = mm(frame_taps(taps, frame, b), w_ref[a, b].reshape(3 * chans, chans))
+        term = mm(frame_taps(taps, frame, b), w_ref[b].reshape(3 * chans, chans))
         total = term if total is None else total + term
     return total
 
 
-def next_kernel(place, mine, packet, far_same, far_other, w_ref, out, taps, acc):
+def next_kernel(place, mine, packet, far_same, far_other, w_ref, w_hbm, out, taps, w_last, acc, sem):
+    copy = pltpu.make_async_copy(w_hbm.at[2], w_last, sem)
+    copy.start()
     x = place[0]
     flip = x == 1
     width = taps.shape[2]
@@ -142,34 +140,39 @@
             (0, top), (1, jnp.where(flip, b, a)), (3, jnp.where(flip, a, b)), (5, bottom)
         ):
             fill(taps, f, row, rows.reshape(-1, width, chans), width, False)
-    acc[...] = frame_conv(taps, w_ref, x, 0)
+    acc[...] = frame_conv(taps, w_ref.at[0], x)
 
     @pl.when(x == 0)
     def _():
-        acc[...] += frame_conv(taps, w_ref, 1, 1)
+        acc[...] += frame_conv(taps, w_ref.at[1], 1)
 
     out[...] = acc[...].astype(out.dtype)
-
-
-def own_kernel(place, taps, w_ref, out):
+    copy.wait()
+
+
+def own_kernel(place, taps, w_ref, w_last, out):
     x = place[0]
-    out[...] = frame_conv(taps, w_ref, x, 2)
+    out[...] = frame_conv(taps, w_last, x)
 
     @pl.when(x == 1)
     def _():
-        out[...] += frame_conv(taps, w_ref, 0, 1)
-
-
-def backward_kernel(main, side, src, dst, place, r0, r1, w_ref, out, taps):
-    width, chans = taps.shape[2], w_ref.shape[-1]
+        out[...] += frame_conv(taps, w_ref.at[1], 0)
+
+
+def fill_slab(place, taps, r0, r1):
+    width, chans = taps.shape[2], r0.shape[-1]
     swapped = place[0] == 1
     for f, (a, b) in enumerate(((r0, r1), (r1, r0))):
         rows = jnp.where(swapped, b[...], a[...])
         fill(taps, f, 0, rows.reshape(4, width, chans), width, True)
-    conv_steps(taps, w_ref, main, side, out, src, dst, True)
-
-
-def last_kernel(place, r0, r1, out0, out1, w_ref, out, block_out, taps, sems):
+
+
+def grad_last_kernel(place, r0, r1, w_ref, out, taps):
+    fill_slab(place, taps, r0, r1)
+    conv_steps(taps, w_ref.at[0], w_ref.at[1], out, 0, 1)
+
+
+def grad_own_kernel(place, r0, r1, out0, out1, w_ref, w_last, out, block_out, taps, sems):
     x = place[0]
     copies = [
         pltpu.make_async_copy(out0, block_out.at[x], sems.at[0]),
@@ -177,18 +180,10 @@
     ]
     for copy in copies:
         copy.start()
-    backward_kernel(2, 1, 1, 0, place, r0, r1, w_ref, out, taps)
+    fill_slab(place, taps, r0, r1)
+    conv_steps(taps, w_last, w_ref.at[1], out, 1, 0)
     for copy in copies:
         copy.wait()
-
-
-def conv_call(kernel, place, operands, weight, width, dtype):
-    chans = weight.shape[-1]
-    return call(
-        kernel, (place, *operands, weight), [SM] + [VM] * (len(operands) + 1),
-        [((2, 2 * width, chans), dtype)], [pltpu.VMEM((2, 4, width, 3 * chans), BF16)],
-        24 * MIB, 2 * 9 * 3 * 128 * chans * chans,
-    )[0]
 
 
 def norm_parts(conv, gain):
@@ -231,12 +226,17 @@
                 slot = (4 * (quarter - q) + j + 17) % 16
                 dst[pl.ds(pl.multiple_of(slot * line, line), line)] = ref[j * line : (j + 1) * line]
 
-    for at, n in CHUNKS:
+    def activation(at, n):
+        _, _, normed = norm_parts(conv_s[at : at + n], gain)
+        return (normed / (1.0 + jnp.exp(-normed))).astype(BF16)
+
+    coming = activation(*CHUNKS[0])
+    act_s[...] = coming
+    for i, (at, n) in enumerate(CHUNKS):
         rows = slice(at, at + n)
-        _, _, normed = norm_parts(conv_s[rows], gain)
-        act = (normed / (1.0 + jnp.exp(-normed))).astype(BF16)
-        if at == 0:
-            act_s[...] = act
+        act = coming
+        if i + 1 < len(CHUNKS):
+            coming = activation(*CHUNKS[i + 1])
         q_s[rows] = mm(act, wq[...]).astype(BF16)
         k_s[rows] = mm(act, wk[...]).astype(BF16)
         v_s[rows] = mm(act, wv[...]).astype(BF16)
@@ -371,20 +371,22 @@
     weight = load(conv_weight)
     cot_same = lax.dynamic_index_in_dim(cot_b, x, 0, keepdims=False)
     cot_other = lax.dynamic_index_in_dim(cot_b, 1 - x, 0, keepdims=False)
+    cot_other = send(cot_other, runs, across)
     quad = (2 * block, chans)
-    for_next, taps = call(
-        next_kernel, (place, mine, packet, far_same, far_other, weight), [SM] + [VM] * 5,
-        [(quad, BF16), ((2, 6, width, 3 * chans), BF16)], [pltpu.VMEM(quad, F32)],
-        24 * MIB, 10**9,
+    for_next, taps, w_last = call(
+        next_kernel, (place, mine, packet, far_same, far_other, weight, conv_weight),
+        [SM] + [VM] * 5 + [HBM],
+        [(quad, BF16), ((2, 6, width, 3 * chans), BF16), (conv_weight.shape[1:], BF16)],
+        [pltpu.VMEM(quad, F32), pltpu.SemaphoreType.DMA],
+        NEXT, 10**9,
     )
     cached = lax.ppermute(for_next, "tm", [(i, i + 1) for i in range(runs - 1)])
-    cot_other = send(cot_other, runs, across)
+    cot_b = join(place, cot_same, cot_other)
+    cot_c = send(cot_b, runs, lambda c, y, x: (c, y ^ 2, x))
     own = call(
-        own_kernel, (place, taps, weight), [SM, VM, VM], [(quad, F32)], [],
+        own_kernel, (place, taps, weight, w_last), [SM, VM, VM, VM], [(quad, F32)], [],
         24 * MIB, 10**9,
     )[0]
-    cot_b = join(place, cot_same, cot_other)
-    cot_c = send(cot_b, runs, lambda c, y, x: (c, y ^ 2, x))
     conv = (own + cached.astype(F32)).astype(BF16)
     conv_c = send(conv, runs, home(1, 0))
     conv_b = send(conv, runs, home(0, 0))
@@ -398,15 +400,14 @@
     out1 = send(out1, runs, home(0, 1))
     out0 = send(out0, runs, home(0, 0))
 
-    def backward(main, side, src, dst, dtype):
-        kernel = functools.partial(backward_kernel, main, side, src, dst)
-        return conv_call(kernel, place, slab, weight, width, dtype)
-
-    slab = (grad0, grad1)
-    for_last = backward(0, 1, 0, 1, BF16)
+    for_last = call(
+        grad_last_kernel, (place, grad0, grad1, weight), [SM, VM, VM, VM],
+        [((2, block, chans), BF16)], [pltpu.VMEM((2, 4, width, 3 * chans), BF16)],
+        24 * MIB, 10**9,
+    )[0]
     handed = lax.ppermute(for_last, "tm", [(i + 1, i) for i in range(runs - 1)])
     own_grad, block_out = call(
-        last_kernel, (place, grad0, grad1, out0, out1, weight), [SM] + [VM] * 5,
+        grad_own_kernel, (place, grad0, grad1, out0, out1, weight, w_last), [SM] + [VM] * 6,
         [((2, block, chans), F32), ((2, block, chans), BF16)],
         [pltpu.VMEM((2, 4, width, 3 * chans), BF16), pltpu.SemaphoreType.DMA((2,))],
         24 * MIB, 10**9, outs=(VM, HBM),

time: 90 us -> 87 us (0.967)
  the two profiles are of different devices: /device:TPU:1 before, /device:TPU:6 now
where the time goes in v4:
time: 87 us; the launch traced here: 85.3 us
  starting transfers between devices  40.5 us (47%)
  Pallas kernels  22.9 us (26%)
  waiting for transfers between devices  14.9 us (17%)
  local copies, waits for them, and re-layouts  5.83 us (7%)
  between operations  1.01 us (1%)
    ppermute x16, starting transfers between devices, send(): return lax.ppermute(value, ('tm', 'rows'), pairs)  27.9 us
    ppermute x16, waiting for transfers between devices, send(): return lax.ppermute(value, ('tm', 'rows'), pairs)  14.9 us
    pallas_call x7, Pallas kernels, call(): pl.pallas_call(kernel, in_specs=specs, out_specs=list(outs) if isinstance...  14.4 us
    ppermute x1, starting transfers between devices, local(): handed = lax.ppermute(for_last, 'tm', [(i + 1, i) for i in range(runs - 1)])  8.66 us
    pallas_call x1, Pallas kernels, attention(): pl.pallas_call(attention_kernel, in_specs=[SM] + [VM] * (len(convs) + len...  8.46 us
    unnamed x16, local copies, waits for them, and re-layouts  4.86 us
    ppermute x1, starting transfers between devices, local(): cached = lax.ppermute(for_next, 'tm', [(i, i + 1) for i in range(runs - 1)])  3.97 us
  transfers between devices with their start and end apart: 18, of which 6 were waited for; matrix products, arithmetic and copies ran while one was open for 1% of the time, Pallas kernels for 13%

profile of v4, /device:TPU:6, one launch (start us, length us, event | category | flops | bytes accessed | tf_op | source)
XLA Modules:
  0.0 85.3 jit_solution(5917393348580376148)
XLA Ops:
  0.6 1.5 %collective-permute-start = (bf16[256,384]{1,0:T(8,128)(2,1)}, bf16[256,384]{1,0:T(8,128)(2,1)S(1)}, u32[]{:S(2)}, u32[]{:S(2)}) collective-permute-start(bf16[256,384]{1,0:T(8,128)(2,1)} %bitcast.11), channel_id=1, source_target_pairs={{0,1},{1,0},{2,3},{3,2},{4,5},{5,4},{6,7},{7,6},{8,9},{9,8},{10,11... | collective-permute-start | bytes 589832 | tf_op jit(solution)/shard_map/ppermute | solution.py:330
  2.1 0.9 %constant_dynamic-slice_fusion = bf16[2,1,64,384]{3,2,1,0:T(8,128)(2,1)S(1)} fusion(bf16[2,2,64,384]{3,2,1,0:T(8,128)(2,1)} %param.8, s32[]{:T(128)S(6)} %select_n.27), kind=kLoop, calls=%fused_computation.3 | loop fusion | bytes 196612 | tf_op jit(solution)/shard_map/jit(dynamic_index_in_dim)/dynamic_slice | solution.py:365
  3.1 3.5 %collective-permute-start.1 = (bf16[128,384]{1,0:T(8,128)(2,1)S(1)}, bf16[128,384]{1,0:T(8,128)(2,1)S(1)}, u32[]{:S(2)}, u32[]{:S(2)}) collective-permute-start(bf16[128,384]{1,0:T(8,128)(2,1)S(1)} %bitcast.14), channel_id=1, source_target_pairs={{1,3},{2,0},{3,5},{4,2},{5,7},{6,4},{9,11},{10,8},{11,13},{12,10},... | collective-permute-start | bytes 294920 | tf_op jit(solution)/shard_map/ppermute | solution.py:330
  6.6 3.9 %collective-permute-start.2 = (bf16[128,384]{1,0:T(8,128)(2,1)S(1)}, bf16[128,384]{1,0:T(8,128)(2,1)S(1)}, u32[]{:S(2)}, u32[]{:S(2)}) collective-permute-start(bf16[128,384]{1,0:T(8,128)(2,1)S(1)} %bitcast.15), channel_id=1, source_target_pairs={{1,2},{2,1},{3,4},{4,3},{5,6},{6,5},{9,10},{10,9},{11,12},{12,11},... | collective-permute-start | bytes 294920 | tf_op jit(solution)/shard_map/ppermute | solution.py:330
  10.5 1.6 %collective-permute-start.8 = (bf16[2,128,384]{2,1,0:T(8,128)(2,1)}, bf16[2,128,384]{2,1,0:T(8,128)(2,1)S(1)}, u32[]{:S(2)}, u32[]{:S(2)}) collective-permute-start(bf16[2,128,384]{2,1,0:T(8,128)(2,1)} %bitcast.16), channel_id=1, source_target_pairs={{0,0},{1,1},{2,8},{3,9},{4,4},{5,5},{6,12},{7,13},{8,2},{9,3},{10,... | collective-permute-start | bytes 589832 | tf_op jit(solution)/shard_map/ppermute | solution.py:330
  12.1 2.6 %shard_map.95.w_ref = bf16[2,3,3,384,384]{4,3,2,1,0:T(8,128)(2,1)S(1)} custom-call(bf16[3,3,3,384,384]{4,3,2,1,0:T(8,128)(2,1)} %w_hbm.3), custom_call_target="tpu_custom_call" | custom-call | bytes 1048576 | tf_op jit(solution)/shard_map/pallas_call | solution.py:21
  14.6 2.3 %copy-done = bf16[2,3,3,384,384]{4,3,2,1,0:T(8,128)(2,1)} copy-done((bf16[2,3,3,384,384]{4,3,2,1,0:T(8,128)(2,1)}, bf16[2,3,3,384,384]{4,3,2,1,0:T(8,128)(2,1)S(1)}, u32[]{:S(2)}) %copy-start) | copy-done | bytes 5308440
  17.1 2.5 %copy-done.1 = bf16[2,3,3,384,384]{4,3,2,1,0:T(8,128)(2,1)S(1)} copy-done((bf16[2,3,3,384,384]{4,3,2,1,0:T(8,128)(2,1)S(1)}, bf16[2,3,3,384,384]{4,3,2,1,0:T(8,128)(2,1)}, u32[]{:S(2)}) %copy-start.1) | copy-done | bytes 5308440
  19.6 2.3 %shard_map.96 = (bf16[256,384]{1,0:T(8,128)(2,1)S(1)}, bf16[2,6,64,1152]{3,2,1,0:T(8,128)(2,1)S(1)}, bf16[3,3,384,384]{3,2,1,0:T(8,128)(2,1)S(1)}) custom-call(s32[2]{0:T(128)S(1)} %pad_add_fusion.place, bf16[256,384]{1,0:T(8,128)(2,1)S(1)} %bitcast.12, bf16[256,384]{1,0:T(8,128)(2,1)S(1)} %collective-permute-done.packet, ...), custom_call_target="tpu_custom_call" | custom-call | flops 1000000000 | bytes 1048576 | tf_op jit(solution)/shard_map/pallas_call | solution.py:21
  21.9 4.0 %collective-permute-start.3 = (bf16[256,384]{1,0:T(8,128)(2,1)S(1)}, bf16[256,384]{1,0:T(8,128)(2,1)S(1)}, u32[]{:S(2)}, u32[]{:S(2)}) collective-permute-start(bf16[256,384]{1,0:T(8,128)(2,1)S(1)} %get-tuple-element.13), channel_id=1, source_target_pairs={{0,8},{8,16},{16,24},{24,32},{32,40},{40,48},{48,56},{56,64},{64,7... | collective-permute-start | bytes 589832 | tf_op jit(solution)/shard_map/ppermute | solution.py:383
  25.9 2.5 %collective-permute-start.9 = (bf16[128,384]{1,0:T(8,128)(2,1)S(1)}, bf16[128,384]{1,0:T(8,128)(2,1)S(1)}, u32[]{:S(2)}, u32[]{:S(2)}) collective-permute-start(bf16[128,384]{1,0:T(8,128)(2,1)S(1)} %get-tuple-element.20), channel_id=1, source_target_pairs={{0,1},{1,0},{2,3},{3,2},{4,5},{5,4},{6,7},{7,6},{8,9},{9,8},{10,11... | collective-permute-start | bytes 294920 | tf_op jit(solution)/shard_map/ppermute | solution.py:330
  28.4 2.8 %shard_map.97 = f32[256,384]{1,0:T(8,128)S(1)} custom-call(s32[2]{0:T(128)S(1)} %pad_add_fusion.place, bf16[2,6,64,1152]{3,2,1,0:T(8,128)(2,1)S(1)} %get-tuple-element.11.taps, bf16[2,3,3,384,384]{4,3,2,1,0:T(8,128)(2,1)S(1)} %copy-done.1, bf16[3,3,384,384]{3,2,1,0:T(8,128)(2,1)S(1)} %get-tuple-element.12.w_last), custom_call_target="tpu_custom_call" | custom-call | flops 1000000000 | bytes 1048576 | tf_op jit(solution)/shard_map/pallas_call | solution.py:21
  31.2 1.0 %collective-permute-done.9.other = bf16[128,384]{1,0:T(8,128)(2,1)S(1)} collective-permute-done((bf16[128,384]{1,0:T(8,128)(2,1)S(1)}, bf16[128,384]{1,0:T(8,128)(2,1)S(1)}, u32[]{:S(2)}, u32[]{:S(2)}) %collective-permute-start.9) | collective-permute-done | bytes 98336 | tf_op jit(solution)/shard_map/ppermute | solution.py:330
  32.8 2.3 %collective-permute-start.10 = (bf16[256,384]{1,0:T(8,128)(2,1)S(1)}, bf16[256,384]{1,0:T(8,128)(2,1)S(1)}, u32[]{:S(2)}, u32[]{:S(2)}) collective-permute-start(bf16[256,384]{1,0:T(8,128)(2,1)S(1)} %shard_map.98.t0), channel_id=1, source_target_pairs={{0,4},{1,5},{2,6},{3,7},{4,0},{5,1},{6,2},{7,3},{8,12},{9,13},{10,... | collective-permute-start | bytes 589832 | tf_op jit(solution)/shard_map/ppermute | solution.py:330
  35.2 0.7 collective-permute-start.4
  35.9 1.4 %collective-permute-start.5 = (bf16[256,384]{1,0:T(8,128)(2,1)S(1)}, bf16[256,384]{1,0:T(8,128)(2,1)S(1)}, u32[]{:S(2)}, u32[]{:S(2)}) collective-permute-start(bf16[256,384]{1,0:T(8,128)(2,1)S(1)} %add_convert_fusion), channel_id=1, source_target_pairs={{0,4},{1,5},{2,12},{3,13},{4,0},{5,1},{6,8},{7,9},{8,6},{9,7},{10,... | collective-permute-start | bytes 589832 | tf_op jit(solution)/shard_map/ppermute | solution.py:330
  37.2 0.8 collective-permute-start.11
  38.1 3.7 %collective-permute-done.10.t2 = bf16[256,384]{1,0:T(8,128)(2,1)S(1)} collective-permute-done((bf16[256,384]{1,0:T(8,128)(2,1)S(1)}, bf16[256,384]{1,0:T(8,128)(2,1)S(1)}, u32[]{:S(2)}, u32[]{:S(2)}) %collective-permute-start.10) | collective-permute-done | bytes 196640 | tf_op jit(solution)/shard_map/ppermute | solution.py:330
  41.8 2.6 %collective-permute-start.6 = (bf16[256,384]{1,0:T(8,128)(2,1)S(1)}, bf16[256,384]{1,0:T(8,128)(2,1)S(1)}, u32[]{:S(2)}, u32[]{:S(2)}) collective-permute-start(bf16[256,384]{1,0:T(8,128)(2,1)S(1)} %collective-permute-done.4.c0), channel_id=1, source_target_pairs={{0,8},{1,9},{2,10},{3,11},{4,12},{5,13},{6,14},{7,15},{8,0},{9,1},... | collective-permute-start | bytes 589832 | tf_op jit(solution)/shard_map/ppermute | solution.py:330
  44.4 0.7 collective-permute-done.5.c2
  45.1 0.8 collective-permute-start.7
  45.9 1.0 %collective-permute-done.7.c3 = bf16[256,384]{1,0:T(8,128)(2,1)S(1)} collective-permute-done((bf16[256,384]{1,0:T(8,128)(2,1)S(1)}, bf16[256,384]{1,0:T(8,128)(2,1)S(1)}, u32[]{:S(2)}, u32[]{:S(2)}) %collective-permute-start.7) | collective-permute-done | bytes 196640 | tf_op jit(solution)/shard_map/ppermute | solution.py:330
  47.0 8.5 %attention.1 = (bf16[128,384]{1,0:T(8,128)(2,1)S(1)}, bf16[128,384]{1,0:T(8,128)(2,1)S(1)}, bf16[256,384]{1,0:T(8,128)(2,1)S(1)}, bf16[256,384]{1,0:T(8,128)(2,1)S(1)}) custom-call(s32[2]{0:T(128)S(1)} %pad_add_fusion.place, bf16[256,384]{1,0:T(8,128)(2,1)S(1)} %collective-permute-done.4.c0, bf16[256,384]{1,0:T(8,128)(2,1)S(1)} %collective-permute-done.5.c2, ...), custom_call_target="tpu_custom_call" | custom-call | flops 4000000000 | bytes 4000000 | tf_op jit(solution)/shard_map/attention/pallas_call | solution.py:301
  55.4 0.7 collective-permute-start.13
  56.1 2.2 %collective-permute-start.14 = (bf16[256,384]{1,0:T(8,128)(2,1)S(1)}, bf16[256,384]{1,0:T(8,128)(2,1)S(1)}, u32[]{:S(2)}, u32[]{:S(2)}) collective-permute-start(bf16[256,384]{1,0:T(8,128)(2,1)S(1)} %get-tuple-element.15), channel_id=1, source_target_pairs={{0,1},{1,0},{2,9},{3,8},{4,5},{5,4},{6,13},{7,12},{8,3},{9,2},{10,... | collective-permute-start | bytes 589832 | tf_op jit(solution)/shard_map/ppermute | solution.py:330
  58.3 5.0 %collective-permute-done.14.r1 = bf16[256,384]{1,0:T(8,128)(2,1)S(1)} collective-permute-done((bf16[256,384]{1,0:T(8,128)(2,1)S(1)}, bf16[256,384]{1,0:T(8,128)(2,1)S(1)}, u32[]{:S(2)}, u32[]{:S(2)}) %collective-permute-start.14) | collective-permute-done | bytes 196640 | tf_op jit(solution)/shard_map/ppermute | solution.py:330
  63.4 2.5 %shard_map.100 = bf16[2,128,384]{2,1,0:T(8,128)(2,1)S(1)} custom-call(s32[2]{0:T(128)S(1)} %pad_add_fusion.place, bf16[256,384]{1,0:T(8,128)(2,1)S(1)} %collective-permute-done.13.r0, bf16[256,384]{1,0:T(8,128)(2,1)S(1)} %collective-permute-done.14.r1, bf16[2,3,3,384,384]{4,3,2,1,0:T(8,128)(2,1)S(1)} %copy-done.1), custom_call_target="tpu_custom_call" | custom-call | flops 1000000000 | bytes 1048576 | tf_op jit(solution)/shard_map/pallas_call | solution.py:21
  65.8 8.7 %collective-permute-start.17 = (bf16[2,128,384]{2,1,0:T(8,128)(2,1)S(1)}, bf16[2,128,384]{2,1,0:T(8,128)(2,1)S(1)}, u32[]{:S(2)}, u32[]{:S(2)}) collective-permute-start(bf16[2,128,384]{2,1,0:T(8,128)(2,1)S(1)} %shard_map.100), channel_id=1, source_target_pairs={{8,0},{16,8},{24,16},{32,24},{40,32},{48,40},{56,48},{64,56},{72,6... | collective-permute-start | bytes 589832 | tf_op jit(solution)/shard_map/ppermute | solution.py:408
  75.2 2.8 %collective-permute-start.16 = (bf16[128,384]{1,0:T(8,128)(2,1)S(1)}, bf16[128,384]{1,0:T(8,128)(2,1)S(1)}, u32[]{:S(2)}, u32[]{:S(2)}) collective-permute-start(bf16[128,384]{1,0:T(8,128)(2,1)S(1)} %get-tuple-element.17), channel_id=1, source_target_pairs={{0,1},{1,0},{2,9},{3,8},{4,5},{5,4},{6,13},{7,12},{8,3},{9,2},{10,... | collective-permute-start | bytes 294920 | tf_op jit(solution)/shard_map/ppermute | solution.py:330
  78.0 3.4 %collective-permute-done.16.out1 = bf16[128,384]{1,0:T(8,128)(2,1)S(1)} collective-permute-done((bf16[128,384]{1,0:T(8,128)(2,1)S(1)}, bf16[128,384]{1,0:T(8,128)(2,1)S(1)}, u32[]{:S(2)}, u32[]{:S(2)}) %collective-permute-start.16) | collective-permute-done | bytes 98336 | tf_op jit(solution)/shard_map/ppermute | solution.py:330
  81.4 3.0 %shard_map.99 = (f32[2,128,384]{2,1,0:T(8,128)S(1)}, bf16[2,128,384]{2,1,0:T(8,128)(2,1)}) custom-call(s32[2]{0:T(128)S(1)} %pad_add_fusion.place, bf16[256,384]{1,0:T(8,128)(2,1)S(1)} %collective-permute-done.13.r0, bf16[256,384]{1,0:T(8,128)(2,1)S(1)} %collective-permute-done.14.r1, bf16[128,384]{1,0:T(8,128)(2,1)S(1)} %collective-permute-done.15.out0, ...), custom_call_target="tpu_custom_call" | custom-call | flops 1000000000 | bytes 1048576 | tf_op jit(solution)/shard_map/pallas_call | solution.py:21
  84.4 0.7 shard_map.101
  (33 shorter events, 1.4 us)
Async XLA Ops:
  0.6 16.4 %collective-permute-start = (bf16[256,384]{1,0:T(8,128)(2,1)}, bf16[256,384]{1,0:T(8,128)(2,1)S(1)}, u32[]{:S(2)}, u32[]{:S(2)}) collective-permute-start(bf16[256,384]{1,0:T(8,128)(2,1)} %bitcast.11), channel_id=1, source_target_pairs={{0,1},{1,0},{2,3},{3,2},{4,5},{5,4},{6,7},{7,6},{8,9},{9,8},{10,11... | collective-permute-start | bytes 589832 | tf_op jit(solution)/shard_map/ppermute | solution.py:330
  3.1 14.0 %collective-permute-start.1 = (bf16[128,384]{1,0:T(8,128)(2,1)S(1)}, bf16[128,384]{1,0:T(8,128)(2,1)S(1)}, u32[]{:S(2)}, u32[]{:S(2)}) collective-permute-start(bf16[128,384]{1,0:T(8,128)(2,1)S(1)} %bitcast.14), channel_id=1, source_target_pairs={{1,3},{2,0},{3,5},{4,2},{5,7},{6,4},{9,11},{10,8},{11,13},{12,10},... | collective-permute-start | bytes 294920 | tf_op jit(solution)/shard_map/ppermute | solution.py:330
  6.6 10.5 %collective-permute-start.2 = (bf16[128,384]{1,0:T(8,128)(2,1)S(1)}, bf16[128,384]{1,0:T(8,128)(2,1)S(1)}, u32[]{:S(2)}, u32[]{:S(2)}) collective-permute-start(bf16[128,384]{1,0:T(8,128)(2,1)S(1)} %bitcast.15), channel_id=1, source_target_pairs={{1,2},{2,1},{3,4},{4,3},{5,6},{6,5},{9,10},{10,9},{11,12},{12,11},... | collective-permute-start | bytes 294920 | tf_op jit(solution)/shard_map/ppermute | solution.py:330
  10.5 15.4 %collective-permute-start.8 = (bf16[2,128,384]{2,1,0:T(8,128)(2,1)}, bf16[2,128,384]{2,1,0:T(8,128)(2,1)S(1)}, u32[]{:S(2)}, u32[]{:S(2)}) collective-permute-start(bf16[2,128,384]{2,1,0:T(8,128)(2,1)} %bitcast.16), channel_id=1, source_target_pairs={{0,0},{1,1},{2,8},{3,9},{4,4},{5,5},{6,12},{7,13},{8,2},{9,3},{10,... | collective-permute-start | bytes 589832 | tf_op jit(solution)/shard_map/ppermute | solution.py:330
  12.1 5.0 %copy-start.2 = (bf16[2,2,64,384]{3,2,1,0:T(8,128)(2,1)S(1)}, bf16[2,2,64,384]{3,2,1,0:T(8,128)(2,1)}, u32[]{:S(2)}) copy-start(bf16[2,2,64,384]{3,2,1,0:T(8,128)(2,1)} %param.8) | copy-start | bytes 589828
  14.6 2.4 %copy-start = (bf16[2,3,3,384,384]{4,3,2,1,0:T(8,128)(2,1)}, bf16[2,3,3,384,384]{4,3,2,1,0:T(8,128)(2,1)S(1)}, u32[]{:S(2)}) copy-start(bf16[2,3,3,384,384]{4,3,2,1,0:T(8,128)(2,1)S(1)} %shard_map.95.w_ref) | copy-start | bytes 15925252
  17.1 2.5 %copy-start.1 = (bf16[2,3,3,384,384]{4,3,2,1,0:T(8,128)(2,1)S(1)}, bf16[2,3,3,384,384]{4,3,2,1,0:T(8,128)(2,1)}, u32[]{:S(2)}) copy-start(bf16[2,3,3,384,384]{4,3,2,1,0:T(8,128)(2,1)} %copy-done) | copy-start | bytes 15925252
  21.9 13.2 %collective-permute-start.3 = (bf16[256,384]{1,0:T(8,128)(2,1)S(1)}, bf16[256,384]{1,0:T(8,128)(2,1)S(1)}, u32[]{:S(2)}, u32[]{:S(2)}) collective-permute-start(bf16[256,384]{1,0:T(8,128)(2,1)S(1)} %get-tuple-element.13), channel_id=1, source_target_pairs={{0,8},{8,16},{16,24},{24,32},{32,40},{40,48},{48,56},{56,64},{64,7... | collective-permute-start | bytes 589832 | tf_op jit(solution)/shard_map/ppermute | solution.py:383
  25.9 6.3 %collective-permute-start.9 = (bf16[128,384]{1,0:T(8,128)(2,1)S(1)}, bf16[128,384]{1,0:T(8,128)(2,1)S(1)}, u32[]{:S(2)}, u32[]{:S(2)}) collective-permute-start(bf16[128,384]{1,0:T(8,128)(2,1)S(1)} %get-tuple-element.20), channel_id=1, source_target_pairs={{0,1},{1,0},{2,3},{3,2},{4,5},{5,4},{6,7},{7,6},{8,9},{9,8},{10,11... | collective-permute-start | bytes 294920 | tf_op jit(solution)/shard_map/ppermute | solution.py:330
  28.4 17.5 %copy-start.7 = (f32[384]{0:T(512)S(1)}, f32[384]{0:T(512)}, u32[]{:S(2)}) copy-start(f32[384]{0:T(512)} %param.10) | copy-start | bytes 4612
  28.4 18.6 %copy-start.3 = (bf16[384,384]{1,0:T(8,128)(2,1)S(1)}, bf16[384,384]{1,0:T(8,128)(2,1)}, u32[]{:S(2)}) copy-start(bf16[384,384]{1,0:T(8,128)(2,1)} %wq.1) | copy-start | bytes 884740
  28.4 18.6 %copy-start.4 = (bf16[384,384]{1,0:T(8,128)(2,1)S(1)}, bf16[384,384]{1,0:T(8,128)(2,1)}, u32[]{:S(2)}) copy-start(bf16[384,384]{1,0:T(8,128)(2,1)} %wk.1) | copy-start | bytes 884740
  28.4 18.6 %copy-start.5 = (bf16[384,384]{1,0:T(8,128)(2,1)S(1)}, bf16[384,384]{1,0:T(8,128)(2,1)}, u32[]{:S(2)}) copy-start(bf16[384,384]{1,0:T(8,128)(2,1)} %wv.1) | copy-start | bytes 884740
  28.4 18.6 %copy-start.6 = (bf16[384,384]{1,0:T(8,128)(2,1)S(1)}, bf16[384,384]{1,0:T(8,128)(2,1)}, u32[]{:S(2)}) copy-start(bf16[384,384]{1,0:T(8,128)(2,1)} %wo.1) | copy-start | bytes 884740
  32.8 9.0 %collective-permute-start.10 = (bf16[256,384]{1,0:T(8,128)(2,1)S(1)}, bf16[256,384]{1,0:T(8,128)(2,1)S(1)}, u32[]{:S(2)}, u32[]{:S(2)}) collective-permute-start(bf16[256,384]{1,0:T(8,128)(2,1)S(1)} %shard_map.98.t0), channel_id=1, source_target_pairs={{0,4},{1,5},{2,6},{3,7},{4,0},{5,1},{6,2},{7,3},{8,12},{9,13},{10,... | collective-permute-start | bytes 589832 | tf_op jit(solution)/shard_map/ppermute | solution.py:330
  35.2 6.6 %collective-permute-start.4 = (bf16[256,384]{1,0:T(8,128)(2,1)S(1)}, bf16[256,384]{1,0:T(8,128)(2,1)S(1)}, u32[]{:S(2)}, u32[]{:S(2)}) collective-permute-start(bf16[256,384]{1,0:T(8,128)(2,1)S(1)} %add_convert_fusion), channel_id=1, source_target_pairs={{0,0},{1,1},{2,8},{3,9},{4,4},{5,5},{6,12},{7,13},{8,2},{9,3},{10,... | collective-permute-start | bytes 589832 | tf_op jit(solution)/shard_map/ppermute | solution.py:330
  35.9 9.2 %collective-permute-start.5 = (bf16[256,384]{1,0:T(8,128)(2,1)S(1)}, bf16[256,384]{1,0:T(8,128)(2,1)S(1)}, u32[]{:S(2)}, u32[]{:S(2)}) collective-permute-start(bf16[256,384]{1,0:T(8,128)(2,1)S(1)} %add_convert_fusion), channel_id=1, source_target_pairs={{0,4},{1,5},{2,12},{3,13},{4,0},{5,1},{6,8},{7,9},{8,6},{9,7},{10,... | collective-permute-start | bytes 589832 | tf_op jit(solution)/shard_map/ppermute | solution.py:330
  37.2 8.6 %collective-permute-start.11 = (bf16[256,384]{1,0:T(8,128)(2,1)S(1)}, bf16[256,384]{1,0:T(8,128)(2,1)S(1)}, u32[]{:S(2)}, u32[]{:S(2)}) collective-permute-start(bf16[256,384]{1,0:T(8,128)(2,1)S(1)} %shard_map.98.t0), channel_id=1, source_target_pairs={{0,8},{1,9},{2,10},{3,11},{4,12},{5,13},{6,14},{7,15},{8,0},{9,1},... | collective-permute-start | bytes 589832 | tf_op jit(solution)/shard_map/ppermute | solution.py:330
  41.8 4.1 %collective-permute-start.12 = (bf16[256,384]{1,0:T(8,128)(2,1)S(1)}, bf16[256,384]{1,0:T(8,128)(2,1)S(1)}, u32[]{:S(2)}, u32[]{:S(2)}) collective-permute-start(bf16[256,384]{1,0:T(8,128)(2,1)S(1)} %collective-permute-done.10.t2), channel_id=1, source_target_pairs={{0,8},{1,9},{2,10},{3,11},{4,12},{5,13},{6,14},{7,15},{8,0},{9,1},... | collective-permute-start | bytes 589832 | tf_op jit(solution)/shard_map/ppermute | solution.py:330
  41.8 4.1 %collective-permute-start.6 = (bf16[256,384]{1,0:T(8,128)(2,1)S(1)}, bf16[256,384]{1,0:T(8,128)(2,1)S(1)}, u32[]{:S(2)}, u32[]{:S(2)}) collective-permute-start(bf16[256,384]{1,0:T(8,128)(2,1)S(1)} %collective-permute-done.4.c0), channel_id=1, source_target_pairs={{0,8},{1,9},{2,10},{3,11},{4,12},{5,13},{6,14},{7,15},{8,0},{9,1},... | collective-permute-start | bytes 589832 | tf_op jit(solution)/shard_map/ppermute | solution.py:330
  45.1 1.9 %collective-permute-start.7 = (bf16[256,384]{1,0:T(8,128)(2,1)S(1)}, bf16[256,384]{1,0:T(8,128)(2,1)S(1)}, u32[]{:S(2)}, u32[]{:S(2)}) collective-permute-start(bf16[256,384]{1,0:T(8,128)(2,1)S(1)} %collective-permute-done.5.c2), channel_id=1, source_target_pairs={{0,8},{1,9},{2,10},{3,11},{4,12},{5,13},{6,14},{7,15},{8,0},{9,1},... | collective-permute-start | bytes 589832 | tf_op jit(solution)/shard_map/ppermute | solution.py:330
  55.4 2.9 %collective-permute-start.13 = (bf16[256,384]{1,0:T(8,128)(2,1)S(1)}, bf16[256,384]{1,0:T(8,128)(2,1)S(1)}, u32[]{:S(2)}, u32[]{:S(2)}) collective-permute-start(bf16[256,384]{1,0:T(8,128)(2,1)S(1)} %get-tuple-element.14), channel_id=1, source_target_pairs={{0,0},{1,1},{2,8},{3,9},{4,4},{5,5},{6,12},{7,13},{8,2},{9,3},{10,... | collective-permute-start | bytes 589832 | tf_op jit(solution)/shard_map/ppermute | solution.py:330
  56.1 7.3 %collective-permute-start.14 = (bf16[256,384]{1,0:T(8,128)(2,1)S(1)}, bf16[256,384]{1,0:T(8,128)(2,1)S(1)}, u32[]{:S(2)}, u32[]{:S(2)}) collective-permute-start(bf16[256,384]{1,0:T(8,128)(2,1)S(1)} %get-tuple-element.15), channel_id=1, source_target_pairs={{0,1},{1,0},{2,9},{3,8},{4,5},{5,4},{6,13},{7,12},{8,3},{9,2},{10,... | collective-permute-start | bytes 589832 | tf_op jit(solution)/shard_map/ppermute | solution.py:330
  65.8 18.6 %collective-permute-start.17 = (bf16[2,128,384]{2,1,0:T(8,128)(2,1)S(1)}, bf16[2,128,384]{2,1,0:T(8,128)(2,1)S(1)}, u32[]{:S(2)}, u32[]{:S(2)}) collective-permute-start(bf16[2,128,384]{2,1,0:T(8,128)(2,1)S(1)} %shard_map.100), channel_id=1, source_target_pairs={{8,0},{16,8},{24,16},{32,24},{40,32},{48,40},{56,48},{64,56},{72,6... | collective-permute-start | bytes 589832 | tf_op jit(solution)/shard_map/ppermute | solution.py:408
  74.5 3.5 %collective-permute-start.15 = (bf16[128,384]{1,0:T(8,128)(2,1)S(1)}, bf16[128,384]{1,0:T(8,128)(2,1)S(1)}, u32[]{:S(2)}, u32[]{:S(2)}) collective-permute-start(bf16[128,384]{1,0:T(8,128)(2,1)S(1)} %get-tuple-element.16), channel_id=1, source_target_pairs={{0,0},{1,1},{2,8},{3,9},{4,4},{5,5},{6,12},{7,13},{8,2},{9,3},{10,... | collective-permute-start | bytes 294920 | tf_op jit(solution)/shard_map/ppermute | solution.py:330
  75.2 6.2 %collective-permute-start.16 = (bf16[128,384]{1,0:T(8,128)(2,1)S(1)}, bf16[128,384]{1,0:T(8,128)(2,1)S(1)}, u32[]{:S(2)}, u32[]{:S(2)}) collective-permute-start(bf16[128,384]{1,0:T(8,128)(2,1)S(1)} %get-tuple-element.17), channel_id=1, source_target_pairs={{0,1},{1,0},{2,9},{3,8},{4,5},{5,4},{6,13},{7,12},{8,3},{9,2},{10,... | collective-permute-start | bytes 294920 | tf_op jit(solution)/shard_map/ppermute | solution.py:330

commit v5 on v4

--- a/solution.py
+++ b/solution.py
@@ -172,7 +172,7 @@
     conv_steps(taps, w_ref.at[0], w_ref.at[1], out, 0, 1)
 
 
-def grad_own_kernel(place, r0, r1, out0, out1, w_ref, w_last, out, block_out, taps, sems):
+def grad_own_kernel(place, taps, out0, out1, w_ref, w_last, out, block_out, sems):
     x = place[0]
     copies = [
         pltpu.make_async_copy(out0, block_out.at[x], sems.at[0]),
@@ -180,7 +180,6 @@
     ]
     for copy in copies:
         copy.start()
-    fill_slab(place, taps, r0, r1)
     conv_steps(taps, w_last, w_ref.at[1], out, 1, 0)
     for copy in copies:
         copy.wait()
@@ -205,7 +204,7 @@
     return lax.dot_general(a, b, (((0,), (0,)), ((), ())), preferred_element_type=F32)
 
 
-CHUNKS = ((0, 384), (384, 256), (640, 256), (896, 128))
+CHUNKS = ((0, 384), (384, 640))
 
 
 def attention_kernel(
@@ -400,16 +399,16 @@
     out1 = send(out1, runs, home(0, 1))
     out0 = send(out0, runs, home(0, 0))
 
-    for_last = call(
+    for_last, taps = call(
         grad_last_kernel, (place, grad0, grad1, weight), [SM, VM, VM, VM],
-        [((2, block, chans), BF16)], [pltpu.VMEM((2, 4, width, 3 * chans), BF16)],
+        [((2, block, chans), BF16), ((2, 4, width, 3 * chans), BF16)], [],
         24 * MIB, 10**9,
-    )[0]
+    )
     handed = lax.ppermute(for_last, "tm", [(i + 1, i) for i in range(runs - 1)])
     own_grad, block_out = call(
-        grad_own_kernel, (place, grad0, grad1, out0, out1, weight, w_last), [SM] + [VM] * 6,
+        grad_own_kernel, (place, taps, out0, out1, weight, w_last), [SM] + [VM] * 5,
         [((2, block, chans), F32), ((2, block, chans), BF16)],
-        [pltpu.VMEM((2, 4, width, 3 * chans), BF16), pltpu.SemaphoreType.DMA((2,))],
+        [pltpu.SemaphoreType.DMA((2,))],
         24 * MIB, 10**9, outs=(VM, HBM),
     )
     video_grad = finish(own_grad, handed)

time: 87 us -> 86.5 us (level)
  no operation moved by 1% of the time
where the time goes in v5:
time: 86.5 us; the launch traced here: 84.8 us
  starting transfers between devices  40.5 us (47%)
  Pallas kernels  22.4 us (26%)
  waiting for transfers between devices  14.9 us (17%)
  local copies, waits for them, and re-layouts  5.85 us (7%)
  between operations  1.01 us (1%)
    ppermute x16, starting transfers between devices, send(): return lax.ppermute(value, ('tm', 'rows'), pairs)  27.9 us
    ppermute x16, waiting for transfers between devices, send(): return lax.ppermute(value, ('tm', 'rows'), pairs)  14.9 us
    pallas_call x7, Pallas kernels, call(): pl.pallas_call(kernel, in_specs=specs, out_specs=list(outs) if isinstance...  14.4 us
    ppermute x1, starting transfers between devices, local(): handed = lax.ppermute(for_last, 'tm', [(i + 1, i) for i in range(runs - 1)])  8.67 us
    pallas_call x1, Pallas kernels, attention(): pl.pallas_call(attention_kernel, in_specs=[SM] + [VM] * (len(convs) + len...  7.98 us
    unnamed x16, local copies, waits for them, and re-layouts  4.88 us
    ppermute x1, starting transfers between devices, local(): cached = lax.ppermute(for_next, 'tm', [(i, i + 1) for i in range(runs - 1)])  3.97 us
  transfers between devices with their start and end apart: 18, of which 6 were waited for; matrix products, arithmetic and copies ran while one was open for 1% of the time, Pallas kernels for 13%

profile of v5, /device:TPU:6, one launch (start us, length us, event | category | flops | bytes accessed | tf_op | source)
XLA Modules:
  0.0 84.8 jit_solution(9820944569640878076)
XLA Ops:
  0.6 1.5 %collective-permute-start = (bf16[256,384]{1,0:T(8,128)(2,1)}, bf16[256,384]{1,0:T(8,128)(2,1)S(1)}, u32[]{:S(2)}, u32[]{:S(2)}) collective-permute-start(bf16[256,384]{1,0:T(8,128)(2,1)} %bitcast.11), channel_id=1, source_target_pairs={{0,1},{1,0},{2,3},{3,2},{4,5},{5,4},{6,7},{7,6},{8,9},{9,8},{10,11... | collective-permute-start | bytes 589832 | tf_op jit(solution)/shard_map/ppermute | solution.py:329
  2.1 0.9 %constant_dynamic-slice_fusion = bf16[2,1,64,384]{3,2,1,0:T(8,128)(2,1)S(1)} fusion(bf16[2,2,64,384]{3,2,1,0:T(8,128)(2,1)} %param.8, s32[]{:T(128)S(6)} %select_n.27), kind=kLoop, calls=%fused_computation.3 | loop fusion | bytes 196612 | tf_op jit(solution)/shard_map/jit(dynamic_index_in_dim)/dynamic_slice | solution.py:364
  3.1 3.5 %collective-permute-start.1 = (bf16[128,384]{1,0:T(8,128)(2,1)S(1)}, bf16[128,384]{1,0:T(8,128)(2,1)S(1)}, u32[]{:S(2)}, u32[]{:S(2)}) collective-permute-start(bf16[128,384]{1,0:T(8,128)(2,1)S(1)} %bitcast.14), channel_id=1, source_target_pairs={{1,3},{2,0},{3,5},{4,2},{5,7},{6,4},{9,11},{10,8},{11,13},{12,10},... | collective-permute-start | bytes 294920 | tf_op jit(solution)/shard_map/ppermute | solution.py:329
  6.6 3.9 %collective-permute-start.2 = (bf16[128,384]{1,0:T(8,128)(2,1)S(1)}, bf16[128,384]{1,0:T(8,128)(2,1)S(1)}, u32[]{:S(2)}, u32[]{:S(2)}) collective-permute-start(bf16[128,384]{1,0:T(8,128)(2,1)S(1)} %bitcast.15), channel_id=1, source_target_pairs={{1,2},{2,1},{3,4},{4,3},{5,6},{6,5},{9,10},{10,9},{11,12},{12,11},... | collective-permute-start | bytes 294920 | tf_op jit(solution)/shard_map/ppermute | solution.py:329
  10.5 1.6 %collective-permute-start.8 = (bf16[2,128,384]{2,1,0:T(8,128)(2,1)}, bf16[2,128,384]{2,1,0:T(8,128)(2,1)S(1)}, u32[]{:S(2)}, u32[]{:S(2)}) collective-permute-start(bf16[2,128,384]{2,1,0:T(8,128)(2,1)} %bitcast.16), channel_id=1, source_target_pairs={{0,0},{1,1},{2,8},{3,9},{4,4},{5,5},{6,12},{7,13},{8,2},{9,3},{10,... | collective-permute-start | bytes 589832 | tf_op jit(solution)/shard_map/ppermute | solution.py:329
  12.1 2.6 %shard_map.95.w_ref = bf16[2,3,3,384,384]{4,3,2,1,0:T(8,128)(2,1)S(1)} custom-call(bf16[3,3,3,384,384]{4,3,2,1,0:T(8,128)(2,1)} %w_hbm.3), custom_call_target="tpu_custom_call" | custom-call | bytes 1048576 | tf_op jit(solution)/shard_map/pallas_call | solution.py:21
  14.6 2.4 %copy-done = bf16[2,3,3,384,384]{4,3,2,1,0:T(8,128)(2,1)} copy-done((bf16[2,3,3,384,384]{4,3,2,1,0:T(8,128)(2,1)}, bf16[2,3,3,384,384]{4,3,2,1,0:T(8,128)(2,1)S(1)}, u32[]{:S(2)}) %copy-start) | copy-done | bytes 5308440
  17.1 2.5 %copy-done.1 = bf16[2,3,3,384,384]{4,3,2,1,0:T(8,128)(2,1)S(1)} copy-done((bf16[2,3,3,384,384]{4,3,2,1,0:T(8,128)(2,1)S(1)}, bf16[2,3,3,384,384]{4,3,2,1,0:T(8,128)(2,1)}, u32[]{:S(2)}) %copy-start.1) | copy-done | bytes 5308440
  19.6 2.3 %shard_map.96 = (bf16[256,384]{1,0:T(8,128)(2,1)S(1)}, bf16[2,6,64,1152]{3,2,1,0:T(8,128)(2,1)S(1)}, bf16[3,3,384,384]{3,2,1,0:T(8,128)(2,1)S(1)}) custom-call(s32[2]{0:T(128)S(1)} %pad_add_fusion.place, bf16[256,384]{1,0:T(8,128)(2,1)S(1)} %bitcast.12, bf16[256,384]{1,0:T(8,128)(2,1)S(1)} %collective-permute-done.packet, ...), custom_call_target="tpu_custom_call" | custom-call | flops 1000000000 | bytes 1048576 | tf_op jit(solution)/shard_map/pallas_call | solution.py:21
  21.9 4.0 %collective-permute-start.3 = (bf16[256,384]{1,0:T(8,128)(2,1)S(1)}, bf16[256,384]{1,0:T(8,128)(2,1)S(1)}, u32[]{:S(2)}, u32[]{:S(2)}) collective-permute-start(bf16[256,384]{1,0:T(8,128)(2,1)S(1)} %get-tuple-element.15), channel_id=1, source_target_pairs={{0,8},{8,16},{16,24},{24,32},{32,40},{40,48},{48,56},{56,64},{64,7... | collective-permute-start | bytes 589832 | tf_op jit(solution)/shard_map/ppermute | solution.py:382
  25.9 2.5 %collective-permute-start.9 = (bf16[128,384]{1,0:T(8,128)(2,1)S(1)}, bf16[128,384]{1,0:T(8,128)(2,1)S(1)}, u32[]{:S(2)}, u32[]{:S(2)}) collective-permute-start(bf16[128,384]{1,0:T(8,128)(2,1)S(1)} %get-tuple-element.24), channel_id=1, source_target_pairs={{0,1},{1,0},{2,3},{3,2},{4,5},{5,4},{6,7},{7,6},{8,9},{9,8},{10,11... | collective-permute-start | bytes 294920 | tf_op jit(solution)/shard_map/ppermute | solution.py:329
  28.4 2.8 %shard_map.97 = f32[256,384]{1,0:T(8,128)S(1)} custom-call(s32[2]{0:T(128)S(1)} %pad_add_fusion.place, bf16[2,6,64,1152]{3,2,1,0:T(8,128)(2,1)S(1)} %get-tuple-element.13.taps, bf16[2,3,3,384,384]{4,3,2,1,0:T(8,128)(2,1)S(1)} %copy-done.1, bf16[3,3,384,384]{3,2,1,0:T(8,128)(2,1)S(1)} %get-tuple-element.14.w_last), custom_call_target="tpu_custom_call" | custom-call | flops 1000000000 | bytes 1048576 | tf_op jit(solution)/shard_map/pallas_call | solution.py:21
  31.2 1.0 %collective-permute-done.9.other = bf16[128,384]{1,0:T(8,128)(2,1)S(1)} collective-permute-done((bf16[128,384]{1,0:T(8,128)(2,1)S(1)}, bf16[128,384]{1,0:T(8,128)(2,1)S(1)}, u32[]{:S(2)}, u32[]{:S(2)}) %collective-permute-start.9) | collective-permute-done | bytes 98336 | tf_op jit(solution)/shard_map/ppermute | solution.py:329
  32.8 2.3 %collective-permute-start.10 = (bf16[256,384]{1,0:T(8,128)(2,1)S(1)}, bf16[256,384]{1,0:T(8,128)(2,1)S(1)}, u32[]{:S(2)}, u32[]{:S(2)}) collective-permute-start(bf16[256,384]{1,0:T(8,128)(2,1)S(1)} %shard_map.98.t0), channel_id=1, source_target_pairs={{0,4},{1,5},{2,6},{3,7},{4,0},{5,1},{6,2},{7,3},{8,12},{9,13},{10,... | collective-permute-start | bytes 589832 | tf_op jit(solution)/shard_map/ppermute | solution.py:329
  35.2 0.7 collective-permute-start.4
  35.9 1.4 %collective-permute-start.5 = (bf16[256,384]{1,0:T(8,128)(2,1)S(1)}, bf16[256,384]{1,0:T(8,128)(2,1)S(1)}, u32[]{:S(2)}, u32[]{:S(2)}) collective-permute-start(bf16[256,384]{1,0:T(8,128)(2,1)S(1)} %add_convert_fusion), channel_id=1, source_target_pairs={{0,4},{1,5},{2,12},{3,13},{4,0},{5,1},{6,8},{7,9},{8,6},{9,7},{10,... | collective-permute-start | bytes 589832 | tf_op jit(solution)/shard_map/ppermute | solution.py:329
  37.2 0.8 collective-permute-start.11
  38.1 3.7 %collective-permute-done.10.t2 = bf16[256,384]{1,0:T(8,128)(2,1)S(1)} collective-permute-done((bf16[256,384]{1,0:T(8,128)(2,1)S(1)}, bf16[256,384]{1,0:T(8,128)(2,1)S(1)}, u32[]{:S(2)}, u32[]{:S(2)}) %collective-permute-start.10) | collective-permute-done | bytes 196640 | tf_op jit(solution)/shard_map/ppermute | solution.py:329
  41.8 2.6 %collective-permute-start.6 = (bf16[256,384]{1,0:T(8,128)(2,1)S(1)}, bf16[256,384]{1,0:T(8,128)(2,1)S(1)}, u32[]{:S(2)}, u32[]{:S(2)}) collective-permute-start(bf16[256,384]{1,0:T(8,128)(2,1)S(1)} %collective-permute-done.4.c0), channel_id=1, source_target_pairs={{0,8},{1,9},{2,10},{3,11},{4,12},{5,13},{6,14},{7,15},{8,0},{9,1},... | collective-permute-start | bytes 589832 | tf_op jit(solution)/shard_map/ppermute | solution.py:329
  44.4 0.7 collective-permute-done.5.c2
  45.1 0.8 collective-permute-start.7
  45.9 1.0 %collective-permute-done.7.c3 = bf16[256,384]{1,0:T(8,128)(2,1)S(1)} collective-permute-done((bf16[256,384]{1,0:T(8,128)(2,1)S(1)}, bf16[256,384]{1,0:T(8,128)(2,1)S(1)}, u32[]{:S(2)}, u32[]{:S(2)}) %collective-permute-start.7) | collective-permute-done | bytes 196640 | tf_op jit(solution)/shard_map/ppermute | solution.py:329
  47.0 8.0 %attention.1 = (bf16[128,384]{1,0:T(8,128)(2,1)S(1)}, bf16[128,384]{1,0:T(8,128)(2,1)S(1)}, bf16[256,384]{1,0:T(8,128)(2,1)S(1)}, bf16[256,384]{1,0:T(8,128)(2,1)S(1)}) custom-call(s32[2]{0:T(128)S(1)} %pad_add_fusion.place, bf16[256,384]{1,0:T(8,128)(2,1)S(1)} %collective-permute-done.4.c0, bf16[256,384]{1,0:T(8,128)(2,1)S(1)} %collective-permute-done.5.c2, ...), custom_call_target="tpu_custom_call" | custom-call | flops 4000000000 | bytes 4000000 | tf_op jit(solution)/shard_map/attention/pallas_call | solution.py:300
  55.0 0.7 collective-permute-start.13
  55.6 2.2 %collective-permute-start.14 = (bf16[256,384]{1,0:T(8,128)(2,1)S(1)}, bf16[256,384]{1,0:T(8,128)(2,1)S(1)}, u32[]{:S(2)}, u32[]{:S(2)}) collective-permute-start(bf16[256,384]{1,0:T(8,128)(2,1)S(1)} %get-tuple-element.17), channel_id=1, source_target_pairs={{0,1},{1,0},{2,9},{3,8},{4,5},{5,4},{6,13},{7,12},{8,3},{9,2},{10,... | collective-permute-start | bytes 589832 | tf_op jit(solution)/shard_map/ppermute | solution.py:329
  57.9 5.0 %collective-permute-done.14.r1 = bf16[256,384]{1,0:T(8,128)(2,1)S(1)} collective-permute-done((bf16[256,384]{1,0:T(8,128)(2,1)S(1)}, bf16[256,384]{1,0:T(8,128)(2,1)S(1)}, u32[]{:S(2)}, u32[]{:S(2)}) %collective-permute-start.14) | collective-permute-done | bytes 196640 | tf_op jit(solution)/shard_map/ppermute | solution.py:329
  62.9 2.5 %shard_map.99 = (bf16[2,128,384]{2,1,0:T(8,128)(2,1)S(1)}, bf16[2,4,64,1152]{3,2,1,0:T(8,128)(2,1)S(1)}) custom-call(s32[2]{0:T(128)S(1)} %pad_add_fusion.place, bf16[256,384]{1,0:T(8,128)(2,1)S(1)} %collective-permute-done.13.r0, bf16[256,384]{1,0:T(8,128)(2,1)S(1)} %collective-permute-done.14.r1, bf16[2,3,3,384,384]{4,3,2,1,0:T(8,128)(2,1)S(1)} %copy-done.1), custom_call_target="tpu_custom_call" | custom-call | flops 1000000000 | bytes 1048576 | tf_op jit(solution)/shard_map/pallas_call | solution.py:21
  65.4 8.7 %collective-permute-start.17 = (bf16[2,128,384]{2,1,0:T(8,128)(2,1)S(1)}, bf16[2,128,384]{2,1,0:T(8,128)(2,1)S(1)}, u32[]{:S(2)}, u32[]{:S(2)}) collective-permute-start(bf16[2,128,384]{2,1,0:T(8,128)(2,1)S(1)} %get-tuple-element.23), channel_id=1, source_target_pairs={{8,0},{16,8},{24,16},{32,24},{40,32},{48,40},{56,48},{64,56},{72,6... | collective-permute-start | bytes 589832 | tf_op jit(solution)/shard_map/ppermute | solution.py:407
  74.7 2.8 %collective-permute-start.16 = (bf16[128,384]{1,0:T(8,128)(2,1)S(1)}, bf16[128,384]{1,0:T(8,128)(2,1)S(1)}, u32[]{:S(2)}, u32[]{:S(2)}) collective-permute-start(bf16[128,384]{1,0:T(8,128)(2,1)S(1)} %get-tuple-element.20), channel_id=1, source_target_pairs={{0,1},{1,0},{2,9},{3,8},{4,5},{5,4},{6,13},{7,12},{8,3},{9,2},{10,... | collective-permute-start | bytes 294920 | tf_op jit(solution)/shard_map/ppermute | solution.py:329
  77.5 3.4 %collective-permute-done.16.out1 = bf16[128,384]{1,0:T(8,128)(2,1)S(1)} collective-permute-done((bf16[128,384]{1,0:T(8,128)(2,1)S(1)}, bf16[128,384]{1,0:T(8,128)(2,1)S(1)}, u32[]{:S(2)}, u32[]{:S(2)}) %collective-permute-start.16) | collective-permute-done | bytes 98336 | tf_op jit(solution)/shard_map/ppermute | solution.py:329
  80.9 3.0 %shard_map.100 = (f32[2,128,384]{2,1,0:T(8,128)S(1)}, bf16[2,128,384]{2,1,0:T(8,128)(2,1)}) custom-call(s32[2]{0:T(128)S(1)} %pad_add_fusion.place, bf16[2,4,64,1152]{3,2,1,0:T(8,128)(2,1)S(1)} %get-tuple-element.18.taps, bf16[128,384]{1,0:T(8,128)(2,1)S(1)} %collective-permute-done.15.out0, bf16[128,384]{1,0:T(8,128)(2,1)S(1)} %collective-permute-done.16.out1, ...), custom_call_target="tpu_custom_call" | custom-call | flops 1000000000 | bytes 1048576 | tf_op jit(solution)/shard_map/pallas_call | solution.py:21
  83.9 0.7 shard_map.101
  (33 shorter events, 1.4 us)
Async XLA Ops:
  0.6 16.5 %collective-permute-start = (bf16[256,384]{1,0:T(8,128)(2,1)}, bf16[256,384]{1,0:T(8,128)(2,1)S(1)}, u32[]{:S(2)}, u32[]{:S(2)}) collective-permute-start(bf16[256,384]{1,0:T(8,128)(2,1)} %bitcast.11), channel_id=1, source_target_pairs={{0,1},{1,0},{2,3},{3,2},{4,5},{5,4},{6,7},{7,6},{8,9},{9,8},{10,11... | collective-permute-start | bytes 589832 | tf_op jit(solution)/shard_map/ppermute | solution.py:329
  3.1 14.0 %collective-permute-start.1 = (bf16[128,384]{1,0:T(8,128)(2,1)S(1)}, bf16[128,384]{1,0:T(8,128)(2,1)S(1)}, u32[]{:S(2)}, u32[]{:S(2)}) collective-permute-start(bf16[128,384]{1,0:T(8,128)(2,1)S(1)} %bitcast.14), channel_id=1, source_target_pairs={{1,3},{2,0},{3,5},{4,2},{5,7},{6,4},{9,11},{10,8},{11,13},{12,10},... | collective-permute-start | bytes 294920 | tf_op jit(solution)/shard_map/ppermute | solution.py:329
  6.6 10.5 %collective-permute-start.2 = (bf16[128,384]{1,0:T(8,128)(2,1)S(1)}, bf16[128,384]{1,0:T(8,128)(2,1)S(1)}, u32[]{:S(2)}, u32[]{:S(2)}) collective-permute-start(bf16[128,384]{1,0:T(8,128)(2,1)S(1)} %bitcast.15), channel_id=1, source_target_pairs={{1,2},{2,1},{3,4},{4,3},{5,6},{6,5},{9,10},{10,9},{11,12},{12,11},... | collective-permute-start | bytes 294920 | tf_op jit(solution)/shard_map/ppermute | solution.py:329
  10.5 15.4 %collective-permute-start.8 = (bf16[2,128,384]{2,1,0:T(8,128)(2,1)}, bf16[2,128,384]{2,1,0:T(8,128)(2,1)S(1)}, u32[]{:S(2)}, u32[]{:S(2)}) collective-permute-start(bf16[2,128,384]{2,1,0:T(8,128)(2,1)} %bitcast.16), channel_id=1, source_target_pairs={{0,0},{1,1},{2,8},{3,9},{4,4},{5,5},{6,12},{7,13},{8,2},{9,3},{10,... | collective-permute-start | bytes 589832 | tf_op jit(solution)/shard_map/ppermute | solution.py:329
  12.1 5.0 %copy-start.2 = (bf16[2,2,64,384]{3,2,1,0:T(8,128)(2,1)S(1)}, bf16[2,2,64,384]{3,2,1,0:T(8,128)(2,1)}, u32[]{:S(2)}) copy-start(bf16[2,2,64,384]{3,2,1,0:T(8,128)(2,1)} %param.8) | copy-start | bytes 589828
  14.6 2.4 %copy-start = (bf16[2,3,3,384,384]{4,3,2,1,0:T(8,128)(2,1)}, bf16[2,3,3,384,384]{4,3,2,1,0:T(8,128)(2,1)S(1)}, u32[]{:S(2)}) copy-start(bf16[2,3,3,384,384]{4,3,2,1,0:T(8,128)(2,1)S(1)} %shard_map.95.w_ref) | copy-start | bytes 15925252
  17.1 2.5 %copy-start.1 = (bf16[2,3,3,384,384]{4,3,2,1,0:T(8,128)(2,1)S(1)}, bf16[2,3,3,384,384]{4,3,2,1,0:T(8,128)(2,1)}, u32[]{:S(2)}) copy-start(bf16[2,3,3,384,384]{4,3,2,1,0:T(8,128)(2,1)} %copy-done) | copy-start | bytes 15925252
  21.9 13.2 %collective-permute-start.3 = (bf16[256,384]{1,0:T(8,128)(2,1)S(1)}, bf16[256,384]{1,0:T(8,128)(2,1)S(1)}, u32[]{:S(2)}, u32[]{:S(2)}) collective-permute-start(bf16[256,384]{1,0:T(8,128)(2,1)S(1)} %get-tuple-element.15), channel_id=1, source_target_pairs={{0,8},{8,16},{16,24},{24,32},{32,40},{40,48},{48,56},{56,64},{64,7... | collective-permute-start | bytes 589832 | tf_op jit(solution)/shard_map/ppermute | solution.py:382
  25.9 6.3 %collective-permute-start.9 = (bf16[128,384]{1,0:T(8,128)(2,1)S(1)}, bf16[128,384]{1,0:T(8,128)(2,1)S(1)}, u32[]{:S(2)}, u32[]{:S(2)}) collective-permute-start(bf16[128,384]{1,0:T(8,128)(2,1)S(1)} %get-tuple-element.24), channel_id=1, source_target_pairs={{0,1},{1,0},{2,3},{3,2},{4,5},{5,4},{6,7},{7,6},{8,9},{9,8},{10,11... | collective-permute-start | bytes 294920 | tf_op jit(solution)/shard_map/ppermute | solution.py:329
  28.4 17.5 %copy-start.7 = (f32[384]{0:T(512)S(1)}, f32[384]{0:T(512)}, u32[]{:S(2)}) copy-start(f32[384]{0:T(512)} %param.10) | copy-start | bytes 4612
  28.4 18.6 %copy-start.3 = (bf16[384,384]{1,0:T(8,128)(2,1)S(1)}, bf16[384,384]{1,0:T(8,128)(2,1)}, u32[]{:S(2)}) copy-start(bf16[384,384]{1,0:T(8,128)(2,1)} %wq.1) | copy-start | bytes 884740
  28.4 18.6 %copy-start.4 = (bf16[384,384]{1,0:T(8,128)(2,1)S(1)}, bf16[384,384]{1,0:T(8,128)(2,1)}, u32[]{:S(2)}) copy-start(bf16[384,384]{1,0:T(8,128)(2,1)} %wk.1) | copy-start | bytes 884740
  28.4 18.6 %copy-start.5 = (bf16[384,384]{1,0:T(8,128)(2,1)S(1)}, bf16[384,384]{1,0:T(8,128)(2,1)}, u32[]{:S(2)}) copy-start(bf16[384,384]{1,0:T(8,128)(2,1)} %wv.1) | copy-start | bytes 884740
  28.4 18.6 %copy-start.6 = (bf16[384,384]{1,0:T(8,128)(2,1)S(1)}, bf16[384,384]{1,0:T(8,128)(2,1)}, u32[]{:S(2)}) copy-start(bf16[384,384]{1,0:T(8,128)(2,1)} %wo.1) | copy-start | bytes 884740
  32.8 9.0 %collective-permute-start.10 = (bf16[256,384]{1,0:T(8,128)(2,1)S(1)}, bf16[256,384]{1,0:T(8,128)(2,1)S(1)}, u32[]{:S(2)}, u32[]{:S(2)}) collective-permute-start(bf16[256,384]{1,0:T(8,128)(2,1)S(1)} %shard_map.98.t0), channel_id=1, source_target_pairs={{0,4},{1,5},{2,6},{3,7},{4,0},{5,1},{6,2},{7,3},{8,12},{9,13},{10,... | collective-permute-start | bytes 589832 | tf_op jit(solution)/shard_map/ppermute | solution.py:329
  35.2 6.6 %collective-permute-start.4 = (bf16[256,384]{1,0:T(8,128)(2,1)S(1)}, bf16[256,384]{1,0:T(8,128)(2,1)S(1)}, u32[]{:S(2)}, u32[]{:S(2)}) collective-permute-start(bf16[256,384]{1,0:T(8,128)(2,1)S(1)} %add_convert_fusion), channel_id=1, source_target_pairs={{0,0},{1,1},{2,8},{3,9},{4,4},{5,5},{6,12},{7,13},{8,2},{9,3},{10,... | collective-permute-start | bytes 589832 | tf_op jit(solution)/shard_map/ppermute | solution.py:329
  35.9 9.2 %collective-permute-start.5 = (bf16[256,384]{1,0:T(8,128)(2,1)S(1)}, bf16[256,384]{1,0:T(8,128)(2,1)S(1)}, u32[]{:S(2)}, u32[]{:S(2)}) collective-permute-start(bf16[256,384]{1,0:T(8,128)(2,1)S(1)} %add_convert_fusion), channel_id=1, source_target_pairs={{0,4},{1,5},{2,12},{3,13},{4,0},{5,1},{6,8},{7,9},{8,6},{9,7},{10,... | collective-permute-start | bytes 589832 | tf_op jit(solution)/shard_map/ppermute | solution.py:329
  37.2 8.7 %collective-permute-start.11 = (bf16[256,384]{1,0:T(8,128)(2,1)S(1)}, bf16[256,384]{1,0:T(8,128)(2,1)S(1)}, u32[]{:S(2)}, u32[]{:S(2)}) collective-permute-start(bf16[256,384]{1,0:T(8,128)(2,1)S(1)} %shard_map.98.t0), channel_id=1, source_target_pairs={{0,8},{1,9},{2,10},{3,11},{4,12},{5,13},{6,14},{7,15},{8,0},{9,1},... | collective-permute-start | bytes 589832 | tf_op jit(solution)/shard_map/ppermute | solution.py:329
  41.8 4.1 %collective-permute-start.12 = (bf16[256,384]{1,0:T(8,128)(2,1)S(1)}, bf16[256,384]{1,0:T(8,128)(2,1)S(1)}, u32[]{:S(2)}, u32[]{:S(2)}) collective-permute-start(bf16[256,384]{1,0:T(8,128)(2,1)S(1)} %collective-permute-done.10.t2), channel_id=1, source_target_pairs={{0,8},{1,9},{2,10},{3,11},{4,12},{5,13},{6,14},{7,15},{8,0},{9,1},... | collective-permute-start | bytes 589832 | tf_op jit(solution)/shard_map/ppermute | solution.py:329
  41.8 4.1 %collective-permute-start.6 = (bf16[256,384]{1,0:T(8,128)(2,1)S(1)}, bf16[256,384]{1,0:T(8,128)(2,1)S(1)}, u32[]{:S(2)}, u32[]{:S(2)}) collective-permute-start(bf16[256,384]{1,0:T(8,128)(2,1)S(1)} %collective-permute-done.4.c0), channel_id=1, source_target_pairs={{0,8},{1,9},{2,10},{3,11},{4,12},{5,13},{6,14},{7,15},{8,0},{9,1},... | collective-permute-start | bytes 589832 | tf_op jit(solution)/shard_map/ppermute | solution.py:329
  45.1 1.9 %collective-permute-start.7 = (bf16[256,384]{1,0:T(8,128)(2,1)S(1)}, bf16[256,384]{1,0:T(8,128)(2,1)S(1)}, u32[]{:S(2)}, u32[]{:S(2)}) collective-permute-start(bf16[256,384]{1,0:T(8,128)(2,1)S(1)} %collective-permute-done.5.c2), channel_id=1, source_target_pairs={{0,8},{1,9},{2,10},{3,11},{4,12},{5,13},{6,14},{7,15},{8,0},{9,1},... | collective-permute-start | bytes 589832 | tf_op jit(solution)/shard_map/ppermute | solution.py:329
  55.0 2.9 %collective-permute-start.13 = (bf16[256,384]{1,0:T(8,128)(2,1)S(1)}, bf16[256,384]{1,0:T(8,128)(2,1)S(1)}, u32[]{:S(2)}, u32[]{:S(2)}) collective-permute-start(bf16[256,384]{1,0:T(8,128)(2,1)S(1)} %get-tuple-element.16), channel_id=1, source_target_pairs={{0,0},{1,1},{2,8},{3,9},{4,4},{5,5},{6,12},{7,13},{8,2},{9,3},{10,... | collective-permute-start | bytes 589832 | tf_op jit(solution)/shard_map/ppermute | solution.py:329
  55.6 7.3 %collective-permute-start.14 = (bf16[256,384]{1,0:T(8,128)(2,1)S(1)}, bf16[256,384]{1,0:T(8,128)(2,1)S(1)}, u32[]{:S(2)}, u32[]{:S(2)}) collective-permute-start(bf16[256,384]{1,0:T(8,128)(2,1)S(1)} %get-tuple-element.17), channel_id=1, source_target_pairs={{0,1},{1,0},{2,9},{3,8},{4,5},{5,4},{6,13},{7,12},{8,3},{9,2},{10,... | collective-permute-start | bytes 589832 | tf_op jit(solution)/shard_map/ppermute | solution.py:329
  65.4 18.5 %collective-permute-start.17 = (bf16[2,128,384]{2,1,0:T(8,128)(2,1)S(1)}, bf16[2,128,384]{2,1,0:T(8,128)(2,1)S(1)}, u32[]{:S(2)}, u32[]{:S(2)}) collective-permute-start(bf16[2,128,384]{2,1,0:T(8,128)(2,1)S(1)} %get-tuple-element.23), channel_id=1, source_target_pairs={{8,0},{16,8},{24,16},{32,24},{40,32},{48,40},{56,48},{64,56},{72,6... | collective-permute-start | bytes 589832 | tf_op jit(solution)/shard_map/ppermute | solution.py:407
  74.0 3.5 %collective-permute-start.15 = (bf16[128,384]{1,0:T(8,128)(2,1)S(1)}, bf16[128,384]{1,0:T(8,128)(2,1)S(1)}, u32[]{:S(2)}, u32[]{:S(2)}) collective-permute-start(bf16[128,384]{1,0:T(8,128)(2,1)S(1)} %get-tuple-element.19), channel_id=1, source_target_pairs={{0,0},{1,1},{2,8},{3,9},{4,4},{5,5},{6,12},{7,13},{8,2},{9,3},{10,... | collective-permute-start | bytes 294920 | tf_op jit(solution)/shard_map/ppermute | solution.py:329
  74.7 6.2 %collective-permute-start.16 = (bf16[128,384]{1,0:T(8,128)(2,1)S(1)}, bf16[128,384]{1,0:T(8,128)(2,1)S(1)}, u32[]{:S(2)}, u32[]{:S(2)}) collective-permute-start(bf16[128,384]{1,0:T(8,128)(2,1)S(1)} %get-tuple-element.20), channel_id=1, source_target_pairs={{0,1},{1,0},{2,9},{3,8},{4,5},{5,4},{6,13},{7,12},{8,3},{9,2},{10,... | collective-permute-start | bytes 294920 | tf_op jit(solution)/shard_map/ppermute | solution.py:329

commit v6 on v5

--- a/solution.py
+++ b/solution.py
@@ -12,8 +12,14 @@
 LOG2E = 1.4426950408889634
 LOAD = 44 * MIB
 NEXT = 42 * MIB
+
+
+def seat():
+    slab, run = lax.axis_index("rows"), lax.axis_index("tm")
+    return lax.rem(slab, 2), 2 * lax.div(slab, 4) + lax.rem(run, 2)
+
+
 VM = pl.BlockSpec(memory_space=pltpu.VMEM)
-SM = pl.BlockSpec(memory_space=pltpu.SMEM)
 HBM = pl.BlockSpec(memory_space=pltpu.HBM)
 
 
@@ -29,16 +35,16 @@
     )(*operands)
 
 
-def join_kernel(place, same, other, out):
-    x = place[0]
+def join_kernel(same, other, out):
+    x, _ = seat()
     half = same.shape[0]
     out[pl.ds(pl.multiple_of(x * half, half), half)] = same[...]
     out[pl.ds(pl.multiple_of((1 - x) * half, half), half)] = other[...]
 
 
-def join(place, same, other):
+def join(same, other):
     shape = (2 * same.shape[0], same.shape[1])
-    return call(join_kernel, (place, same, other), [SM, VM, VM], [(shape, BF16)], [], 4 * MIB)[0]
+    return call(join_kernel, (same, other), [VM, VM], [(shape, BF16)], [], 4 * MIB)[0]
 
 
 def load_kernel(w_hbm, w_out, sem):
@@ -123,10 +129,10 @@
     return total
 
 
-def next_kernel(place, mine, packet, far_same, far_other, w_ref, w_hbm, out, taps, w_last, acc, sem):
+def next_kernel(mine, packet, far_same, far_other, w_ref, w_hbm, out, taps, w_last, acc, sem):
     copy = pltpu.make_async_copy(w_hbm.at[2], w_last, sem)
     copy.start()
-    x = place[0]
+    x, _ = seat()
     flip = x == 1
     width = taps.shape[2]
     chans = w_ref.shape[-1]
@@ -150,8 +156,8 @@
     copy.wait()
 
 
-def own_kernel(place, taps, w_ref, w_last, out):
-    x = place[0]
+def own_kernel(taps, w_ref, w_last, out):
+    x, _ = seat()
     out[...] = frame_conv(taps, w_last, x)
 
     @pl.when(x == 1)
@@ -159,21 +165,21 @@
         out[...] += frame_conv(taps, w_ref.at[1], 0)
 
 
-def fill_slab(place, taps, r0, r1):
+def fill_slab(taps, r0, r1):
     width, chans = taps.shape[2], r0.shape[-1]
-    swapped = place[0] == 1
+    swapped = seat()[0] == 1
     for f, (a, b) in enumerate(((r0, r1), (r1, r0))):
         rows = jnp.where(swapped, b[...], a[...])
         fill(taps, f, 0, rows.reshape(4, width, chans), width, True)
 
 
-def grad_last_kernel(place, r0, r1, w_ref, out, taps):
-    fill_slab(place, taps, r0, r1)
+def grad_last_kernel(r0, r1, w_ref, out, taps):
+    fill_slab(taps, r0, r1)
     conv_steps(taps, w_ref.at[0], w_ref.at[1], out, 0, 1)
 
 
-def grad_own_kernel(place, taps, out0, out1, w_ref, w_last, out, block_out, sems):
-    x = place[0]
+def grad_own_kernel(taps, out0, out1, w_ref, w_last, out, block_out, sems):
+    x, _ = seat()
     copies = [
         pltpu.make_async_copy(out0, block_out.at[x], sems.at[0]),
         pltpu.make_async_copy(out1, block_out.at[1 - x], sems.at[1]),
@@ -208,10 +214,10 @@
 
 
 def attention_kernel(
-    place, c0, c2, c1, c3, t0, t2, t1, t3, gain_ref, wq, wk, wv, wo,
+    c0, c2, c1, c3, t0, t2, t1, t3, gain_ref, wq, wk, wv, wo,
     out0, out1, grad0, grad1, conv_s, cot_s, act_s, q_s, k_s, v_s, g_s, gk_s, gv_s, out_s, grad_s,
 ):
-    x, q = place[0], place[1]
+    x, q = seat()
     line = c0.shape[0] // 4
     own = 6 * line
     chans = wq.shape[0]
@@ -293,13 +299,13 @@
         ref[...] = grad_s[pl.ds(pl.multiple_of(2 * to_x * line, line), 4 * line)]
 
 
-def attention(place, convs, cots, gain, wq, wk, wv, wo):
+def attention(convs, cots, gain, wq, wk, wv, wo):
     block, chans = convs[0].shape[0] // 2, convs[0].shape[1]
     own, whole = 3 * block, 8 * block
     act = lambda n, t=BF16: pltpu.VMEM((n, chans), t)
     return pl.pallas_call(
         attention_kernel,
-        in_specs=[SM] + [VM] * (len(convs) + len(cots) + 5),
+        in_specs=[VM] * (len(convs) + len(cots) + 5),
         out_specs=[VM] * 4,
         out_shape=[jax.ShapeDtypeStruct((n * block, chans), BF16) for n in (1, 1, 2, 2)],
         scratch_shapes=[act(whole), act(whole), act(own)]
@@ -310,7 +316,7 @@
             flops=4 * 10**9, bytes_accessed=4 * 10**6, transcendentals=1 << 20
         ),
         name="attention",
-    )(place, *convs, *cots, gain, wq, wk, wv, wo)
+    )(*convs, *cots, gain, wq, wk, wv, wo)
 
 
 def site(h, c, y, x):
@@ -355,10 +361,7 @@
     frames, height, width, chans = video.shape
     runs, slabs = lax.axis_size("tm"), lax.axis_size("rows")
     assert (frames, height, slabs) == (2, 2, 8)
-    slab_at = lax.axis_index("rows")
-    x = slab_at % 2
-    quarter = 2 * (slab_at // 4) + lax.axis_index("tm") % 2
-    place = jnp.stack([x, quarter]).astype(jnp.int32)
+    x, _ = seat()
     block = 2 * width
 
     edge = lax.dynamic_index_in_dim(video, x, 1, keepdims=False).reshape(block, chans)
@@ -373,17 +376,17 @@
     cot_other = send(cot_other, runs, across)
     quad = (2 * block, chans)
     for_next, taps, w_last = call(
-        next_kernel, (place, mine, packet, far_same, far_other, weight, conv_weight),
-        [SM] + [VM] * 5 + [HBM],
+        next_kernel, (mine, packet, far_same, far_other, weight, conv_weight),
+        [VM] * 5 + [HBM],
         [(quad, BF16), ((2, 6, width, 3 * chans), BF16), (conv_weight.shape[1:], BF16)],
         [pltpu.VMEM(quad, F32), pltpu.SemaphoreType.DMA],
         NEXT, 10**9,
     )
     cached = lax.ppermute(for_next, "tm", [(i, i + 1) for i in range(runs - 1)])
-    cot_b = join(place, cot_same, cot_other)
+    cot_b = join(cot_same, cot_other)
     cot_c = send(cot_b, runs, lambda c, y, x: (c, y ^ 2, x))
     own = call(
-        own_kernel, (place, taps, weight, w_last), [SM, VM, VM, VM], [(quad, F32)], [],
+        own_kernel, (taps, weight, w_last), [VM, VM, VM], [(quad, F32)], [],
         24 * MIB, 10**9,
     )[0]
     conv = (own + cached.astype(F32)).astype(BF16)
@@ -392,7 +395,7 @@
     cots = (cot_b, cot_c, send(cot_b, runs, swap), send(cot_c, runs, swap))
     convs = (conv_b, conv_c, send(conv_b, runs, swap), send(conv_c, runs, swap))
     out0, out1, grad0, grad1 = attention(
-        place, convs, cots, norm_gain.reshape(1, chans), w_query, w_key, w_value, w_out
+        convs, cots, norm_gain.reshape(1, chans), w_query, w_key, w_value, w_out
     )
     grad1 = send(grad1, runs, home(0, 1))
     grad0 = send(grad0, runs, home(0, 0))
@@ -400,13 +403,13 @@
     out0 = send(out0, runs, home(0, 0))
 
     for_last, taps = call(
-        grad_last_kernel, (place, grad0, grad1, weight), [SM, VM, VM, VM],
+        grad_last_kernel, (grad0, grad1, weight), [VM, VM, VM],
         [((2, block, chans), BF16), ((2, 4, width, 3 * chans), BF16)], [],
         24 * MIB, 10**9,
     )
     handed = lax.ppermute(for_last, "tm", [(i + 1, i) for i in range(runs - 1)])
     own_grad, block_out = call(
-        grad_own_kernel, (place, taps, out0, out1, weight, w_last), [SM] + [VM] * 5,
+        grad_own_kernel, (taps, out0, out1, weight, w_last), [VM] * 5,
         [((2, block, chans), F32), ((2, block, chans), BF16)],
         [pltpu.SemaphoreType.DMA((2,))],
         24 * MIB, 10**9, outs=(VM, HBM),

time: 86.5 us -> 84.4 us (0.976)
  waiting for transfers between devices: 14.9 us -> 21.4 us
  starting transfers between devices: 40.5 us -> 35.1 us
  Pallas kernels: 22.4 us -> 19.4 us
    ppermute x16, waiting for transfers between devices: 14.9 us -> 21.4 us  [send(): return lax.ppermute(value, ('tm', 'rows'), pairs)]
    ppermute x16, starting transfers between devices: 27.9 us -> 23.6 us  [send(): return lax.ppermute(value, ('tm', 'rows'), pairs)]
    pallas_call x7, Pallas kernels: 14.4 us -> 11.8 us  [call(): pl.pallas_call(kernel, in_specs=specs, out_specs=list(outs) if isinstance...]
    ppermute x1, starting transfers between devices: 3.97 us -> 3 us  [local(): cached = lax.ppermute(for_next, 'tm', [(i, i + 1) for i in range(runs - 1)])]
  transfers between devices with their start and end apart: 18 -> 18, of which waited for: 6 -> 7; matrix products, arithmetic and copies ran while one was open for 1% -> 1% of each run, Pallas kernels for 13% -> 11%
where the time goes in v6:
time: 84.4 us; the launch traced here: 82.8 us
  starting transfers between devices  35.1 us (42%)
  waiting for transfers between devices  21.4 us (25%)
  Pallas kernels  19.4 us (23%)
  local copies, waits for them, and re-layouts  5.83 us (7%)
  between operations  1.03 us (1%)
    ppermute x16, starting transfers between devices, send(): return lax.ppermute(value, ('tm', 'rows'), pairs)  23.6 us
    ppermute x16, waiting for transfers between devices, send(): return lax.ppermute(value, ('tm', 'rows'), pairs)  21.4 us
    pallas_call x7, Pallas kernels, call(): pl.pallas_call(kernel, in_specs=specs, out_specs=list(outs) if isinstance...  11.8 us
    ppermute x1, starting transfers between devices, local(): handed = lax.ppermute(for_last, 'tm', [(i + 1, i) for i in range(runs - 1)])  8.52 us
    pallas_call x1, Pallas kernels, attention(): pl.pallas_call(attention_kernel, in_specs=[VM] * (len(convs) + len(cots)...  7.53 us
    unnamed x16, local copies, waits for them, and re-layouts  4.9 us
    ppermute x1, starting transfers between devices, local(): cached = lax.ppermute(for_next, 'tm', [(i, i + 1) for i in range(runs - 1)])  3 us
  transfers between devices with their start and end apart: 18, of which 7 were waited for; matrix products, arithmetic and copies ran while one was open for 1% of the time, Pallas kernels for 11%

profile of v6, /device:TPU:6, one launch (start us, length us, event | category | flops | bytes accessed | tf_op | source)
XLA Modules:
  0.0 82.8 jit_solution(13631076403080124320)
XLA Ops:
  0.6 1.5 %collective-permute-start = (bf16[256,384]{1,0:T(8,128)(2,1)}, bf16[256,384]{1,0:T(8,128)(2,1)S(1)}, u32[]{:S(2)}, u32[]{:S(2)}) collective-permute-start(bf16[256,384]{1,0:T(8,128)(2,1)} %bitcast.9), channel_id=1, source_target_pairs={{0,1},{1,0},{2,3},{3,2},{4,5},{5,4},{6,7},{7,6},{8,9},{9,8},{10,11... | collective-permute-start | bytes 589832 | tf_op jit(solution)/shard_map/ppermute | solution.py:335
  2.1 1.6 %collective-permute-start.8 = (bf16[2,128,384]{2,1,0:T(8,128)(2,1)}, bf16[2,128,384]{2,1,0:T(8,128)(2,1)S(1)}, u32[]{:S(2)}, u32[]{:S(2)}) collective-permute-start(bf16[2,128,384]{2,1,0:T(8,128)(2,1)} %bitcast.14), channel_id=1, source_target_pairs={{0,0},{1,1},{2,8},{3,9},{4,4},{5,5},{6,12},{7,13},{8,2},{9,3},{10,... | collective-permute-start | bytes 589832 | tf_op jit(solution)/shard_map/ppermute | solution.py:335
  3.7 0.9 %constant_dynamic-slice_fusion = bf16[2,1,64,384]{3,2,1,0:T(8,128)(2,1)S(1)} fusion(bf16[2,2,64,384]{3,2,1,0:T(8,128)(2,1)} %param.8, s32[]{:T(128)S(6)} %select_n.9), kind=kLoop, calls=%fused_computation.3 | loop fusion | bytes 196612 | tf_op jit(solution)/shard_map/jit(dynamic_index_in_dim)/dynamic_slice | solution.py:367
  4.6 3.8 %collective-permute-start.1 = (bf16[128,384]{1,0:T(8,128)(2,1)S(1)}, bf16[128,384]{1,0:T(8,128)(2,1)S(1)}, u32[]{:S(2)}, u32[]{:S(2)}) collective-permute-start(bf16[128,384]{1,0:T(8,128)(2,1)S(1)} %bitcast.12), channel_id=1, source_target_pairs={{1,3},{2,0},{3,5},{4,2},{5,7},{6,4},{9,11},{10,8},{11,13},{12,10},... | collective-permute-start | bytes 294920 | tf_op jit(solution)/shard_map/ppermute | solution.py:335
  8.5 3.6 %collective-permute-start.2 = (bf16[128,384]{1,0:T(8,128)(2,1)S(1)}, bf16[128,384]{1,0:T(8,128)(2,1)S(1)}, u32[]{:S(2)}, u32[]{:S(2)}) collective-permute-start(bf16[128,384]{1,0:T(8,128)(2,1)S(1)} %bitcast.13), channel_id=1, source_target_pairs={{1,2},{2,1},{3,4},{4,3},{5,6},{6,5},{9,10},{10,9},{11,12},{12,11},... | collective-permute-start | bytes 294920 | tf_op jit(solution)/shard_map/ppermute | solution.py:335
  12.0 2.6 %shard_map.95.w_ref = bf16[2,3,3,384,384]{4,3,2,1,0:T(8,128)(2,1)S(1)} custom-call(bf16[3,3,3,384,384]{4,3,2,1,0:T(8,128)(2,1)} %w_hbm.3), custom_call_target="tpu_custom_call" | custom-call | bytes 1048576 | tf_op jit(solution)/shard_map/pallas_call | solution.py:27
  14.6 2.4 %copy-done = bf16[2,3,3,384,384]{4,3,2,1,0:T(8,128)(2,1)} copy-done((bf16[2,3,3,384,384]{4,3,2,1,0:T(8,128)(2,1)}, bf16[2,3,3,384,384]{4,3,2,1,0:T(8,128)(2,1)S(1)}, u32[]{:S(2)}) %copy-start) | copy-done | bytes 5308440
  17.0 0.4 collective-permute-done.2.far_other
  17.4 2.5 %copy-done.1 = bf16[2,3,3,384,384]{4,3,2,1,0:T(8,128)(2,1)S(1)} copy-done((bf16[2,3,3,384,384]{4,3,2,1,0:T(8,128)(2,1)S(1)}, bf16[2,3,3,384,384]{4,3,2,1,0:T(8,128)(2,1)}, u32[]{:S(2)}) %copy-start.1) | copy-done | bytes 5308440
  19.9 2.0 %shard_map.96 = (bf16[256,384]{1,0:T(8,128)(2,1)S(1)}, bf16[2,6,64,1152]{3,2,1,0:T(8,128)(2,1)S(1)}, bf16[3,3,384,384]{3,2,1,0:T(8,128)(2,1)S(1)}) custom-call(bf16[256,384]{1,0:T(8,128)(2,1)S(1)} %bitcast.10, bf16[256,384]{1,0:T(8,128)(2,1)S(1)} %collective-permute-done.packet, bf16[128,384]{1,0:T(8,128)(2,1)S(1)} %collective-permute-done.1.far_same, ...), custom_call_target="tpu_custom_call" | custom-call | flops 1000000000 | bytes 1048576 | tf_op jit(solution)/shard_map/pallas_call | solution.py:27
  21.9 3.0 %collective-permute-start.3 = (bf16[256,384]{1,0:T(8,128)(2,1)S(1)}, bf16[256,384]{1,0:T(8,128)(2,1)S(1)}, u32[]{:S(2)}, u32[]{:S(2)}) collective-permute-start(bf16[256,384]{1,0:T(8,128)(2,1)S(1)} %get-tuple-element.15), channel_id=1, source_target_pairs={{0,8},{8,16},{16,24},{24,32},{32,40},{40,48},{48,56},{56,64},{64,7... | collective-permute-start | bytes 589832 | tf_op jit(solution)/shard_map/ppermute | solution.py:385
  25.1 2.3 %shard_map.97 = f32[256,384]{1,0:T(8,128)S(1)} custom-call(bf16[2,6,64,1152]{3,2,1,0:T(8,128)(2,1)S(1)} %get-tuple-element.13.taps, bf16[2,3,3,384,384]{4,3,2,1,0:T(8,128)(2,1)S(1)} %copy-done.1, bf16[3,3,384,384]{3,2,1,0:T(8,128)(2,1)S(1)} %get-tuple-element.14.w_last), custom_call_target="tpu_custom_call" | custom-call | flops 1000000000 | bytes 1048576 | tf_op jit(solution)/shard_map/pallas_call | solution.py:27
  27.3 4.8 %collective-permute-done.9.other = bf16[128,384]{1,0:T(8,128)(2,1)S(1)} collective-permute-done((bf16[128,384]{1,0:T(8,128)(2,1)S(1)}, bf16[128,384]{1,0:T(8,128)(2,1)S(1)}, u32[]{:S(2)}, u32[]{:S(2)}) %collective-permute-start.9) | collective-permute-done | bytes 98336 | tf_op jit(solution)/shard_map/ppermute | solution.py:335
  32.2 2.8 %collective-permute-start.10 = (bf16[256,384]{1,0:T(8,128)(2,1)S(1)}, bf16[256,384]{1,0:T(8,128)(2,1)S(1)}, u32[]{:S(2)}, u32[]{:S(2)}) collective-permute-start(bf16[256,384]{1,0:T(8,128)(2,1)S(1)} %shard_map.98.t0), channel_id=1, source_target_pairs={{0,4},{1,5},{2,6},{3,7},{4,0},{5,1},{6,2},{7,3},{8,12},{9,13},{10,... | collective-permute-start | bytes 589832 | tf_op jit(solution)/shard_map/ppermute | solution.py:335
  35.1 0.7 collective-permute-start.4
  35.7 1.9 %collective-permute-start.5 = (bf16[256,384]{1,0:T(8,128)(2,1)S(1)}, bf16[256,384]{1,0:T(8,128)(2,1)S(1)}, u32[]{:S(2)}, u32[]{:S(2)}) collective-permute-start(bf16[256,384]{1,0:T(8,128)(2,1)S(1)} %add_convert_fusion), channel_id=1, source_target_pairs={{0,4},{1,5},{2,12},{3,13},{4,0},{5,1},{6,8},{7,9},{8,6},{9,7},{10,... | collective-permute-start | bytes 589832 | tf_op jit(solution)/shard_map/ppermute | solution.py:335
  37.9 3.6 %collective-permute-done.10.t2 = bf16[256,384]{1,0:T(8,128)(2,1)S(1)} collective-permute-done((bf16[256,384]{1,0:T(8,128)(2,1)S(1)}, bf16[256,384]{1,0:T(8,128)(2,1)S(1)}, u32[]{:S(2)}, u32[]{:S(2)}) %collective-permute-start.10) | collective-permute-done | bytes 196640 | tf_op jit(solution)/shard_map/ppermute | solution.py:335
  41.5 1.8 %collective-permute-start.6 = (bf16[256,384]{1,0:T(8,128)(2,1)S(1)}, bf16[256,384]{1,0:T(8,128)(2,1)S(1)}, u32[]{:S(2)}, u32[]{:S(2)}) collective-permute-start(bf16[256,384]{1,0:T(8,128)(2,1)S(1)} %collective-permute-done.4.c0), channel_id=1, source_target_pairs={{0,8},{1,9},{2,10},{3,11},{4,12},{5,13},{6,14},{7,15},{8,0},{9,1},... | collective-permute-start | bytes 589832 | tf_op jit(solution)/shard_map/ppermute | solution.py:335
  43.3 1.7 %collective-permute-done.5.c2 = bf16[256,384]{1,0:T(8,128)(2,1)S(1)} collective-permute-done((bf16[256,384]{1,0:T(8,128)(2,1)S(1)}, bf16[256,384]{1,0:T(8,128)(2,1)S(1)}, u32[]{:S(2)}, u32[]{:S(2)}) %collective-permute-start.5) | collective-permute-done | bytes 196640 | tf_op jit(solution)/shard_map/ppermute | solution.py:335
  45.0 0.6 collective-permute-start.7
  45.6 1.0 %collective-permute-done.7.c3 = bf16[256,384]{1,0:T(8,128)(2,1)S(1)} collective-permute-done((bf16[256,384]{1,0:T(8,128)(2,1)S(1)}, bf16[256,384]{1,0:T(8,128)(2,1)S(1)}, u32[]{:S(2)}, u32[]{:S(2)}) %collective-permute-start.7) | collective-permute-done | bytes 196640 | tf_op jit(solution)/shard_map/ppermute | solution.py:335
  46.7 7.5 %attention.1 = (bf16[128,384]{1,0:T(8,128)(2,1)S(1)}, bf16[128,384]{1,0:T(8,128)(2,1)S(1)}, bf16[256,384]{1,0:T(8,128)(2,1)S(1)}, bf16[256,384]{1,0:T(8,128)(2,1)S(1)}) custom-call(bf16[256,384]{1,0:T(8,128)(2,1)S(1)} %collective-permute-done.4.c0, bf16[256,384]{1,0:T(8,128)(2,1)S(1)} %collective-permute-done.5.c2, ...), custom_call_target="tpu_custom_call" | custom-call | flops 4000000000 | bytes 4000000 | tf_op jit(solution)/shard_map/attention/pallas_call | solution.py:306
  54.2 0.7 collective-permute-start.13
  54.9 0.9 %collective-permute-start.14 = (bf16[256,384]{1,0:T(8,128)(2,1)S(1)}, bf16[256,384]{1,0:T(8,128)(2,1)S(1)}, u32[]{:S(2)}, u32[]{:S(2)}) collective-permute-start(bf16[256,384]{1,0:T(8,128)(2,1)S(1)} %get-tuple-element.17), channel_id=1, source_target_pairs={{0,1},{1,0},{2,9},{3,8},{4,5},{5,4},{6,13},{7,12},{8,3},{9,2},{10,... | collective-permute-start | bytes 589832 | tf_op jit(solution)/shard_map/ppermute | solution.py:335
  55.8 6.3 %collective-permute-done.14.r1 = bf16[256,384]{1,0:T(8,128)(2,1)S(1)} collective-permute-done((bf16[256,384]{1,0:T(8,128)(2,1)S(1)}, bf16[256,384]{1,0:T(8,128)(2,1)S(1)}, u32[]{:S(2)}, u32[]{:S(2)}) %collective-permute-start.14) | collective-permute-done | bytes 196640 | tf_op jit(solution)/shard_map/ppermute | solution.py:335
  62.1 1.9 %shard_map.99 = (bf16[2,128,384]{2,1,0:T(8,128)(2,1)S(1)}, bf16[2,4,64,1152]{3,2,1,0:T(8,128)(2,1)S(1)}) custom-call(bf16[256,384]{1,0:T(8,128)(2,1)S(1)} %collective-permute-done.13.r0, bf16[256,384]{1,0:T(8,128)(2,1)S(1)} %collective-permute-done.14.r1, bf16[2,3,3,384,384]{4,3,2,1,0:T(8,128)(2,1)S(1)} %copy-done.1), custom_call_target="tpu_custom_call" | custom-call | flops 1000000000 | bytes 1048576 | tf_op jit(solution)/shard_map/pallas_call | solution.py:27
  64.1 8.5 %collective-permute-start.17 = (bf16[2,128,384]{2,1,0:T(8,128)(2,1)S(1)}, bf16[2,128,384]{2,1,0:T(8,128)(2,1)S(1)}, u32[]{:S(2)}, u32[]{:S(2)}) collective-permute-start(bf16[2,128,384]{2,1,0:T(8,128)(2,1)S(1)} %get-tuple-element.23), channel_id=1, source_target_pairs={{8,0},{16,8},{24,16},{32,24},{40,32},{48,40},{56,48},{64,56},{72,6... | collective-permute-start | bytes 589832 | tf_op jit(solution)/shard_map/ppermute | solution.py:410
  72.6 0.7 collective-permute-start.15
  73.3 2.7 %collective-permute-start.16 = (bf16[128,384]{1,0:T(8,128)(2,1)S(1)}, bf16[128,384]{1,0:T(8,128)(2,1)S(1)}, u32[]{:S(2)}, u32[]{:S(2)}) collective-permute-start(bf16[128,384]{1,0:T(8,128)(2,1)S(1)} %get-tuple-element.20), channel_id=1, source_target_pairs={{0,1},{1,0},{2,9},{3,8},{4,5},{5,4},{6,13},{7,12},{8,3},{9,2},{10,... | collective-permute-start | bytes 294920 | tf_op jit(solution)/shard_map/ppermute | solution.py:335
  76.0 3.5 %collective-permute-done.16.out1 = bf16[128,384]{1,0:T(8,128)(2,1)S(1)} collective-permute-done((bf16[128,384]{1,0:T(8,128)(2,1)S(1)}, bf16[128,384]{1,0:T(8,128)(2,1)S(1)}, u32[]{:S(2)}, u32[]{:S(2)}) %collective-permute-start.16) | collective-permute-done | bytes 98336 | tf_op jit(solution)/shard_map/ppermute | solution.py:335
  79.5 2.4 %shard_map.100 = (f32[2,128,384]{2,1,0:T(8,128)S(1)}, bf16[2,128,384]{2,1,0:T(8,128)(2,1)}) custom-call(bf16[2,4,64,1152]{3,2,1,0:T(8,128)(2,1)S(1)} %get-tuple-element.18.taps, bf16[128,384]{1,0:T(8,128)(2,1)S(1)} %collective-permute-done.15.out0, bf16[128,384]{1,0:T(8,128)(2,1)S(1)} %collective-permute-done.16.out1, ...), custom_call_target="tpu_custom_call" | custom-call | flops 1000000000 | bytes 1048576 | tf_op jit(solution)/shard_map/pallas_call | solution.py:27
  81.9 0.7 shard_map.101
  (32 shorter events, 0.6 us)
Async XLA Ops:
  0.6 16.7 %collective-permute-start = (bf16[256,384]{1,0:T(8,128)(2,1)}, bf16[256,384]{1,0:T(8,128)(2,1)S(1)}, u32[]{:S(2)}, u32[]{:S(2)}) collective-permute-start(bf16[256,384]{1,0:T(8,128)(2,1)} %bitcast.9), channel_id=1, source_target_pairs={{0,1},{1,0},{2,3},{3,2},{4,5},{5,4},{6,7},{7,6},{8,9},{9,8},{10,11... | collective-permute-start | bytes 589832 | tf_op jit(solution)/shard_map/ppermute | solution.py:335
  2.1 22.7 %collective-permute-start.8 = (bf16[2,128,384]{2,1,0:T(8,128)(2,1)}, bf16[2,128,384]{2,1,0:T(8,128)(2,1)S(1)}, u32[]{:S(2)}, u32[]{:S(2)}) collective-permute-start(bf16[2,128,384]{2,1,0:T(8,128)(2,1)} %bitcast.14), channel_id=1, source_target_pairs={{0,0},{1,1},{2,8},{3,9},{4,4},{5,5},{6,12},{7,13},{8,2},{9,3},{10,... | collective-permute-start | bytes 589832 | tf_op jit(solution)/shard_map/ppermute | solution.py:335
  4.6 12.4 %collective-permute-start.1 = (bf16[128,384]{1,0:T(8,128)(2,1)S(1)}, bf16[128,384]{1,0:T(8,128)(2,1)S(1)}, u32[]{:S(2)}, u32[]{:S(2)}) collective-permute-start(bf16[128,384]{1,0:T(8,128)(2,1)S(1)} %bitcast.12), channel_id=1, source_target_pairs={{1,3},{2,0},{3,5},{4,2},{5,7},{6,4},{9,11},{10,8},{11,13},{12,10},... | collective-permute-start | bytes 294920 | tf_op jit(solution)/shard_map/ppermute | solution.py:335
  8.5 8.9 %collective-permute-start.2 = (bf16[128,384]{1,0:T(8,128)(2,1)S(1)}, bf16[128,384]{1,0:T(8,128)(2,1)S(1)}, u32[]{:S(2)}, u32[]{:S(2)}) collective-permute-start(bf16[128,384]{1,0:T(8,128)(2,1)S(1)} %bitcast.13), channel_id=1, source_target_pairs={{1,2},{2,1},{3,4},{4,3},{5,6},{6,5},{9,10},{10,9},{11,12},{12,11},... | collective-permute-start | bytes 294920 | tf_op jit(solution)/shard_map/ppermute | solution.py:335
  12.0 5.4 %copy-start.2 = (bf16[2,2,64,384]{3,2,1,0:T(8,128)(2,1)S(1)}, bf16[2,2,64,384]{3,2,1,0:T(8,128)(2,1)}, u32[]{:S(2)}) copy-start(bf16[2,2,64,384]{3,2,1,0:T(8,128)(2,1)} %param.8) | copy-start | bytes 589828
  14.6 2.4 %copy-start = (bf16[2,3,3,384,384]{4,3,2,1,0:T(8,128)(2,1)}, bf16[2,3,3,384,384]{4,3,2,1,0:T(8,128)(2,1)S(1)}, u32[]{:S(2)}) copy-start(bf16[2,3,3,384,384]{4,3,2,1,0:T(8,128)(2,1)S(1)} %shard_map.95.w_ref) | copy-start | bytes 15925252
  17.4 2.5 %copy-start.1 = (bf16[2,3,3,384,384]{4,3,2,1,0:T(8,128)(2,1)S(1)}, bf16[2,3,3,384,384]{4,3,2,1,0:T(8,128)(2,1)}, u32[]{:S(2)}) copy-start(bf16[2,3,3,384,384]{4,3,2,1,0:T(8,128)(2,1)} %copy-done) | copy-start | bytes 15925252
  21.9 13.2 %collective-permute-start.3 = (bf16[256,384]{1,0:T(8,128)(2,1)S(1)}, bf16[256,384]{1,0:T(8,128)(2,1)S(1)}, u32[]{:S(2)}, u32[]{:S(2)}) collective-permute-start(bf16[256,384]{1,0:T(8,128)(2,1)S(1)} %get-tuple-element.15), channel_id=1, source_target_pairs={{0,8},{8,16},{16,24},{24,32},{32,40},{40,48},{48,56},{56,64},{64,7... | collective-permute-start | bytes 589832 | tf_op jit(solution)/shard_map/ppermute | solution.py:385
  24.9 7.2 %collective-permute-start.9 = (bf16[128,384]{1,0:T(8,128)(2,1)S(1)}, bf16[128,384]{1,0:T(8,128)(2,1)S(1)}, u32[]{:S(2)}, u32[]{:S(2)}) collective-permute-start(bf16[128,384]{1,0:T(8,128)(2,1)S(1)} %get-tuple-element.24), channel_id=1, source_target_pairs={{0,1},{1,0},{2,3},{3,2},{4,5},{5,4},{6,7},{7,6},{8,9},{9,8},{10,11... | collective-permute-start | bytes 294920 | tf_op jit(solution)/shard_map/ppermute | solution.py:335
  25.0 20.6 %copy-start.7 = (f32[384]{0:T(512)S(1)}, f32[384]{0:T(512)}, u32[]{:S(2)}) copy-start(f32[384]{0:T(512)} %param.10) | copy-start | bytes 4612
  25.0 21.6 %copy-start.3 = (bf16[384,384]{1,0:T(8,128)(2,1)S(1)}, bf16[384,384]{1,0:T(8,128)(2,1)}, u32[]{:S(2)}) copy-start(bf16[384,384]{1,0:T(8,128)(2,1)} %wq.1) | copy-start | bytes 884740
  25.0 21.6 %copy-start.4 = (bf16[384,384]{1,0:T(8,128)(2,1)S(1)}, bf16[384,384]{1,0:T(8,128)(2,1)}, u32[]{:S(2)}) copy-start(bf16[384,384]{1,0:T(8,128)(2,1)} %wk.1) | copy-start | bytes 884740
  25.0 21.6 %copy-start.5 = (bf16[384,384]{1,0:T(8,128)(2,1)S(1)}, bf16[384,384]{1,0:T(8,128)(2,1)}, u32[]{:S(2)}) copy-start(bf16[384,384]{1,0:T(8,128)(2,1)} %wv.1) | copy-start | bytes 884740
  25.1 21.6 %copy-start.6 = (bf16[384,384]{1,0:T(8,128)(2,1)S(1)}, bf16[384,384]{1,0:T(8,128)(2,1)}, u32[]{:S(2)}) copy-start(bf16[384,384]{1,0:T(8,128)(2,1)} %wo.1) | copy-start | bytes 884740
  32.2 9.3 %collective-permute-start.10 = (bf16[256,384]{1,0:T(8,128)(2,1)S(1)}, bf16[256,384]{1,0:T(8,128)(2,1)S(1)}, u32[]{:S(2)}, u32[]{:S(2)}) collective-permute-start(bf16[256,384]{1,0:T(8,128)(2,1)S(1)} %shard_map.98.t0), channel_id=1, source_target_pairs={{0,4},{1,5},{2,6},{3,7},{4,0},{5,1},{6,2},{7,3},{8,12},{9,13},{10,... | collective-permute-start | bytes 589832 | tf_op jit(solution)/shard_map/ppermute | solution.py:335
  35.1 6.4 %collective-permute-start.4 = (bf16[256,384]{1,0:T(8,128)(2,1)S(1)}, bf16[256,384]{1,0:T(8,128)(2,1)S(1)}, u32[]{:S(2)}, u32[]{:S(2)}) collective-permute-start(bf16[256,384]{1,0:T(8,128)(2,1)S(1)} %add_convert_fusion), channel_id=1, source_target_pairs={{0,0},{1,1},{2,8},{3,9},{4,4},{5,5},{6,12},{7,13},{8,2},{9,3},{10,... | collective-permute-start | bytes 589832 | tf_op jit(solution)/shard_map/ppermute | solution.py:335
  35.7 9.2 %collective-permute-start.5 = (bf16[256,384]{1,0:T(8,128)(2,1)S(1)}, bf16[256,384]{1,0:T(8,128)(2,1)S(1)}, u32[]{:S(2)}, u32[]{:S(2)}) collective-permute-start(bf16[256,384]{1,0:T(8,128)(2,1)S(1)} %add_convert_fusion), channel_id=1, source_target_pairs={{0,4},{1,5},{2,12},{3,13},{4,0},{5,1},{6,8},{7,9},{8,6},{9,7},{10,... | collective-permute-start | bytes 589832 | tf_op jit(solution)/shard_map/ppermute | solution.py:335
  37.6 8.0 %collective-permute-start.11 = (bf16[256,384]{1,0:T(8,128)(2,1)S(1)}, bf16[256,384]{1,0:T(8,128)(2,1)S(1)}, u32[]{:S(2)}, u32[]{:S(2)}) collective-permute-start(bf16[256,384]{1,0:T(8,128)(2,1)S(1)} %shard_map.98.t0), channel_id=1, source_target_pairs={{0,8},{1,9},{2,10},{3,11},{4,12},{5,13},{6,14},{7,15},{8,0},{9,1},... | collective-permute-start | bytes 589832 | tf_op jit(solution)/shard_map/ppermute | solution.py:335
  41.5 4.1 %collective-permute-start.12 = (bf16[256,384]{1,0:T(8,128)(2,1)S(1)}, bf16[256,384]{1,0:T(8,128)(2,1)S(1)}, u32[]{:S(2)}, u32[]{:S(2)}) collective-permute-start(bf16[256,384]{1,0:T(8,128)(2,1)S(1)} %collective-permute-done.10.t2), channel_id=1, source_target_pairs={{0,8},{1,9},{2,10},{3,11},{4,12},{5,13},{6,14},{7,15},{8,0},{9,1},... | collective-permute-start | bytes 589832 | tf_op jit(solution)/shard_map/ppermute | solution.py:335
  41.5 4.1 %collective-permute-start.6 = (bf16[256,384]{1,0:T(8,128)(2,1)S(1)}, bf16[256,384]{1,0:T(8,128)(2,1)S(1)}, u32[]{:S(2)}, u32[]{:S(2)}) collective-permute-start(bf16[256,384]{1,0:T(8,128)(2,1)S(1)} %collective-permute-done.4.c0), channel_id=1, source_target_pairs={{0,8},{1,9},{2,10},{3,11},{4,12},{5,13},{6,14},{7,15},{8,0},{9,1},... | collective-permute-start | bytes 589832 | tf_op jit(solution)/shard_map/ppermute | solution.py:335
  45.0 1.7 %collective-permute-start.7 = (bf16[256,384]{1,0:T(8,128)(2,1)S(1)}, bf16[256,384]{1,0:T(8,128)(2,1)S(1)}, u32[]{:S(2)}, u32[]{:S(2)}) collective-permute-start(bf16[256,384]{1,0:T(8,128)(2,1)S(1)} %collective-permute-done.5.c2), channel_id=1, source_target_pairs={{0,8},{1,9},{2,10},{3,11},{4,12},{5,13},{6,14},{7,15},{8,0},{9,1},... | collective-permute-start | bytes 589832 | tf_op jit(solution)/shard_map/ppermute | solution.py:335
  54.2 1.6 %collective-permute-start.13 = (bf16[256,384]{1,0:T(8,128)(2,1)S(1)}, bf16[256,384]{1,0:T(8,128)(2,1)S(1)}, u32[]{:S(2)}, u32[]{:S(2)}) collective-permute-start(bf16[256,384]{1,0:T(8,128)(2,1)S(1)} %get-tuple-element.16), channel_id=1, source_target_pairs={{0,0},{1,1},{2,8},{3,9},{4,4},{5,5},{6,12},{7,13},{8,2},{9,3},{10,... | collective-permute-start | bytes 589832 | tf_op jit(solution)/shard_map/ppermute | solution.py:335
  54.9 7.3 %collective-permute-start.14 = (bf16[256,384]{1,0:T(8,128)(2,1)S(1)}, bf16[256,384]{1,0:T(8,128)(2,1)S(1)}, u32[]{:S(2)}, u32[]{:S(2)}) collective-permute-start(bf16[256,384]{1,0:T(8,128)(2,1)S(1)} %get-tuple-element.17), channel_id=1, source_target_pairs={{0,1},{1,0},{2,9},{3,8},{4,5},{5,4},{6,13},{7,12},{8,3},{9,2},{10,... | collective-permute-start | bytes 589832 | tf_op jit(solution)/shard_map/ppermute | solution.py:335
  64.1 17.8 %collective-permute-start.17 = (bf16[2,128,384]{2,1,0:T(8,128)(2,1)S(1)}, bf16[2,128,384]{2,1,0:T(8,128)(2,1)S(1)}, u32[]{:S(2)}, u32[]{:S(2)}) collective-permute-start(bf16[2,128,384]{2,1,0:T(8,128)(2,1)S(1)} %get-tuple-element.23), channel_id=1, source_target_pairs={{8,0},{16,8},{24,16},{32,24},{40,32},{48,40},{56,48},{64,56},{72,6... | collective-permute-start | bytes 589832 | tf_op jit(solution)/shard_map/ppermute | solution.py:410
  72.6 3.4 %collective-permute-start.15 = (bf16[128,384]{1,0:T(8,128)(2,1)S(1)}, bf16[128,384]{1,0:T(8,128)(2,1)S(1)}, u32[]{:S(2)}, u32[]{:S(2)}) collective-permute-start(bf16[128,384]{1,0:T(8,128)(2,1)S(1)} %get-tuple-element.19), channel_id=1, source_target_pairs={{0,0},{1,1},{2,8},{3,9},{4,4},{5,5},{6,12},{7,13},{8,2},{9,3},{10,... | collective-permute-start | bytes 294920 | tf_op jit(solution)/shard_map/ppermute | solution.py:335
  73.3 6.2 %collective-permute-start.16 = (bf16[128,384]{1,0:T(8,128)(2,1)S(1)}, bf16[128,384]{1,0:T(8,128)(2,1)S(1)}, u32[]{:S(2)}, u32[]{:S(2)}) collective-permute-start(bf16[128,384]{1,0:T(8,128)(2,1)S(1)} %get-tuple-element.20), channel_id=1, source_target_pairs={{0,1},{1,0},{2,9},{3,8},{4,5},{5,4},{6,13},{7,12},{8,3},{9,2},{10,... | collective-permute-start | bytes 294920 | tf_op jit(solution)/shard_map/ppermute | solution.py:335

commit v7 on v6

--- a/solution.py
+++ b/solution.py
@@ -60,21 +60,27 @@
     )[0]
 
 
-def finish_kernel(own, handed, video_grad, total, sems):
-    copies = []
+def finish_kernel(own, handed, out0, out1, video_grad, block_out, total, sems):
+    x, _ = seat()
+    copies = [
+        pltpu.make_async_copy(out0, block_out.at[x], sems.at[2]),
+        pltpu.make_async_copy(out1, block_out.at[1 - x], sems.at[3]),
+    ]
+    for copy in copies:
+        copy.start()
     for f in range(2):
         total[f] = (own[f] + handed[f].astype(F32)).astype(BF16)
         copies.append(pltpu.make_async_copy(total.at[f], video_grad.at[f], sems.at[f]))
-        copies[f].start()
+        copies[-1].start()
     for copy in copies:
         copy.wait()
 
 
-def finish(own, handed):
+def finish(own, handed, out0, out1):
     return call(
-        finish_kernel, (own, handed), [VM, VM], [(own.shape, BF16)],
-        [pltpu.VMEM(own.shape, BF16), pltpu.SemaphoreType.DMA((2,))], 8 * MIB, outs=HBM,
-    )[0]
+        finish_kernel, (own, handed, out0, out1), [VM] * 4, [(own.shape, BF16)] * 2,
+        [pltpu.VMEM(own.shape, BF16), pltpu.SemaphoreType.DMA((4,))], 8 * MIB, outs=HBM,
+    )
 
 
 def spread(rows_f32, width):
@@ -178,17 +184,8 @@
     conv_steps(taps, w_ref.at[0], w_ref.at[1], out, 0, 1)
 
 
-def grad_own_kernel(taps, out0, out1, w_ref, w_last, out, block_out, sems):
-    x, _ = seat()
-    copies = [
-        pltpu.make_async_copy(out0, block_out.at[x], sems.at[0]),
-        pltpu.make_async_copy(out1, block_out.at[1 - x], sems.at[1]),
-    ]
-    for copy in copies:
-        copy.start()
+def grad_own_kernel(taps, w_ref, w_last, out):
     conv_steps(taps, w_last, w_ref.at[1], out, 1, 0)
-    for copy in copies:
-        copy.wait()
 
 
 def norm_parts(conv, gain):
@@ -408,13 +405,11 @@
         24 * MIB, 10**9,
     )
     handed = lax.ppermute(for_last, "tm", [(i + 1, i) for i in range(runs - 1)])
-    own_grad, block_out = call(
-        grad_own_kernel, (taps, out0, out1, weight, w_last), [VM] * 5,
-        [((2, block, chans), F32), ((2, block, chans), BF16)],
-        [pltpu.SemaphoreType.DMA((2,))],
-        24 * MIB, 10**9, outs=(VM, HBM),
-    )
-    video_grad = finish(own_grad, handed)
+    own_grad = call(
+        grad_own_kernel, (taps, weight, w_last), [VM] * 3, [((2, block, chans), F32)], [],
+        24 * MIB, 10**9,
+    )[0]
+    video_grad, block_out = finish(own_grad, handed, out0, out1)
     return block_out.reshape(video.shape), video_grad.reshape(video.shape)
 
 

time: 84.4 us -> 82 us (0.972)
  waiting for transfers between devices: 21.4 us -> 19.5 us
    ppermute x16, waiting for transfers between devices: 21.4 us -> 19.5 us  [send(): return lax.ppermute(value, ('tm', 'rows'), pairs)]
where the time goes in v7:
time: 82 us; the launch traced here: 80.4 us
  starting transfers between devices  35.1 us (43%)
  waiting for transfers between devices  19.5 us (24%)
  Pallas kernels  18.9 us (23%)
  local copies, waits for them, and re-layouts  5.83 us (7%)
  between operations  1.02 us (1%)
    ppermute x16, starting transfers between devices, send(): return lax.ppermute(value, ('tm', 'rows'), pairs)  23.6 us
    ppermute x16, waiting for transfers between devices, send(): return lax.ppermute(value, ('tm', 'rows'), pairs)  19.5 us
    pallas_call x7, Pallas kernels, call(): pl.pallas_call(kernel, in_specs=specs, out_specs=list(outs) if isinstance...  11.4 us
    ppermute x1, starting transfers between devices, local(): handed = lax.ppermute(for_last, 'tm', [(i + 1, i) for i in range(runs - 1)])  8.52 us
    pallas_call x1, Pallas kernels, attention(): pl.pallas_call(attention_kernel, in_specs=[VM] * (len(convs) + len(cots)...  7.53 us
    unnamed x16, local copies, waits for them, and re-layouts  4.9 us
    ppermute x1, starting transfers between devices, local(): cached = lax.ppermute(for_next, 'tm', [(i, i + 1) for i in range(runs - 1)])  3 us
  transfers between devices with their start and end apart: 18, of which 7 were waited for; matrix products, arithmetic and copies ran while one was open for 1% of the time, Pallas kernels for 11%

profile of v7, /device:TPU:6, one launch (start us, length us, event | category | flops | bytes accessed | tf_op | source)
XLA Modules:
  0.0 80.4 jit_solution(7878882440856153900)
XLA Ops:
  0.6 1.5 %collective-permute-start = (bf16[256,384]{1,0:T(8,128)(2,1)}, bf16[256,384]{1,0:T(8,128)(2,1)S(1)}, u32[]{:S(2)}, u32[]{:S(2)}) collective-permute-start(bf16[256,384]{1,0:T(8,128)(2,1)} %bitcast.9), channel_id=1, source_target_pairs={{0,1},{1,0},{2,3},{3,2},{4,5},{5,4},{6,7},{7,6},{8,9},{9,8},{10,11... | collective-permute-start | bytes 589832 | tf_op jit(solution)/shard_map/ppermute | solution.py:332
  2.1 1.6 %collective-permute-start.8 = (bf16[2,128,384]{2,1,0:T(8,128)(2,1)}, bf16[2,128,384]{2,1,0:T(8,128)(2,1)S(1)}, u32[]{:S(2)}, u32[]{:S(2)}) collective-permute-start(bf16[2,128,384]{2,1,0:T(8,128)(2,1)} %bitcast.13), channel_id=1, source_target_pairs={{0,0},{1,1},{2,8},{3,9},{4,4},{5,5},{6,12},{7,13},{8,2},{9,3},{10,... | collective-permute-start | bytes 589832 | tf_op jit(solution)/shard_map/ppermute | solution.py:332
  3.7 0.9 %constant_dynamic-slice_fusion = bf16[2,1,64,384]{3,2,1,0:T(8,128)(2,1)S(1)} fusion(bf16[2,2,64,384]{3,2,1,0:T(8,128)(2,1)} %param.8, s32[]{:T(128)S(6)} %select_n.9), kind=kLoop, calls=%fused_computation.3 | loop fusion | bytes 196612 | tf_op jit(solution)/shard_map/jit(dynamic_index_in_dim)/dynamic_slice | solution.py:364
  4.6 3.8 %collective-permute-start.1 = (bf16[128,384]{1,0:T(8,128)(2,1)S(1)}, bf16[128,384]{1,0:T(8,128)(2,1)S(1)}, u32[]{:S(2)}, u32[]{:S(2)}) collective-permute-start(bf16[128,384]{1,0:T(8,128)(2,1)S(1)} %bitcast.11), channel_id=1, source_target_pairs={{1,3},{2,0},{3,5},{4,2},{5,7},{6,4},{9,11},{10,8},{11,13},{12,10},... | collective-permute-start | bytes 294920 | tf_op jit(solution)/shard_map/ppermute | solution.py:332
  8.5 3.6 %collective-permute-start.2 = (bf16[128,384]{1,0:T(8,128)(2,1)S(1)}, bf16[128,384]{1,0:T(8,128)(2,1)S(1)}, u32[]{:S(2)}, u32[]{:S(2)}) collective-permute-start(bf16[128,384]{1,0:T(8,128)(2,1)S(1)} %bitcast.12), channel_id=1, source_target_pairs={{1,2},{2,1},{3,4},{4,3},{5,6},{6,5},{9,10},{10,9},{11,12},{12,11},... | collective-permute-start | bytes 294920 | tf_op jit(solution)/shard_map/ppermute | solution.py:332
  12.0 2.6 %shard_map.95.w_ref = bf16[2,3,3,384,384]{4,3,2,1,0:T(8,128)(2,1)S(1)} custom-call(bf16[3,3,3,384,384]{4,3,2,1,0:T(8,128)(2,1)} %w_hbm.3), custom_call_target="tpu_custom_call" | custom-call | bytes 1048576 | tf_op jit(solution)/shard_map/pallas_call | solution.py:27
  14.6 2.4 %copy-done = bf16[2,3,3,384,384]{4,3,2,1,0:T(8,128)(2,1)} copy-done((bf16[2,3,3,384,384]{4,3,2,1,0:T(8,128)(2,1)}, bf16[2,3,3,384,384]{4,3,2,1,0:T(8,128)(2,1)S(1)}, u32[]{:S(2)}) %copy-start) | copy-done | bytes 5308440
  17.0 0.4 collective-permute-done.2.far_other
  17.4 2.5 %copy-done.1 = bf16[2,3,3,384,384]{4,3,2,1,0:T(8,128)(2,1)S(1)} copy-done((bf16[2,3,3,384,384]{4,3,2,1,0:T(8,128)(2,1)S(1)}, bf16[2,3,3,384,384]{4,3,2,1,0:T(8,128)(2,1)}, u32[]{:S(2)}) %copy-start.1) | copy-done | bytes 5308440
  19.9 2.0 %shard_map.96 = (bf16[256,384]{1,0:T(8,128)(2,1)S(1)}, bf16[2,6,64,1152]{3,2,1,0:T(8,128)(2,1)S(1)}, bf16[3,3,384,384]{3,2,1,0:T(8,128)(2,1)S(1)}) custom-call(bf16[256,384]{1,0:T(8,128)(2,1)S(1)} %bitcast.10, bf16[256,384]{1,0:T(8,128)(2,1)S(1)} %collective-permute-done.packet, bf16[128,384]{1,0:T(8,128)(2,1)S(1)} %collective-permute-done.1.far_same, ...), custom_call_target="tpu_custom_call" | custom-call | flops 1000000000 | bytes 1048576 | tf_op jit(solution)/shard_map/pallas_call | solution.py:27
  21.9 3.0 %collective-permute-start.3 = (bf16[256,384]{1,0:T(8,128)(2,1)S(1)}, bf16[256,384]{1,0:T(8,128)(2,1)S(1)}, u32[]{:S(2)}, u32[]{:S(2)}) collective-permute-start(bf16[256,384]{1,0:T(8,128)(2,1)S(1)} %get-tuple-element.15), channel_id=1, source_target_pairs={{0,8},{8,16},{16,24},{24,32},{32,40},{40,48},{48,56},{56,64},{64,7... | collective-permute-start | bytes 589832 | tf_op jit(solution)/shard_map/ppermute | solution.py:382
  25.1 2.3 %shard_map.97 = f32[256,384]{1,0:T(8,128)S(1)} custom-call(bf16[2,6,64,1152]{3,2,1,0:T(8,128)(2,1)S(1)} %get-tuple-element.13.taps, bf16[2,3,3,384,384]{4,3,2,1,0:T(8,128)(2,1)S(1)} %copy-done.1, bf16[3,3,384,384]{3,2,1,0:T(8,128)(2,1)S(1)} %get-tuple-element.14.w_last), custom_call_target="tpu_custom_call" | custom-call | flops 1000000000 | bytes 1048576 | tf_op jit(solution)/shard_map/pallas_call | solution.py:27
  27.3 4.8 %collective-permute-done.9.other = bf16[128,384]{1,0:T(8,128)(2,1)S(1)} collective-permute-done((bf16[128,384]{1,0:T(8,128)(2,1)S(1)}, bf16[128,384]{1,0:T(8,128)(2,1)S(1)}, u32[]{:S(2)}, u32[]{:S(2)}) %collective-permute-start.9) | collective-permute-done | bytes 98336 | tf_op jit(solution)/shard_map/ppermute | solution.py:332
  32.2 2.8 %collective-permute-start.10 = (bf16[256,384]{1,0:T(8,128)(2,1)S(1)}, bf16[256,384]{1,0:T(8,128)(2,1)S(1)}, u32[]{:S(2)}, u32[]{:S(2)}) collective-permute-start(bf16[256,384]{1,0:T(8,128)(2,1)S(1)} %shard_map.98.t0), channel_id=1, source_target_pairs={{0,4},{1,5},{2,6},{3,7},{4,0},{5,1},{6,2},{7,3},{8,12},{9,13},{10,... | collective-permute-start | bytes 589832 | tf_op jit(solution)/shard_map/ppermute | solution.py:332
  35.1 0.7 collective-permute-start.4
  35.7 1.9 %collective-permute-start.5 = (bf16[256,384]{1,0:T(8,128)(2,1)S(1)}, bf16[256,384]{1,0:T(8,128)(2,1)S(1)}, u32[]{:S(2)}, u32[]{:S(2)}) collective-permute-start(bf16[256,384]{1,0:T(8,128)(2,1)S(1)} %add_convert_fusion), channel_id=1, source_target_pairs={{0,4},{1,5},{2,12},{3,13},{4,0},{5,1},{6,8},{7,9},{8,6},{9,7},{10,... | collective-permute-start | bytes 589832 | tf_op jit(solution)/shard_map/ppermute | solution.py:332
  37.9 3.6 %collective-permute-done.10.t2 = bf16[256,384]{1,0:T(8,128)(2,1)S(1)} collective-permute-done((bf16[256,384]{1,0:T(8,128)(2,1)S(1)}, bf16[256,384]{1,0:T(8,128)(2,1)S(1)}, u32[]{:S(2)}, u32[]{:S(2)}) %collective-permute-start.10) | collective-permute-done | bytes 196640 | tf_op jit(solution)/shard_map/ppermute | solution.py:332
  41.5 1.8 %collective-permute-start.6 = (bf16[256,384]{1,0:T(8,128)(2,1)S(1)}, bf16[256,384]{1,0:T(8,128)(2,1)S(1)}, u32[]{:S(2)}, u32[]{:S(2)}) collective-permute-start(bf16[256,384]{1,0:T(8,128)(2,1)S(1)} %collective-permute-done.4.c0), channel_id=1, source_target_pairs={{0,8},{1,9},{2,10},{3,11},{4,12},{5,13},{6,14},{7,15},{8,0},{9,1},... | collective-permute-start | bytes 589832 | tf_op jit(solution)/shard_map/ppermute | solution.py:332
  43.3 1.7 %collective-permute-done.5.c2 = bf16[256,384]{1,0:T(8,128)(2,1)S(1)} collective-permute-done((bf16[256,384]{1,0:T(8,128)(2,1)S(1)}, bf16[256,384]{1,0:T(8,128)(2,1)S(1)}, u32[]{:S(2)}, u32[]{:S(2)}) %collective-permute-start.5) | collective-permute-done | bytes 196640 | tf_op jit(solution)/shard_map/ppermute | solution.py:332
  45.0 0.6 collective-permute-start.7
  45.6 1.0 %collective-permute-done.7.c3 = bf16[256,384]{1,0:T(8,128)(2,1)S(1)} collective-permute-done((bf16[256,384]{1,0:T(8,128)(2,1)S(1)}, bf16[256,384]{1,0:T(8,128)(2,1)S(1)}, u32[]{:S(2)}, u32[]{:S(2)}) %collective-permute-start.7) | collective-permute-done | bytes 196640 | tf_op jit(solution)/shard_map/ppermute | solution.py:332
  46.7 7.5 %attention.1 = (bf16[128,384]{1,0:T(8,128)(2,1)S(1)}, bf16[128,384]{1,0:T(8,128)(2,1)S(1)}, bf16[256,384]{1,0:T(8,128)(2,1)S(1)}, bf16[256,384]{1,0:T(8,128)(2,1)S(1)}) custom-call(bf16[256,384]{1,0:T(8,128)(2,1)S(1)} %collective-permute-done.4.c0, bf16[256,384]{1,0:T(8,128)(2,1)S(1)} %collective-permute-done.5.c2, ...), custom_call_target="tpu_custom_call" | custom-call | flops 4000000000 | bytes 4000000 | tf_op jit(solution)/shard_map/attention/pallas_call | solution.py:303
  54.2 0.7 collective-permute-start.13
  54.9 0.9 %collective-permute-start.14 = (bf16[256,384]{1,0:T(8,128)(2,1)S(1)}, bf16[256,384]{1,0:T(8,128)(2,1)S(1)}, u32[]{:S(2)}, u32[]{:S(2)}) collective-permute-start(bf16[256,384]{1,0:T(8,128)(2,1)S(1)} %get-tuple-element.17), channel_id=1, source_target_pairs={{0,1},{1,0},{2,9},{3,8},{4,5},{5,4},{6,13},{7,12},{8,3},{9,2},{10,... | collective-permute-start | bytes 589832 | tf_op jit(solution)/shard_map/ppermute | solution.py:332
  55.8 6.3 %collective-permute-done.14.r1 = bf16[256,384]{1,0:T(8,128)(2,1)S(1)} collective-permute-done((bf16[256,384]{1,0:T(8,128)(2,1)S(1)}, bf16[256,384]{1,0:T(8,128)(2,1)S(1)}, u32[]{:S(2)}, u32[]{:S(2)}) %collective-permute-start.14) | collective-permute-done | bytes 196640 | tf_op jit(solution)/shard_map/ppermute | solution.py:332
  62.1 1.9 %shard_map.99 = (bf16[2,128,384]{2,1,0:T(8,128)(2,1)S(1)}, bf16[2,4,64,1152]{3,2,1,0:T(8,128)(2,1)S(1)}) custom-call(bf16[256,384]{1,0:T(8,128)(2,1)S(1)} %collective-permute-done.13.r0, bf16[256,384]{1,0:T(8,128)(2,1)S(1)} %collective-permute-done.14.r1, bf16[2,3,3,384,384]{4,3,2,1,0:T(8,128)(2,1)S(1)} %copy-done.1), custom_call_target="tpu_custom_call" | custom-call | flops 1000000000 | bytes 1048576 | tf_op jit(solution)/shard_map/pallas_call | solution.py:27
  64.1 8.5 %collective-permute-start.15 = (bf16[2,128,384]{2,1,0:T(8,128)(2,1)S(1)}, bf16[2,128,384]{2,1,0:T(8,128)(2,1)S(1)}, u32[]{:S(2)}, u32[]{:S(2)}) collective-permute-start(bf16[2,128,384]{2,1,0:T(8,128)(2,1)S(1)} %get-tuple-element.19), channel_id=1, source_target_pairs={{8,0},{16,8},{24,16},{32,24},{40,32},{48,40},{56,48},{64,56},{72,6... | collective-permute-start | bytes 589832 | tf_op jit(solution)/shard_map/ppermute | solution.py:407
  72.6 0.7 collective-permute-start.16
  73.3 2.7 %collective-permute-start.17 = (bf16[128,384]{1,0:T(8,128)(2,1)S(1)}, bf16[128,384]{1,0:T(8,128)(2,1)S(1)}, u32[]{:S(2)}, u32[]{:S(2)}) collective-permute-start(bf16[128,384]{1,0:T(8,128)(2,1)S(1)} %get-tuple-element.21), channel_id=1, source_target_pairs={{0,1},{1,0},{2,9},{3,8},{4,5},{5,4},{6,13},{7,12},{8,3},{9,2},{10,... | collective-permute-start | bytes 294920 | tf_op jit(solution)/shard_map/ppermute | solution.py:332
  76.0 1.9 %shard_map.100.own = f32[2,128,384]{2,1,0:T(8,128)S(1)} custom-call(bf16[2,4,64,1152]{3,2,1,0:T(8,128)(2,1)S(1)} %get-tuple-element.18.taps, bf16[2,3,3,384,384]{4,3,2,1,0:T(8,128)(2,1)S(1)} %copy-done.1, bf16[3,3,384,384]{3,2,1,0:T(8,128)(2,1)S(1)} %get-tuple-element.14.w_last), custom_call_target="tpu_custom_call" | custom-call | flops 1000000000 | bytes 1048576 | tf_op jit(solution)/shard_map/pallas_call | solution.py:27
  77.9 1.6 %collective-permute-done.17.out1 = bf16[128,384]{1,0:T(8,128)(2,1)S(1)} collective-permute-done((bf16[128,384]{1,0:T(8,128)(2,1)S(1)}, bf16[128,384]{1,0:T(8,128)(2,1)S(1)}, u32[]{:S(2)}, u32[]{:S(2)}) %collective-permute-start.17) | collective-permute-done | bytes 98336 | tf_op jit(solution)/shard_map/ppermute | solution.py:332
  79.5 0.8 shard_map.101
  (32 shorter events, 0.6 us)
Async XLA Ops:
  0.6 16.7 %collective-permute-start = (bf16[256,384]{1,0:T(8,128)(2,1)}, bf16[256,384]{1,0:T(8,128)(2,1)S(1)}, u32[]{:S(2)}, u32[]{:S(2)}) collective-permute-start(bf16[256,384]{1,0:T(8,128)(2,1)} %bitcast.9), channel_id=1, source_target_pairs={{0,1},{1,0},{2,3},{3,2},{4,5},{5,4},{6,7},{7,6},{8,9},{9,8},{10,11... | collective-permute-start | bytes 589832 | tf_op jit(solution)/shard_map/ppermute | solution.py:332
  2.1 22.7 %collective-permute-start.8 = (bf16[2,128,384]{2,1,0:T(8,128)(2,1)}, bf16[2,128,384]{2,1,0:T(8,128)(2,1)S(1)}, u32[]{:S(2)}, u32[]{:S(2)}) collective-permute-start(bf16[2,128,384]{2,1,0:T(8,128)(2,1)} %bitcast.13), channel_id=1, source_target_pairs={{0,0},{1,1},{2,8},{3,9},{4,4},{5,5},{6,12},{7,13},{8,2},{9,3},{10,... | collective-permute-start | bytes 589832 | tf_op jit(solution)/shard_map/ppermute | solution.py:332
  4.6 12.4 %collective-permute-start.1 = (bf16[128,384]{1,0:T(8,128)(2,1)S(1)}, bf16[128,384]{1,0:T(8,128)(2,1)S(1)}, u32[]{:S(2)}, u32[]{:S(2)}) collective-permute-start(bf16[128,384]{1,0:T(8,128)(2,1)S(1)} %bitcast.11), channel_id=1, source_target_pairs={{1,3},{2,0},{3,5},{4,2},{5,7},{6,4},{9,11},{10,8},{11,13},{12,10},... | collective-permute-start | bytes 294920 | tf_op jit(solution)/shard_map/ppermute | solution.py:332
  8.5 8.9 %collective-permute-start.2 = (bf16[128,384]{1,0:T(8,128)(2,1)S(1)}, bf16[128,384]{1,0:T(8,128)(2,1)S(1)}, u32[]{:S(2)}, u32[]{:S(2)}) collective-permute-start(bf16[128,384]{1,0:T(8,128)(2,1)S(1)} %bitcast.12), channel_id=1, source_target_pairs={{1,2},{2,1},{3,4},{4,3},{5,6},{6,5},{9,10},{10,9},{11,12},{12,11},... | collective-permute-start | bytes 294920 | tf_op jit(solution)/shard_map/ppermute | solution.py:332
  12.0 5.4 %copy-start.2 = (bf16[2,2,64,384]{3,2,1,0:T(8,128)(2,1)S(1)}, bf16[2,2,64,384]{3,2,1,0:T(8,128)(2,1)}, u32[]{:S(2)}) copy-start(bf16[2,2,64,384]{3,2,1,0:T(8,128)(2,1)} %param.8) | copy-start | bytes 589828
  14.6 2.4 %copy-start = (bf16[2,3,3,384,384]{4,3,2,1,0:T(8,128)(2,1)}, bf16[2,3,3,384,384]{4,3,2,1,0:T(8,128)(2,1)S(1)}, u32[]{:S(2)}) copy-start(bf16[2,3,3,384,384]{4,3,2,1,0:T(8,128)(2,1)S(1)} %shard_map.95.w_ref) | copy-start | bytes 15925252
  17.4 2.5 %copy-start.1 = (bf16[2,3,3,384,384]{4,3,2,1,0:T(8,128)(2,1)S(1)}, bf16[2,3,3,384,384]{4,3,2,1,0:T(8,128)(2,1)}, u32[]{:S(2)}) copy-start(bf16[2,3,3,384,384]{4,3,2,1,0:T(8,128)(2,1)} %copy-done) | copy-start | bytes 15925252
  21.9 13.2 %collective-permute-start.3 = (bf16[256,384]{1,0:T(8,128)(2,1)S(1)}, bf16[256,384]{1,0:T(8,128)(2,1)S(1)}, u32[]{:S(2)}, u32[]{:S(2)}) collective-permute-start(bf16[256,384]{1,0:T(8,128)(2,1)S(1)} %get-tuple-element.15), channel_id=1, source_target_pairs={{0,8},{8,16},{16,24},{24,32},{32,40},{40,48},{48,56},{56,64},{64,7... | collective-permute-start | bytes 589832 | tf_op jit(solution)/shard_map/ppermute | solution.py:382
  24.9 7.2 %collective-permute-start.9 = (bf16[128,384]{1,0:T(8,128)(2,1)S(1)}, bf16[128,384]{1,0:T(8,128)(2,1)S(1)}, u32[]{:S(2)}, u32[]{:S(2)}) collective-permute-start(bf16[128,384]{1,0:T(8,128)(2,1)S(1)} %get-tuple-element.24), channel_id=1, source_target_pairs={{0,1},{1,0},{2,3},{3,2},{4,5},{5,4},{6,7},{7,6},{8,9},{9,8},{10,11... | collective-permute-start | bytes 294920 | tf_op jit(solution)/shard_map/ppermute | solution.py:332
  25.0 20.6 %copy-start.7 = (f32[384]{0:T(512)S(1)}, f32[384]{0:T(512)}, u32[]{:S(2)}) copy-start(f32[384]{0:T(512)} %param.10) | copy-start | bytes 4612
  25.0 21.6 %copy-start.3 = (bf16[384,384]{1,0:T(8,128)(2,1)S(1)}, bf16[384,384]{1,0:T(8,128)(2,1)}, u32[]{:S(2)}) copy-start(bf16[384,384]{1,0:T(8,128)(2,1)} %wq.1) | copy-start | bytes 884740
  25.0 21.6 %copy-start.4 = (bf16[384,384]{1,0:T(8,128)(2,1)S(1)}, bf16[384,384]{1,0:T(8,128)(2,1)}, u32[]{:S(2)}) copy-start(bf16[384,384]{1,0:T(8,128)(2,1)} %wk.1) | copy-start | bytes 884740
  25.0 21.6 %copy-start.5 = (bf16[384,384]{1,0:T(8,128)(2,1)S(1)}, bf16[384,384]{1,0:T(8,128)(2,1)}, u32[]{:S(2)}) copy-start(bf16[384,384]{1,0:T(8,128)(2,1)} %wv.1) | copy-start | bytes 884740
  25.1 21.6 %copy-start.6 = (bf16[384,384]{1,0:T(8,128)(2,1)S(1)}, bf16[384,384]{1,0:T(8,128)(2,1)}, u32[]{:S(2)}) copy-start(bf16[384,384]{1,0:T(8,128)(2,1)} %wo.1) | copy-start | bytes 884740
  32.2 9.3 %collective-permute-start.10 = (bf16[256,384]{1,0:T(8,128)(2,1)S(1)}, bf16[256,384]{1,0:T(8,128)(2,1)S(1)}, u32[]{:S(2)}, u32[]{:S(2)}) collective-permute-start(bf16[256,384]{1,0:T(8,128)(2,1)S(1)} %shard_map.98.t0), channel_id=1, source_target_pairs={{0,4},{1,5},{2,6},{3,7},{4,0},{5,1},{6,2},{7,3},{8,12},{9,13},{10,... | collective-permute-start | bytes 589832 | tf_op jit(solution)/shard_map/ppermute | solution.py:332
  35.1 6.4 %collective-permute-start.4 = (bf16[256,384]{1,0:T(8,128)(2,1)S(1)}, bf16[256,384]{1,0:T(8,128)(2,1)S(1)}, u32[]{:S(2)}, u32[]{:S(2)}) collective-permute-start(bf16[256,384]{1,0:T(8,128)(2,1)S(1)} %add_convert_fusion), channel_id=1, source_target_pairs={{0,0},{1,1},{2,8},{3,9},{4,4},{5,5},{6,12},{7,13},{8,2},{9,3},{10,... | collective-permute-start | bytes 589832 | tf_op jit(solution)/shard_map/ppermute | solution.py:332
  35.7 9.2 %collective-permute-start.5 = (bf16[256,384]{1,0:T(8,128)(2,1)S(1)}, bf16[256,384]{1,0:T(8,128)(2,1)S(1)}, u32[]{:S(2)}, u32[]{:S(2)}) collective-permute-start(bf16[256,384]{1,0:T(8,128)(2,1)S(1)} %add_convert_fusion), channel_id=1, source_target_pairs={{0,4},{1,5},{2,12},{3,13},{4,0},{5,1},{6,8},{7,9},{8,6},{9,7},{10,... | collective-permute-start | bytes 589832 | tf_op jit(solution)/shard_map/ppermute | solution.py:332
  37.6 8.0 %collective-permute-start.11 = (bf16[256,384]{1,0:T(8,128)(2,1)S(1)}, bf16[256,384]{1,0:T(8,128)(2,1)S(1)}, u32[]{:S(2)}, u32[]{:S(2)}) collective-permute-start(bf16[256,384]{1,0:T(8,128)(2,1)S(1)} %shard_map.98.t0), channel_id=1, source_target_pairs={{0,8},{1,9},{2,10},{3,11},{4,12},{5,13},{6,14},{7,15},{8,0},{9,1},... | collective-permute-start | bytes 589832 | tf_op jit(solution)/shard_map/ppermute | solution.py:332
  41.5 4.1 %collective-permute-start.12 = (bf16[256,384]{1,0:T(8,128)(2,1)S(1)}, bf16[256,384]{1,0:T(8,128)(2,1)S(1)}, u32[]{:S(2)}, u32[]{:S(2)}) collective-permute-start(bf16[256,384]{1,0:T(8,128)(2,1)S(1)} %collective-permute-done.10.t2), channel_id=1, source_target_pairs={{0,8},{1,9},{2,10},{3,11},{4,12},{5,13},{6,14},{7,15},{8,0},{9,1},... | collective-permute-start | bytes 589832 | tf_op jit(solution)/shard_map/ppermute | solution.py:332
  41.5 4.1 %collective-permute-start.6 = (bf16[256,384]{1,0:T(8,128)(2,1)S(1)}, bf16[256,384]{1,0:T(8,128)(2,1)S(1)}, u32[]{:S(2)}, u32[]{:S(2)}) collective-permute-start(bf16[256,384]{1,0:T(8,128)(2,1)S(1)} %collective-permute-done.4.c0), channel_id=1, source_target_pairs={{0,8},{1,9},{2,10},{3,11},{4,12},{5,13},{6,14},{7,15},{8,0},{9,1},... | collective-permute-start | bytes 589832 | tf_op jit(solution)/shard_map/ppermute | solution.py:332
  45.0 1.7 %collective-permute-start.7 = (bf16[256,384]{1,0:T(8,128)(2,1)S(1)}, bf16[256,384]{1,0:T(8,128)(2,1)S(1)}, u32[]{:S(2)}, u32[]{:S(2)}) collective-permute-start(bf16[256,384]{1,0:T(8,128)(2,1)S(1)} %collective-permute-done.5.c2), channel_id=1, source_target_pairs={{0,8},{1,9},{2,10},{3,11},{4,12},{5,13},{6,14},{7,15},{8,0},{9,1},... | collective-permute-start | bytes 589832 | tf_op jit(solution)/shard_map/ppermute | solution.py:332
  54.2 1.6 %collective-permute-start.13 = (bf16[256,384]{1,0:T(8,128)(2,1)S(1)}, bf16[256,384]{1,0:T(8,128)(2,1)S(1)}, u32[]{:S(2)}, u32[]{:S(2)}) collective-permute-start(bf16[256,384]{1,0:T(8,128)(2,1)S(1)} %get-tuple-element.16), channel_id=1, source_target_pairs={{0,0},{1,1},{2,8},{3,9},{4,4},{5,5},{6,12},{7,13},{8,2},{9,3},{10,... | collective-permute-start | bytes 589832 | tf_op jit(solution)/shard_map/ppermute | solution.py:332
  54.9 7.3 %collective-permute-start.14 = (bf16[256,384]{1,0:T(8,128)(2,1)S(1)}, bf16[256,384]{1,0:T(8,128)(2,1)S(1)}, u32[]{:S(2)}, u32[]{:S(2)}) collective-permute-start(bf16[256,384]{1,0:T(8,128)(2,1)S(1)} %get-tuple-element.17), channel_id=1, source_target_pairs={{0,1},{1,0},{2,9},{3,8},{4,5},{5,4},{6,13},{7,12},{8,3},{9,2},{10,... | collective-permute-start | bytes 589832 | tf_op jit(solution)/shard_map/ppermute | solution.py:332
  64.1 15.4 %collective-permute-start.15 = (bf16[2,128,384]{2,1,0:T(8,128)(2,1)S(1)}, bf16[2,128,384]{2,1,0:T(8,128)(2,1)S(1)}, u32[]{:S(2)}, u32[]{:S(2)}) collective-permute-start(bf16[2,128,384]{2,1,0:T(8,128)(2,1)S(1)} %get-tuple-element.19), channel_id=1, source_target_pairs={{8,0},{16,8},{24,16},{32,24},{40,32},{48,40},{56,48},{64,56},{72,6... | collective-permute-start | bytes 589832 | tf_op jit(solution)/shard_map/ppermute | solution.py:407
  72.6 5.3 %collective-permute-start.16 = (bf16[128,384]{1,0:T(8,128)(2,1)S(1)}, bf16[128,384]{1,0:T(8,128)(2,1)S(1)}, u32[]{:S(2)}, u32[]{:S(2)}) collective-permute-start(bf16[128,384]{1,0:T(8,128)(2,1)S(1)} %get-tuple-element.20), channel_id=1, source_target_pairs={{0,0},{1,1},{2,8},{3,9},{4,4},{5,5},{6,12},{7,13},{8,2},{9,3},{10,... | collective-permute-start | bytes 294920 | tf_op jit(solution)/shard_map/ppermute | solution.py:332
  73.3 6.2 %collective-permute-start.17 = (bf16[128,384]{1,0:T(8,128)(2,1)S(1)}, bf16[128,384]{1,0:T(8,128)(2,1)S(1)}, u32[]{:S(2)}, u32[]{:S(2)}) collective-permute-start(bf16[128,384]{1,0:T(8,128)(2,1)S(1)} %get-tuple-element.21), channel_id=1, source_target_pairs={{0,1},{1,0},{2,9},{3,8},{4,5},{5,4},{6,13},{7,12},{8,3},{9,2},{10,... | collective-permute-start | bytes 294920 | tf_op jit(solution)/shard_map/ppermute | solution.py:332
